TPU v7x, 32 devices: a whole 2x2x4 slice. The times are simulated.
32 devices in a mesh: wide: 8 (over y, x, core), narrow: 4 (over z).
Axes of the slice: x: 2, y: 2, z: 4, core: 2. Of those that a mesh axis runs over, the one named last changes fastest.
Arguments:
- activity: bfloat16 [32, 8, 512, 512], P(('wide', 'narrow')), may hold values from 0 to 1
- tile_coords: int32 [32, 2], replicated, may hold values from 0 to 7, as said below
- user_owner: int32 [8], replicated, may hold values from 0 to 7, each once
- item_owner: int32 [8], replicated, may hold values from 0 to 7, each once
- user_factor: float32 [4096, 256], P('wide', 'narrow'), may hold values from 0 to 1
- item_factor: float32 [4096, 256], P('wide', 'narrow'), may hold values from 0 to 1
- time_factor: float32 [8, 256], replicated, may hold values from 0.0003 to 0.003
- user_dual: float32 [4096, 256], P('wide', 'narrow'), may hold values from -1.8 to 1.8
- item_dual: float32 [4096, 256], P('wide', 'narrow'), may hold values from -1.8 to 1.8
Outputs:
- new_users: float32 [4096, 256], P('wide', 'narrow')
- new_items: float32 [4096, 256], P('wide', 'narrow')
- new_user_dual: float32 [4096, 256], P('wide', 'narrow')
- new_item_dual: float32 [4096, 256], P('wide', 'narrow')
Inputs may be any that keep to these rules, and one draw needn't show every extreme that they name: `tile_coords`: no pair of blocks appears twice. `user_owner`: each stored row block holds exactly one user block. `item_owner`: each stored row block holds exactly one item block.
All inputs are finite; a program needn't handle non-finite values.
Results may differ from a plain program's by a relative error of at most 0.0017.
The roundings to bfloat16 on the way count: a program that leaves them out, or rounds other values in their place, can miss the bound.
Values may be sent and summed in bfloat16 or wider, within the bound.
No kernel may reach another device: no remote copies, remote signals or barrier semaphores. Data moves between devices by JAX's collectives and lax.ppermute only.
A program may use at most 64 MiB of HBM per device.

v0:
```python
import functools

import jax
import jax.numpy as jnp
from jax import lax
from jax.experimental import pallas as pl
from jax.experimental.pallas import tpu as pltpu
from jax.sharding import PartitionSpec as P


PASSES = 2
LEAF = 8
HIGHEST = lax.Precision.HIGHEST
ROOM = pltpu.CompilerParams(vmem_limit_bytes=16 * 2**20)


def eliminate(left, right):
    panel, width = left.shape
    lane = lax.broadcasted_iota(jnp.int32, (LEAF, width), 1)
    sub = lax.broadcasted_iota(jnp.int32, (LEAF, width), 0)
    for j in range(0, panel, LEAF):
        cols = [jnp.broadcast_to(left[:, j + m : j + m + 1], (panel, width)) for m in range(LEAF)]
        d = [c[j : j + LEAF] for c in cols]
        for k in range(LEAF):
            r = 1.0 / d[k][k : k + 1]
            pivot = d[k]
            here = sub == k
            for m in range(LEAF):
                if m != k:
                    f = d[m][k : k + 1] * r
                    d[m] = jnp.where(here, f, d[m] - pivot * f)
            d[k] = jnp.where(here, r, -pivot * r)
        inside = (lane >= j) & (lane < j + LEAF)
        el = jnp.where(inside, jnp.where(lane == sub + j, 1.0, 0.0), left[j : j + LEAF])
        er = right[j : j + LEAF]
        rl = sum(d[m] * el[m : m + 1] for m in range(LEAF))
        rr = sum(d[m] * er[m : m + 1] for m in range(LEAF))
        new_left, new_right = [], []
        for i in range(0, panel, LEAF):
            if i == j:
                new_left.append(rl)
                new_right.append(rr)
            else:
                c = [col[i : i + LEAF] for col in cols]
                ul = sum(c[m] * rl[m : m + 1] for m in range(LEAF))
                ur = sum(c[m] * rr[m : m + 1] for m in range(LEAF))
                new_left.append(jnp.where(inside, 0.0, left[i : i + LEAF]) - ul)
                new_right.append(right[i : i + LEAF] - ur)
        left = jnp.concatenate(new_left, 0)
        right = jnp.concatenate(new_right, 0)
    return left, right


def eliminate_panel(panel, k, work_ref):
    rank = work_ref.shape[0]
    half = rank // 2
    lane = lax.broadcasted_iota(jnp.int32, (1, rank), 1)
    rows = pl.ds(k * panel, panel)
    left, right = eliminate(work_ref[rows, :half], work_ref[rows, half:])
    done = jnp.concatenate([left, right], 1)
    full = work_ref[...]
    change = jnp.dot(full[:, :panel], done, precision=HIGHEST, preferred_element_type=jnp.float32)
    work_ref[...] = pltpu.roll(jnp.where(lane < panel, 0.0, full) - change, rank - panel, 1)
    work_ref[rows, :] = pltpu.roll(done, rank - panel, 1)


def first_half_kernel(panel, time_ref, *refs):
    pieces, (work_ref, penalty_ref) = refs[:-2], refs[-2:]
    rank = work_ref.shape[0]
    half = rank // 2
    for r, piece in enumerate(pieces):
        start = (lax.axis_index("wide") % 2 ^ r) * half
        work_ref[pl.ds(pl.multiple_of(start, half), half), :] = piece[...]
    time = time_ref[...]
    times = lax.dot_general(
        time, time, (((0,), (0,)), ((), ())), precision=HIGHEST, preferred_element_type=jnp.float32
    )
    gram = work_ref[...] * times
    row = lax.broadcasted_iota(jnp.int32, (rank, rank), 0)
    col = lax.broadcasted_iota(jnp.int32, (rank, rank), 1)
    trace = jnp.sum(jnp.where(row == col, gram, 0.0), axis=0, keepdims=True)
    penalty = jnp.sum(trace, axis=1, keepdims=True) / rank
    penalty_ref[...] = jnp.broadcast_to(penalty, penalty_ref.shape)
    work_ref[...] = gram + jnp.where(row == col, penalty, 0.0)
    eliminate_panel(panel, 0, work_ref)


def second_half_kernel(panel, half_ref, inverse_ref):
    inverse_ref[...] = half_ref[...]
    eliminate_panel(panel, 1, inverse_ref)


def penalty_inverse(pieces, time_factor):
    rank = time_factor.shape[1]
    half, penalty = kernel_call(
        functools.partial(first_half_kernel, rank // 2),
        [shape((rank, rank)), shape((1, 128))], time_factor, *pieces, flops=6_000_000_000,
    )
    (inverse,) = kernel_call(
        functools.partial(second_half_kernel, rank // 2),
        [shape((rank, rank))], half, flops=6_000_000_000,
    )
    return penalty, inverse


def kernel_call(kernel, out_shape, *args, scratch=(), flops=1_000_000, smem=False):
    spec = pl.BlockSpec(memory_space=pltpu.SMEM) if smem else pl.BlockSpec(memory_space=pltpu.VMEM)
    size = sum(x.size * x.dtype.itemsize for x in (*args, *out_shape))
    return pl.pallas_call(
        kernel,
        out_shape=tuple(out_shape),
        in_specs=[spec] * len(args),
        out_specs=tuple(pl.BlockSpec(memory_space=pltpu.VMEM) for _ in out_shape),
        scratch_shapes=list(scratch),
        compiler_params=ROOM,
        cost_estimate=pl.CostEstimate(flops=flops, bytes_accessed=size, transcendentals=0),
    )(*args)


def shape(dims, dtype=jnp.float32):
    return jax.ShapeDtypeStruct(tuple(dims), dtype)


def swap(x, axis, mask):
    size = lax.axis_size(axis)
    return lax.ppermute(x, axis, [(i, i ^ mask) for i in range(size)])


def swaps(pieces):
    return [pieces[0]] + [swap(pieces[d], "narrow", d) for d in range(1, len(pieces))]


def for_each_position(body):
    me = lax.axis_index("narrow")
    for v in range(lax.axis_size("narrow")):
        pl.when(me == v)(functools.partial(body, v))


def rows_of(d, height):
    return pl.ds(pl.multiple_of((lax.axis_index("narrow") ^ d) * height, height), height)


def positions_kernel(coords_ref, user_ref, item_ref, table_ref):
    wide, narrow = lax.axis_index("wide"), lax.axis_index("narrow")
    count = lax.axis_size("narrow")
    for d in range(count):
        tile = wide * count + (narrow ^ d)
        user = user_ref[coords_ref[0, tile]] ^ wide
        item = item_ref[coords_ref[1, tile]] ^ wide
        table_ref[d : d + 1, :] = jnp.full((1, 128), user, jnp.int32)
        table_ref[count + d : count + d + 1, :] = jnp.full((1, 128), item, jnp.int32)


def positions(tile_coords, user_owner, item_owner):
    count = lax.axis_size("narrow")
    (table,) = kernel_call(
        positions_kernel, [shape((2 * count, 128), jnp.int32)],
        tile_coords.T, user_owner, item_owner, smem=True,
    )
    return table[:count], table[count:]


def split_kernel(stack_ref, *outputs):
    width = outputs[0].shape[1]

    def body(v):
        for d, out in enumerate(outputs):
            out[...] = stack_ref[:, (v ^ d) * width : ((v ^ d) + 1) * width]

    for_each_position(body)


def split(stack):
    count = lax.axis_size("narrow")
    height, rows = stack.shape
    return kernel_call(split_kernel, [shape((height, rows // count))] * count, stack)


def store_pair(value, pair_ref):
    rank = value.shape[0]
    rounded = value.astype(pair_ref.dtype)
    pair_ref[:rank] = rounded
    pair_ref[rank:] = (value - rounded.astype(jnp.float32)).astype(pair_ref.dtype)


def pair_kernel(count, *refs):
    pieces, (factor_ref, pair_ref) = refs[:count], refs[count:]
    height = pieces[0].shape[0]
    for d, piece in enumerate(pieces):
        factor_ref[rows_of(d, height), :] = piece[...]
    store_pair(factor_ref[...], pair_ref)


def assemble_kernel(count, *refs):
    factor_ref, pieces, outputs = refs[0], refs[1 : count + 1], refs[count + 1 :]
    height = pieces[0].shape[0] // 3
    for d, piece in enumerate(pieces):
        rows = rows_of(d, height)
        outputs[0][rows, :] = piece[:height]
        outputs[1][rows, :] = piece[height : 2 * height]
        outputs[3][rows, :] = piece[2 * height :]
    outputs[2][...] = factor_ref[...] + outputs[3][...]


def gram_kernel(*refs):
    pairs, (half_ref, rows_ref) = refs[:-2], refs[-2:]
    rank = rows_ref.shape[0]
    width = pairs[0].shape[1]
    for k, pair in enumerate(pairs):
        rows_ref[:, k * width : (k + 1) * width] = pair[:rank].astype(jnp.float32) + pair[
            rank:
        ].astype(jnp.float32)
    half = half_ref.shape[0]
    start = pl.multiple_of(lax.axis_index("wide") % 2 * half, half)
    half_ref[...] = lax.dot_general(
        rows_ref[pl.ds(start, half), :], rows_ref[...], (((1,), (1,)), ((), ())),
        precision=HIGHEST, preferred_element_type=jnp.float32,
    )


def joint_gram(pairs):
    rank, width = pairs[0].shape[0] // 2, pairs[0].shape[1]
    (total,) = kernel_call(
        gram_kernel, [shape((rank // 2, rank))], *pairs,
        scratch=[pltpu.VMEM((rank, len(pairs) * width), jnp.float32)],
        flops=1_500_000_000,
    )
    mask = 1
    while mask < lax.axis_size("narrow"):
        total = total + swap(total, "narrow", mask)
        mask *= 2
    return total, swap(total, "wide", 1)


def pick_kernel(count, table_ref, *refs):
    pairs, outputs = refs[:-count], refs[-count:]
    for d, out in enumerate(outputs):
        rank = out.shape[0]
        here = table_ref[d : d + 1, :1].astype(jnp.float32).astype(out.dtype)
        here = jnp.broadcast_to(here, out.shape)
        value = pairs[0][:rank]
        for r in range(1, len(pairs)):
            value = jnp.where(here == r, pairs[r][:rank], value)
        out[...] = value


def all_pairs(pair):
    chips = lax.axis_size("wide") // 2
    same = [pair] + [swap(pair, "wide", 2 * m) for m in range(1, chips)]
    return [x for a in same for x in (a, swap(a, "wide", 1))]


def fetch_rows(pairs, table):
    count = lax.axis_size("narrow")
    rank, width = pairs[0].shape[0] // 2, pairs[0].shape[1]
    picked = kernel_call(
        functools.partial(pick_kernel, count), [shape((rank, width), jnp.bfloat16)] * count,
        table, *pairs, flops=5_000_000_000,
    )
    return swaps(picked)


def tile_kernel(forward, count, activity_ref, time_ref, *refs):
    pieces, outputs, (stage_ref, sums_ref) = refs[:count], refs[count : 2 * count], refs[2 * count :]
    me = lax.axis_index("narrow")
    for d, piece in enumerate(pieces):
        stage_ref[me ^ d] = piece[...]
    low = jnp.concatenate([stage_ref[q] for q in range(count)], axis=1)
    low = low.astype(jnp.float32)
    times = time_ref[...].T
    total = None
    for k in range(activity_ref.shape[1]):
        khatri = (low * times[:, k : k + 1]).astype(jnp.bfloat16)
        dims = (((1,), (1 if forward else 0,)), ((), ()))
        term = lax.dot_general(khatri, activity_ref[0, k], dims, preferred_element_type=jnp.float32)
        total = term if total is None else total + term
    width = outputs[0].shape[1]
    for q in range(count):
        sums_ref[q] = total[:, q * width : (q + 1) * width]
    for d, out in enumerate(outputs):
        out[...] = sums_ref[me ^ d]


def tile_sums(activity, pieces, time_factor, forward):
    count = len(pieces)
    rank = time_factor.shape[1]
    _, steps, rows, cols = activity.shape
    width = (rows if forward else cols) // count
    return kernel_call(
        functools.partial(tile_kernel, forward, count), [shape((rank, width))] * count,
        activity, time_factor, *pieces,
        scratch=[
            pltpu.VMEM((count, *pieces[0].shape), jnp.bfloat16),
            pltpu.VMEM((count, rank, width), jnp.float32),
        ],
        flops=2 * rank * steps * rows * cols,
    )


def place_kernel(count, table_ref, *refs):
    received, outputs = refs[:count], refs[count:]
    values = [x[...] for x in received]
    for r, out in enumerate(outputs):
        total = None
        for d, value in enumerate(values):
            here = jnp.broadcast_to(table_ref[d : d + 1, :1] == r, value.shape)
            term = jnp.where(here, value, 0.0)
            total = term if total is None else total + term
        out[...] = total


def owner_sums(partials, table):
    received = swaps(partials)
    size = lax.axis_size("wide")
    placed = kernel_call(
        functools.partial(place_kernel, len(received)), [shape(received[0].shape)] * size,
        table, *received,
    )
    arrived = [swap(placed[2 * m + 1], "wide", 1) for m in range(1, size // 2)]
    terms = [placed[0], swap(placed[1], "wide", 1)]
    for m in range(1, size // 2):
        terms.append(swap(placed[2 * m] + arrived[m - 1], "wide", 2 * m))
    return terms


def update_kernel(terms, count, *refs):
    sums = refs[0][...]
    for term in refs[1:terms]:
        sums = sums + term[...]
    shifted_ref, dual_ref, penalty_ref, inverse_ref = refs[terms : terms + 4]
    outputs = refs[terms + 4 :]
    value_ref = outputs[-1]
    penalty = penalty_ref[:1, :1]
    inverse = inverse_ref[...]
    shifted, dual = shifted_ref[...], dual_ref[...]
    for _ in range(PASSES):
        target = jnp.dot(
            inverse, sums + penalty * shifted, precision=HIGHEST, preferred_element_type=jnp.float32
        )
        value = target - dual
        dual = jnp.maximum(-value, 0.0)
        shifted = jnp.abs(value)
    value_ref[...] = value
    height = outputs[0].shape[0]
    for d in range(count):
        outputs[d][...] = value_ref[rows_of(d, height), :]
    if len(outputs) > count + 1:
        store_pair(jnp.maximum(value, 0.0), outputs[count])


def admm(terms, shifted, dual, penalty, inverse, more):
    count = lax.axis_size("narrow")
    rank, width = shifted.shape
    out = [shape((rank // count, width))] * count
    if more:
        out += [shape((2 * rank, width), jnp.bfloat16)]
    return kernel_call(
        functools.partial(update_kernel, len(terms), count), out,
        *terms, shifted, dual, penalty, inverse,
        scratch=[pltpu.VMEM((rank, width), jnp.float32)],
        flops=12 * rank * rank * width * PASSES,
    )


def final_kernel(count, *refs):
    pieces, (factor_ref, dual_ref) = refs[:count], refs[count:]
    width = pieces[0].shape[1]

    def body(v):
        for d, piece in enumerate(pieces):
            lanes = slice((v ^ d) * width, ((v ^ d) + 1) * width)
            value = piece[...]
            factor_ref[:, lanes] = jnp.maximum(value, 0.0)
            dual_ref[:, lanes] = jnp.maximum(-value, 0.0)

    for_each_position(body)


def to_columns(pieces):
    received = swaps(pieces)
    height, width = received[0].shape
    count = len(received)
    factor, dual = kernel_call(
        functools.partial(final_kernel, count), [shape((height, count * width))] * 2,
        *received,
    )
    return factor.T, dual.T


def local(
    activity,
    tile_coords,
    user_owner,
    item_owner,
    user_factor,
    item_factor,
    time_factor,
    user_dual,
    item_dual,
):
    return sweep(
        activity, tile_coords, user_owner, item_owner, user_factor.T, item_factor.T,
        time_factor, user_dual.T, item_dual.T,
    )


def sweep(
    activity, tile_coords, user_owner, item_owner, user_factor, item_factor, time_factor,
    user_dual, item_dual,
):
    rank = time_factor.shape[1]
    count = lax.axis_size("narrow")
    user_table, item_table = positions(tile_coords, user_owner, item_owner)

    pieces = swaps(split(item_factor))
    rows = shape((rank, pieces[0].shape[1]))
    pair = shape((2 * rank, rows.shape[1]), jnp.bfloat16)
    item_rows, pair = kernel_call(functools.partial(pair_kernel, count), [rows, pair], *pieces)
    stack = jnp.concatenate([user_factor + user_dual, user_dual, item_dual])
    user_shifted, udual_rows, item_shifted, idual_rows = kernel_call(
        functools.partial(assemble_kernel, count), [rows] * 4,
        item_rows, *swaps(split(stack)),
    )

    pairs = all_pairs(pair)
    partials = tile_sums(activity, fetch_rows(pairs, item_table), time_factor, True)
    terms = owner_sums(partials, user_table)
    penalty, inverse = penalty_inverse(joint_gram(pairs), time_factor)
    *user_pieces, pair = admm(terms, user_shifted, udual_rows, penalty, inverse, True)

    pairs = all_pairs(pair)
    partials = tile_sums(activity, fetch_rows(pairs, user_table), time_factor, False)
    terms = owner_sums(partials, item_table)
    penalty, inverse = penalty_inverse(joint_gram(pairs), time_factor)
    new_users, new_user_dual = to_columns(user_pieces)
    item_pieces = admm(terms, item_shifted, idual_rows, penalty, inverse, False)
    new_items, new_item_dual = to_columns(item_pieces)
    return (new_users, new_items, new_user_dual, new_item_dual)


def solution(mesh):
    in_specs = (
        P(("wide", "narrow"), None, None, None),
        P(),
        P(),
        P(),
        P("wide", "narrow"),
        P("wide", "narrow"),
        P(),
        P("wide", "narrow"),
        P("wide", "narrow"),
    )
    out_specs = (P("wide", "narrow"), P("wide", "narrow"), P("wide", "narrow"), P("wide", "narrow"))
    return jax.shard_map(local, mesh=mesh, in_specs=in_specs, out_specs=out_specs, check_vma=False)
```

profile of v0, /device:TPU:0, one launch (start us, length us, event | category | flops | bytes accessed | tf_op | source)
XLA Modules:
  0.0 151.0 jit_solution(12251615843209380581)
XLA Ops:
  0.6 0.9 copy-done.1
  1.6 3.1 %collective-permute-start = (f32[64,128]{1,0:T(8,128)S(1)}, f32[64,128]{1,0:T(8,128)S(1)}, u32[]{:S(2)}, u32[]{:S(2)}) collective-permute-start(f32[64,128]{1,0:T(8,128)S(1)} %get-tuple-element.68), channel_id=1, source_target_pairs={{0,1},{1,0},{2,3},{3,2},{4,5},{5,4},{6,7},{7,6},{8,9},{9,8},{10,11... | collective-permute-start | bytes 98312 | tf_op jit(solution)/shard_map/ppermute | solution.py:126
  4.7 2.6 %collective-permute-start.1 = (f32[64,128]{1,0:T(8,128)S(1)}, f32[64,128]{1,0:T(8,128)S(1)}, u32[]{:S(2)}, u32[]{:S(2)}) collective-permute-start(f32[64,128]{1,0:T(8,128)S(1)} %get-tuple-element.69), channel_id=1, source_target_pairs={{0,2},{1,3},{2,0},{3,1},{4,6},{5,7},{6,4},{7,5},{8,10},{9,11},{10,... | collective-permute-start | bytes 98312 | tf_op jit(solution)/shard_map/ppermute | solution.py:126
  7.3 2.8 %collective-permute-done.1.refs_2_ = f32[64,128]{1,0:T(8,128)S(1)} collective-permute-done((f32[64,128]{1,0:T(8,128)S(1)}, f32[64,128]{1,0:T(8,128)S(1)}, u32[]{:S(2)}, u32[]{:S(2)}) %collective-permute-start.1) | collective-permute-done | bytes 32800 | tf_op jit(solution)/shard_map/ppermute | solution.py:126
  10.1 2.9 %collective-permute-done.2.refs_3_ = f32[64,128]{1,0:T(8,128)S(1)} collective-permute-done((f32[64,128]{1,0:T(8,128)S(1)}, f32[64,128]{1,0:T(8,128)S(1)}, u32[]{:S(2)}, u32[]{:S(2)}) %collective-permute-start.2) | collective-permute-done | bytes 32800 | tf_op jit(solution)/shard_map/ppermute | solution.py:126
  13.0 1.6 %collective-permute-start.4 = (bf16[512,128]{1,0:T(8,128)(2,1)S(1)}, bf16[512,128]{1,0:T(8,128)(2,1)S(1)}, u32[]{:S(2)}, u32[]{:S(2)}) collective-permute-start(bf16[512,128]{1,0:T(8,128)(2,1)S(1)} %get-tuple-element.71.refs_0_), channel_id=1, source_target_pairs={{0,8},{4,12},{8,0},{12,4},{16,24},{20,28},{24,16},{28,20},{1,9},{5... | collective-permute-start | bytes 393224 | tf_op jit(solution)/shard_map/ppermute | solution.py:126
  14.6 1.5 %collective-permute-start.6 = (bf16[512,128]{1,0:T(8,128)(2,1)S(1)}, bf16[512,128]{1,0:T(8,128)(2,1)S(1)}, u32[]{:S(2)}, u32[]{:S(2)}) collective-permute-start(bf16[512,128]{1,0:T(8,128)(2,1)S(1)} %get-tuple-element.71.refs_0_), channel_id=1, source_target_pairs={{0,16},{4,20},{8,24},{12,28},{16,0},{20,4},{24,8},{28,12},{1,17},{... | collective-permute-start | bytes 393224 | tf_op jit(solution)/shard_map/ppermute | solution.py:126
  16.6 0.7 copy-done.3
  17.2 0.7 copy-done.4
  17.9 0.7 copy-done.5
  20.3 1.6 %collective-permute-done.8.refs_6_ = bf16[512,128]{1,0:T(8,128)(2,1)S(1)} collective-permute-done((bf16[512,128]{1,0:T(8,128)(2,1)S(1)}, bf16[512,128]{1,0:T(8,128)(2,1)S(1)}, u32[]{:S(2)}, u32[]{:S(2)}) %collective-permute-start.8) | collective-permute-done | bytes 131104 | tf_op jit(solution)/shard_map/ppermute | solution.py:126
  22.0 1.3 collective-permute-done.9.refs_7_
  23.3 1.2 shard_map.128
  24.9 2.0 %collective-permute-start.10 = (bf16[256,128]{1,0:T(8,128)(2,1)S(1)}, bf16[256,128]{1,0:T(8,128)(2,1)S(1)}, u32[]{:S(2)}, u32[]{:S(2)}) collective-permute-start(bf16[256,128]{1,0:T(8,128)(2,1)S(1)} %get-tuple-element.73), channel_id=1, source_target_pairs={{0,1},{1,0},{2,3},{3,2},{4,5},{5,4},{6,7},{7,6},{8,9},{9,8},{10,11... | collective-permute-start | bytes 196616 | tf_op jit(solution)/shard_map/ppermute | solution.py:126
  26.9 2.4 %collective-permute-start.12 = (bf16[256,128]{1,0:T(8,128)(2,1)S(1)}, bf16[256,128]{1,0:T(8,128)(2,1)S(1)}, u32[]{:S(2)}, u32[]{:S(2)}) collective-permute-start(bf16[256,128]{1,0:T(8,128)(2,1)S(1)} %get-tuple-element.75), channel_id=1, source_target_pairs={{0,3},{1,2},{2,1},{3,0},{4,7},{5,6},{6,5},{7,4},{8,11},{9,10},{10,... | collective-permute-start | bytes 196616 | tf_op jit(solution)/shard_map/ppermute | solution.py:126
  29.4 4.8 %collective-permute-done.10.refs_1_ = bf16[256,128]{1,0:T(8,128)(2,1)S(1)} collective-permute-done((bf16[256,128]{1,0:T(8,128)(2,1)S(1)}, bf16[256,128]{1,0:T(8,128)(2,1)S(1)}, u32[]{:S(2)}, u32[]{:S(2)}) %collective-permute-start.10) | collective-permute-done | bytes 65568 | tf_op jit(solution)/shard_map/ppermute | solution.py:126
  34.5 1.5 %shard_map.124 = (f32[256,128]{1,0:T(8,128)S(1)}, f32[256,128]{1,0:T(8,128)S(1)}, f32[256,128]{1,0:T(8,128)S(1)}, f32[256,128]{1,0:T(8,128)S(1)}) custom-call(bf16[1,8,512,512]{3,2,1,0:T(8,128)(2,1)S(1)} %copy-done, f32[8,256]{1,0:T(8,128)S(1)} %copy-done.2, bf16[256,128]{1,0:T(8,128)(2,1)S(1)} %get-tuple-element.72.refs_0_, ...), custom_call_target="tpu_custom_call" | custom-call | flops 1073741824 | bytes 4988928 | tf_op jit(solution)/shard_map/pallas_call | solution.py:109
  36.0 1.7 %collective-permute-start.13 = (f32[256,128]{1,0:T(8,128)S(1)}, f32[256,128]{1,0:T(8,128)S(1)}, u32[]{:S(2)}, u32[]{:S(2)}) collective-permute-start(f32[256,128]{1,0:T(8,128)S(1)} %get-tuple-element.77), channel_id=1, source_target_pairs={{0,1},{1,0},{2,3},{3,2},{4,5},{5,4},{6,7},{7,6},{8,9},{9,8},{10,11... | collective-permute-start | bytes 393224 | tf_op jit(solution)/shard_map/ppermute | solution.py:126
  37.7 1.0 collective-permute-start.14
  38.7 1.7 %collective-permute-start.15 = (f32[256,128]{1,0:T(8,128)S(1)}, f32[256,128]{1,0:T(8,128)S(1)}, u32[]{:S(2)}, u32[]{:S(2)}) collective-permute-start(f32[256,128]{1,0:T(8,128)S(1)} %get-tuple-element.79), channel_id=1, source_target_pairs={{0,3},{1,2},{2,1},{3,0},{4,7},{5,6},{6,5},{7,4},{8,11},{9,10},{10,... | collective-permute-start | bytes 393224 | tf_op jit(solution)/shard_map/ppermute | solution.py:126
  40.5 1.0 collective-permute-start.27
  41.7 1.8 %collective-permute-start.23 = (f32[192,128]{1,0:T(8,128)S(1)}, f32[192,128]{1,0:T(8,128)S(1)}, u32[]{:S(2)}, u32[]{:S(2)}) collective-permute-start(f32[192,128]{1,0:T(8,128)S(1)} %get-tuple-element.90), channel_id=1, source_target_pairs={{0,1},{1,0},{2,3},{3,2},{4,5},{5,4},{6,7},{7,6},{8,9},{9,8},{10,11... | collective-permute-start | bytes 294920 | tf_op jit(solution)/shard_map/ppermute | solution.py:126
  43.6 1.0 collective-permute-start.24
  44.6 8.9 %collective-permute-done.14.refs_2_ = f32[256,128]{1,0:T(8,128)S(1)} collective-permute-done((f32[256,128]{1,0:T(8,128)S(1)}, f32[256,128]{1,0:T(8,128)S(1)}, u32[]{:S(2)}, u32[]{:S(2)}) %collective-permute-start.14) | collective-permute-done | bytes 131104 | tf_op jit(solution)/shard_map/ppermute | solution.py:126
  54.5 5.7 %collective-permute-done.27 = f32[128,256]{1,0:T(8,128)S(1)} collective-permute-done((f32[128,256]{1,0:T(8,128)S(1)}, f32[128,256]{1,0:T(8,128)S(1)}, u32[]{:S(2)}, u32[]{:S(2)}) %collective-permute-start.27) | collective-permute-done | bytes 131104 | tf_op jit(solution)/shard_map/ppermute | solution.py:126
  60.8 0.8 collective-permute-done.24.refs_3_
  61.6 1.4 collective-permute-start.25
  63.0 5.0 %collective-permute-done.25.refs_4_ = f32[192,128]{1,0:T(8,128)S(1)} collective-permute-done((f32[192,128]{1,0:T(8,128)S(1)}, f32[192,128]{1,0:T(8,128)S(1)}, u32[]{:S(2)}, u32[]{:S(2)}) %collective-permute-start.25) | collective-permute-done | bytes 98336 | tf_op jit(solution)/shard_map/ppermute | solution.py:126
  68.2 0.7 collective-permute-start.22
  68.9 1.5 collective-permute-start.20
  70.4 1.6 %collective-permute-start.18 = (f32[256,128]{1,0:T(8,128)S(1)}, f32[256,128]{1,0:T(8,128)S(1)}, u32[]{:S(2)}, u32[]{:S(2)}) collective-permute-start(f32[256,128]{1,0:T(8,128)S(1)} %add.33), channel_id=1, source_target_pairs={{0,8},{4,12},{8,0},{12,4},{16,24},{20,28},{24,16},{28,20},{1,9},{5... | collective-permute-start | bytes 393224 | tf_op jit(solution)/shard_map/ppermute | solution.py:126
  71.9 5.0 %shard_map.129 = (f32[256,256]{1,0:T(8,128)S(1)}, f32[1,128]{1,0:T(1,128)S(1)}) custom-call(f32[8,256]{1,0:T(8,128)S(1)} %copy-done.2, f32[128,256]{1,0:T(8,128)S(1)} %add.38.refs_0_, f32[128,256]{1,0:T(8,128)S(1)} %collective-permute-done.28.refs_1_), custom_call_target="tpu_custom_call" | custom-call | flops 6000000000 | bytes 532992 | tf_op jit(solution)/shard_map/pallas_call | solution.py:109
  76.9 4.2 %shard_map.130.refs_8_ = f32[256,256]{1,0:T(8,128)S(1)} custom-call(f32[256,256]{1,0:T(8,128)S(1)} %get-tuple-element.96.half_ref), custom_call_target="tpu_custom_call" | custom-call | flops 6000000000 | bytes 524288 | tf_op jit(solution)/shard_map/pallas_call | solution.py:109
  81.1 1.2 shard_map.131
  82.3 0.6 collective-permute-start.33
  82.9 0.6 collective-permute-start.35
  83.5 2.3 %collective-permute-start.37 = (bf16[512,128]{1,0:T(8,128)(2,1)S(1)}, bf16[512,128]{1,0:T(8,128)(2,1)S(1)}, u32[]{:S(2)}, u32[]{:S(2)}) collective-permute-start(bf16[512,128]{1,0:T(8,128)(2,1)S(1)} %get-tuple-element.102.refs_0_), channel_id=1, source_target_pairs={{0,24},{4,28},{8,16},{12,20},{16,8},{20,12},{24,0},{28,4},{1,25},{... | collective-permute-start | bytes 393224 | tf_op jit(solution)/shard_map/ppermute | solution.py:126
  85.9 2.9 %collective-permute-done.33.refs_2_ = bf16[512,128]{1,0:T(8,128)(2,1)S(1)} collective-permute-done((bf16[512,128]{1,0:T(8,128)(2,1)S(1)}, bf16[512,128]{1,0:T(8,128)(2,1)S(1)}, u32[]{:S(2)}, u32[]{:S(2)}) %collective-permute-start.33) | collective-permute-done | bytes 131104 | tf_op jit(solution)/shard_map/ppermute | solution.py:126
  89.3 1.4 collective-permute-done.37.refs_6_
  90.7 1.3 collective-permute-done.38.refs_7_
  92.4 2.0 %collective-permute-start.40 = (bf16[256,128]{1,0:T(8,128)(2,1)S(1)}, bf16[256,128]{1,0:T(8,128)(2,1)S(1)}, u32[]{:S(2)}, u32[]{:S(2)}) collective-permute-start(bf16[256,128]{1,0:T(8,128)(2,1)S(1)} %get-tuple-element.105), channel_id=1, source_target_pairs={{0,2},{1,3},{2,0},{3,1},{4,6},{5,7},{6,4},{7,5},{8,10},{9,11},{10,... | collective-permute-start | bytes 196616 | tf_op jit(solution)/shard_map/ppermute | solution.py:126
  94.4 2.4 %collective-permute-start.41 = (bf16[256,128]{1,0:T(8,128)(2,1)S(1)}, bf16[256,128]{1,0:T(8,128)(2,1)S(1)}, u32[]{:S(2)}, u32[]{:S(2)}) collective-permute-start(bf16[256,128]{1,0:T(8,128)(2,1)S(1)} %get-tuple-element.106), channel_id=1, source_target_pairs={{0,3},{1,2},{2,1},{3,0},{4,7},{5,6},{6,5},{7,4},{8,11},{9,10},{10,... | collective-permute-start | bytes 196616 | tf_op jit(solution)/shard_map/ppermute | solution.py:126
  96.8 1.4 shard_map.136
  98.3 2.7 %collective-permute-done.40.refs_2_ = bf16[256,128]{1,0:T(8,128)(2,1)S(1)} collective-permute-done((bf16[256,128]{1,0:T(8,128)(2,1)S(1)}, bf16[256,128]{1,0:T(8,128)(2,1)S(1)}, u32[]{:S(2)}, u32[]{:S(2)}) %collective-permute-start.40) | collective-permute-done | bytes 65568 | tf_op jit(solution)/shard_map/ppermute | solution.py:126
  101.0 1.5 %shard_map.134 = (f32[256,128]{1,0:T(8,128)S(1)}, f32[256,128]{1,0:T(8,128)S(1)}, f32[256,128]{1,0:T(8,128)S(1)}, f32[256,128]{1,0:T(8,128)S(1)}) custom-call(bf16[1,8,512,512]{3,2,1,0:T(8,128)(2,1)S(1)} %copy-done, f32[8,256]{1,0:T(8,128)S(1)} %copy-done.2, bf16[256,128]{1,0:T(8,128)(2,1)S(1)} %get-tuple-element.103.refs_0_, ...), custom_call_target="tpu_custom_call" | custom-call | flops 1073741824 | bytes 4988928 | tf_op jit(solution)/shard_map/pallas_call | solution.py:109
  102.6 1.3 collective-permute-start.42
  103.9 1.7 %collective-permute-start.43 = (f32[256,128]{1,0:T(8,128)S(1)}, f32[256,128]{1,0:T(8,128)S(1)}, u32[]{:S(2)}, u32[]{:S(2)}) collective-permute-start(f32[256,128]{1,0:T(8,128)S(1)} %get-tuple-element.109), channel_id=1, source_target_pairs={{0,2},{1,3},{2,0},{3,1},{4,6},{5,7},{6,4},{7,5},{8,10},{9,11},{10,... | collective-permute-start | bytes 393224 | tf_op jit(solution)/shard_map/ppermute | solution.py:126
  105.6 1.4 collective-permute-start.44
  107.4 1.5 %collective-permute-done.42.refs_1_ = f32[256,128]{1,0:T(8,128)S(1)} collective-permute-done((f32[256,128]{1,0:T(8,128)S(1)}, f32[256,128]{1,0:T(8,128)S(1)}, u32[]{:S(2)}, u32[]{:S(2)}) %collective-permute-start.42) | collective-permute-done | bytes 131104 | tf_op jit(solution)/shard_map/ppermute | solution.py:126
  108.9 9.9 %collective-permute-done.43.refs_2_ = f32[256,128]{1,0:T(8,128)S(1)} collective-permute-done((f32[256,128]{1,0:T(8,128)S(1)}, f32[256,128]{1,0:T(8,128)S(1)}, u32[]{:S(2)}, u32[]{:S(2)}) %collective-permute-start.43) | collective-permute-done | bytes 131104 | tf_op jit(solution)/shard_map/ppermute | solution.py:126
  119.8 3.0 %collective-permute-done.53 = f32[128,256]{1,0:T(8,128)S(1)} collective-permute-done((f32[128,256]{1,0:T(8,128)S(1)}, f32[128,256]{1,0:T(8,128)S(1)}, u32[]{:S(2)}, u32[]{:S(2)}) %collective-permute-start.53) | collective-permute-done | bytes 131104 | tf_op jit(solution)/shard_map/ppermute | solution.py:126
  122.9 0.6 collective-permute-start.29
  123.6 2.8 %collective-permute-start.51 = (f32[256,128]{1,0:T(8,128)S(1)}, f32[256,128]{1,0:T(8,128)S(1)}, u32[]{:S(2)}, u32[]{:S(2)}) collective-permute-start(f32[256,128]{1,0:T(8,128)S(1)} %add.41), channel_id=1, source_target_pairs={{0,24},{4,28},{8,16},{12,20},{16,8},{20,12},{24,0},{28,4},{1,25},{... | collective-permute-start | bytes 393224 | tf_op jit(solution)/shard_map/ppermute | solution.py:126
  126.4 1.1 collective-permute-start.49
  127.6 4.9 %shard_map.137 = (f32[256,256]{1,0:T(8,128)S(1)}, f32[1,128]{1,0:T(1,128)S(1)}) custom-call(f32[8,256]{1,0:T(8,128)S(1)} %copy-done.2, f32[128,256]{1,0:T(8,128)S(1)} %add.43.refs_0_, f32[128,256]{1,0:T(8,128)S(1)} %collective-permute-done.54.refs_1_), custom_call_target="tpu_custom_call" | custom-call | flops 6000000000 | bytes 532992 | tf_op jit(solution)/shard_map/pallas_call | solution.py:109
  132.6 4.2 %shard_map.138.refs_8_ = f32[256,256]{1,0:T(8,128)S(1)} custom-call(f32[256,256]{1,0:T(8,128)S(1)} %get-tuple-element.122.half_ref), custom_call_target="tpu_custom_call" | custom-call | flops 6000000000 | bytes 524288 | tf_op jit(solution)/shard_map/pallas_call | solution.py:109
  136.8 2.1 %collective-permute-start.30 = (f32[64,128]{1,0:T(8,128)S(1)}, f32[64,128]{1,0:T(8,128)S(1)}, u32[]{:S(2)}, u32[]{:S(2)}) collective-permute-start(f32[64,128]{1,0:T(8,128)S(1)} %get-tuple-element.99), channel_id=1, source_target_pairs={{0,2},{1,3},{2,0},{3,1},{4,6},{5,7},{6,4},{7,5},{8,10},{9,11},{10,... | collective-permute-start | bytes 98312 | tf_op jit(solution)/shard_map/ppermute | solution.py:126
  138.9 2.1 %collective-permute-start.31 = (f32[64,128]{1,0:T(8,128)S(1)}, f32[64,128]{1,0:T(8,128)S(1)}, u32[]{:S(2)}, u32[]{:S(2)}) collective-permute-start(f32[64,128]{1,0:T(8,128)S(1)} %get-tuple-element.100), channel_id=1, source_target_pairs={{0,3},{1,2},{2,1},{3,0},{4,7},{5,6},{6,5},{7,4},{8,11},{9,10},{10,... | collective-permute-start | bytes 98312 | tf_op jit(solution)/shard_map/ppermute | solution.py:126
  141.0 1.2 shard_map.139
  142.2 2.3 %collective-permute-start.56 = (f32[64,128]{1,0:T(8,128)S(1)}, f32[64,128]{1,0:T(8,128)S(1)}, u32[]{:S(2)}, u32[]{:S(2)}) collective-permute-start(f32[64,128]{1,0:T(8,128)S(1)} %get-tuple-element.125), channel_id=1, source_target_pairs={{0,2},{1,3},{2,0},{3,1},{4,6},{5,7},{6,4},{7,5},{8,10},{9,11},{10,... | collective-permute-start | bytes 98312 | tf_op jit(solution)/shard_map/ppermute | solution.py:126
  144.5 2.1 %collective-permute-start.57 = (f32[64,128]{1,0:T(8,128)S(1)}, f32[64,128]{1,0:T(8,128)S(1)}, u32[]{:S(2)}, u32[]{:S(2)}) collective-permute-start(f32[64,128]{1,0:T(8,128)S(1)} %get-tuple-element.126), channel_id=1, source_target_pairs={{0,3},{1,2},{2,1},{3,0},{4,7},{5,6},{6,5},{7,4},{8,11},{9,10},{10,... | collective-permute-start | bytes 98312 | tf_op jit(solution)/shard_map/ppermute | solution.py:126
  146.6 0.7 shard_map.132
  147.4 2.9 %collective-permute-done.57.refs_3_ = f32[64,128]{1,0:T(8,128)S(1)} collective-permute-done((f32[64,128]{1,0:T(8,128)S(1)}, f32[64,128]{1,0:T(8,128)S(1)}, u32[]{:S(2)}, u32[]{:S(2)}) %collective-permute-start.57) | collective-permute-done | bytes 32800 | tf_op jit(solution)/shard_map/ppermute | solution.py:126
  150.2 0.7 shard_map.140
  (104 shorter events, 7.6 us)
Async XLA Ops:
  0.6 0.9 copy-start.1
  1.6 5.7 %collective-permute-start = (f32[64,128]{1,0:T(8,128)S(1)}, f32[64,128]{1,0:T(8,128)S(1)}, u32[]{:S(2)}, u32[]{:S(2)}) collective-permute-start(f32[64,128]{1,0:T(8,128)S(1)} %get-tuple-element.68), channel_id=1, source_target_pairs={{0,1},{1,0},{2,3},{3,2},{4,5},{5,4},{6,7},{7,6},{8,9},{9,8},{10,11... | collective-permute-start | bytes 98312 | tf_op jit(solution)/shard_map/ppermute | solution.py:126
  4.7 5.4 %collective-permute-start.1 = (f32[64,128]{1,0:T(8,128)S(1)}, f32[64,128]{1,0:T(8,128)S(1)}, u32[]{:S(2)}, u32[]{:S(2)}) collective-permute-start(f32[64,128]{1,0:T(8,128)S(1)} %get-tuple-element.69), channel_id=1, source_target_pairs={{0,2},{1,3},{2,0},{3,1},{4,6},{5,7},{6,4},{7,5},{8,10},{9,11},{10,... | collective-permute-start | bytes 98312 | tf_op jit(solution)/shard_map/ppermute | solution.py:126
  7.3 5.7 %collective-permute-start.2 = (f32[64,128]{1,0:T(8,128)S(1)}, f32[64,128]{1,0:T(8,128)S(1)}, u32[]{:S(2)}, u32[]{:S(2)}) collective-permute-start(f32[64,128]{1,0:T(8,128)S(1)} %get-tuple-element.70), channel_id=1, source_target_pairs={{0,3},{1,2},{2,1},{3,0},{4,7},{5,6},{6,5},{7,4},{8,11},{9,10},{10,... | collective-permute-start | bytes 98312 | tf_op jit(solution)/shard_map/ppermute | solution.py:126
  13.0 6.2 %collective-permute-start.4 = (bf16[512,128]{1,0:T(8,128)(2,1)S(1)}, bf16[512,128]{1,0:T(8,128)(2,1)S(1)}, u32[]{:S(2)}, u32[]{:S(2)}) collective-permute-start(bf16[512,128]{1,0:T(8,128)(2,1)S(1)} %get-tuple-element.71.refs_0_), channel_id=1, source_target_pairs={{0,8},{4,12},{8,0},{12,4},{16,24},{20,28},{24,16},{28,20},{1,9},{5... | collective-permute-start | bytes 393224 | tf_op jit(solution)/shard_map/ppermute | solution.py:126
  14.6 5.8 %collective-permute-start.6 = (bf16[512,128]{1,0:T(8,128)(2,1)S(1)}, bf16[512,128]{1,0:T(8,128)(2,1)S(1)}, u32[]{:S(2)}, u32[]{:S(2)}) collective-permute-start(bf16[512,128]{1,0:T(8,128)(2,1)S(1)} %get-tuple-element.71.refs_0_), channel_id=1, source_target_pairs={{0,16},{4,20},{8,24},{12,28},{16,0},{20,4},{24,8},{28,12},{1,17},{... | collective-permute-start | bytes 393224 | tf_op jit(solution)/shard_map/ppermute | solution.py:126
  16.1 5.9 %collective-permute-start.8 = (bf16[512,128]{1,0:T(8,128)(2,1)S(1)}, bf16[512,128]{1,0:T(8,128)(2,1)S(1)}, u32[]{:S(2)}, u32[]{:S(2)}) collective-permute-start(bf16[512,128]{1,0:T(8,128)(2,1)S(1)} %get-tuple-element.71.refs_0_), channel_id=1, source_target_pairs={{0,24},{4,28},{8,16},{12,20},{16,8},{20,12},{24,0},{28,4},{1,25},{... | collective-permute-start | bytes 393224 | tf_op jit(solution)/shard_map/ppermute | solution.py:126
  19.1 2.8 %collective-permute-start.3 = (bf16[512,128]{1,0:T(8,128)(2,1)S(1)}, bf16[512,128]{1,0:T(8,128)(2,1)S(1)}, u32[]{:S(2)}, u32[]{:S(2)}) collective-permute-start(bf16[512,128]{1,0:T(8,128)(2,1)S(1)} %get-tuple-element.71.refs_0_), channel_id=1, source_target_pairs={{0,4},{4,0},{8,12},{12,8},{16,20},{20,16},{24,28},{28,24},{1,5},{5... | collective-permute-start | bytes 393224 | tf_op jit(solution)/shard_map/ppermute | solution.py:126
  19.2 2.7 %collective-permute-start.5 = (bf16[512,128]{1,0:T(8,128)(2,1)S(1)}, bf16[512,128]{1,0:T(8,128)(2,1)S(1)}, u32[]{:S(2)}, u32[]{:S(2)}) collective-permute-start(bf16[512,128]{1,0:T(8,128)(2,1)S(1)} %collective-permute-done.4.refs_2_), channel_id=1, source_target_pairs={{0,4},{4,0},{8,12},{12,8},{16,20},{20,16},{24,28},{28,24},{1,5},{5... | collective-permute-start | bytes 393224 | tf_op jit(solution)/shard_map/ppermute | solution.py:126
  20.3 1.7 %collective-permute-start.7 = (bf16[512,128]{1,0:T(8,128)(2,1)S(1)}, bf16[512,128]{1,0:T(8,128)(2,1)S(1)}, u32[]{:S(2)}, u32[]{:S(2)}) collective-permute-start(bf16[512,128]{1,0:T(8,128)(2,1)S(1)} %collective-permute-done.6.refs_4_), channel_id=1, source_target_pairs={{0,4},{4,0},{8,12},{12,8},{16,20},{20,16},{24,28},{28,24},{1,5},{5... | collective-permute-start | bytes 393224 | tf_op jit(solution)/shard_map/ppermute | solution.py:126
  22.0 1.3 collective-permute-start.9
  24.5 16.0 %collective-permute-start.26 = (f32[128,256]{1,0:T(8,128)S(1)}, f32[128,256]{1,0:T(8,128)S(1)}, u32[]{:S(2)}, u32[]{:S(2)}) collective-permute-start(f32[128,256]{1,0:T(8,128)S(1)} %shard_map.128), channel_id=1, source_target_pairs={{0,1},{1,0},{2,3},{3,2},{4,5},{5,4},{6,7},{7,6},{8,9},{9,8},{10,11... | collective-permute-start | bytes 393224 | tf_op jit(solution)/shard_map/ppermute | solution.py:126
  24.6 4.8 %copy-start.6 = (f32[512,64]{0,1:T(8,128)S(1)}, f32[512,64]{0,1:T(8,128)}, u32[]{:S(2)}) copy-start(f32[512,64]{0,1:T(8,128)} %param.16) | copy-start | bytes 393220
  24.6 4.8 %copy-start.7 = (f32[512,64]{0,1:T(8,128)S(1)}, f32[512,64]{0,1:T(8,128)}, u32[]{:S(2)}) copy-start(f32[512,64]{0,1:T(8,128)} %param.13) | copy-start | bytes 393220
  24.6 9.8 %copy-start = (bf16[1,8,512,512]{3,2,1,0:T(8,128)(2,1)S(1)}, bf16[1,8,512,512]{3,2,1,0:T(8,128)(2,1)}, u32[]{:S(2)}) copy-start(bf16[1,8,512,512]{3,2,1,0:T(8,128)(2,1)} %activity_ref.3) | copy-start | bytes 12582916
  24.6 9.8 %copy-start.2 = (f32[8,256]{1,0:T(8,128)S(1)}, f32[8,256]{1,0:T(8,128)}, u32[]{:S(2)}) copy-start(f32[8,256]{1,0:T(8,128)} %time_ref.7) | copy-start | bytes 24580
  24.9 16.6 %copy-start.8 = (f32[512,64]{0,1:T(8,128)S(1)}, f32[512,64]{0,1:T(8,128)}, u32[]{:S(2)}) copy-start(f32[512,64]{0,1:T(8,128)} %param.17) | copy-start | bytes 393220
  24.9 9.3 %collective-permute-start.10 = (bf16[256,128]{1,0:T(8,128)(2,1)S(1)}, bf16[256,128]{1,0:T(8,128)(2,1)S(1)}, u32[]{:S(2)}, u32[]{:S(2)}) collective-permute-start(bf16[256,128]{1,0:T(8,128)(2,1)S(1)} %get-tuple-element.73), channel_id=1, source_target_pairs={{0,1},{1,0},{2,3},{3,2},{4,5},{5,4},{6,7},{7,6},{8,9},{9,8},{10,11... | collective-permute-start | bytes 196616 | tf_op jit(solution)/shard_map/ppermute | solution.py:126
  26.9 7.5 %collective-permute-start.11 = (bf16[256,128]{1,0:T(8,128)(2,1)S(1)}, bf16[256,128]{1,0:T(8,128)(2,1)S(1)}, u32[]{:S(2)}, u32[]{:S(2)}) collective-permute-start(bf16[256,128]{1,0:T(8,128)(2,1)S(1)} %get-tuple-element.74), channel_id=1, source_target_pairs={{0,2},{1,3},{2,0},{3,1},{4,6},{5,7},{6,4},{7,5},{8,10},{9,11},{10,... | collective-permute-start | bytes 196616 | tf_op jit(solution)/shard_map/ppermute | solution.py:126
  26.9 7.5 %collective-permute-start.12 = (bf16[256,128]{1,0:T(8,128)(2,1)S(1)}, bf16[256,128]{1,0:T(8,128)(2,1)S(1)}, u32[]{:S(2)}, u32[]{:S(2)}) collective-permute-start(bf16[256,128]{1,0:T(8,128)(2,1)S(1)} %get-tuple-element.75), channel_id=1, source_target_pairs={{0,3},{1,2},{2,1},{3,0},{4,7},{5,6},{6,5},{7,4},{8,11},{9,10},{10,... | collective-permute-start | bytes 196616 | tf_op jit(solution)/shard_map/ppermute | solution.py:126
  36.0 7.5 %collective-permute-start.13 = (f32[256,128]{1,0:T(8,128)S(1)}, f32[256,128]{1,0:T(8,128)S(1)}, u32[]{:S(2)}, u32[]{:S(2)}) collective-permute-start(f32[256,128]{1,0:T(8,128)S(1)} %get-tuple-element.77), channel_id=1, source_target_pairs={{0,1},{1,0},{2,3},{3,2},{4,5},{5,4},{6,7},{7,6},{8,9},{9,8},{10,11... | collective-permute-start | bytes 393224 | tf_op jit(solution)/shard_map/ppermute | solution.py:126
  37.7 15.7 %collective-permute-start.14 = (f32[256,128]{1,0:T(8,128)S(1)}, f32[256,128]{1,0:T(8,128)S(1)}, u32[]{:S(2)}, u32[]{:S(2)}) collective-permute-start(f32[256,128]{1,0:T(8,128)S(1)} %get-tuple-element.78), channel_id=1, source_target_pairs={{0,2},{1,3},{2,0},{3,1},{4,6},{5,7},{6,4},{7,5},{8,10},{9,11},{10,... | collective-permute-start | bytes 393224 | tf_op jit(solution)/shard_map/ppermute | solution.py:126
  38.7 14.7 %collective-permute-start.15 = (f32[256,128]{1,0:T(8,128)S(1)}, f32[256,128]{1,0:T(8,128)S(1)}, u32[]{:S(2)}, u32[]{:S(2)}) collective-permute-start(f32[256,128]{1,0:T(8,128)S(1)} %get-tuple-element.79), channel_id=1, source_target_pairs={{0,3},{1,2},{2,1},{3,0},{4,7},{5,6},{6,5},{7,4},{8,11},{9,10},{10,... | collective-permute-start | bytes 393224 | tf_op jit(solution)/shard_map/ppermute | solution.py:126
  40.5 19.7 %collective-permute-start.27 = (f32[128,256]{1,0:T(8,128)S(1)}, f32[128,256]{1,0:T(8,128)S(1)}, u32[]{:S(2)}, u32[]{:S(2)}) collective-permute-start(f32[128,256]{1,0:T(8,128)S(1)} %add.37), channel_id=1, source_target_pairs={{0,2},{1,3},{2,0},{3,1},{4,6},{5,7},{6,4},{7,5},{8,10},{9,11},{10,... | collective-permute-start | bytes 393224 | tf_op jit(solution)/shard_map/ppermute | solution.py:126
  41.7 18.5 %collective-permute-start.23 = (f32[192,128]{1,0:T(8,128)S(1)}, f32[192,128]{1,0:T(8,128)S(1)}, u32[]{:S(2)}, u32[]{:S(2)}) collective-permute-start(f32[192,128]{1,0:T(8,128)S(1)} %get-tuple-element.90), channel_id=1, source_target_pairs={{0,1},{1,0},{2,3},{3,2},{4,5},{5,4},{6,7},{7,6},{8,9},{9,8},{10,11... | collective-permute-start | bytes 294920 | tf_op jit(solution)/shard_map/ppermute | solution.py:126
  43.6 18.0 %collective-permute-start.24 = (f32[192,128]{1,0:T(8,128)S(1)}, f32[192,128]{1,0:T(8,128)S(1)}, u32[]{:S(2)}, u32[]{:S(2)}) collective-permute-start(f32[192,128]{1,0:T(8,128)S(1)} %get-tuple-element.91), channel_id=1, source_target_pairs={{0,2},{1,3},{2,0},{3,1},{4,6},{5,7},{6,4},{7,5},{8,10},{9,11},{10,... | collective-permute-start | bytes 294920 | tf_op jit(solution)/shard_map/ppermute | solution.py:126
  53.9 14.3 %collective-permute-start.21 = (f32[256,128]{1,0:T(8,128)S(1)}, f32[256,128]{1,0:T(8,128)S(1)}, u32[]{:S(2)}, u32[]{:S(2)}) collective-permute-start(f32[256,128]{1,0:T(8,128)S(1)} %get-tuple-element.87), channel_id=1, source_target_pairs={{0,4},{4,0},{8,12},{12,8},{16,20},{20,16},{24,28},{28,24},{1,5},{5... | collective-permute-start | bytes 393224 | tf_op jit(solution)/shard_map/ppermute | solution.py:126
  54.0 14.9 %collective-permute-start.19 = (f32[256,128]{1,0:T(8,128)S(1)}, f32[256,128]{1,0:T(8,128)S(1)}, u32[]{:S(2)}, u32[]{:S(2)}) collective-permute-start(f32[256,128]{1,0:T(8,128)S(1)} %get-tuple-element.85), channel_id=1, source_target_pairs={{0,4},{4,0},{8,12},{12,8},{16,20},{20,16},{24,28},{28,24},{1,5},{5... | collective-permute-start | bytes 393224 | tf_op jit(solution)/shard_map/ppermute | solution.py:126
  60.1 10.2 %collective-permute-start.17 = (f32[256,128]{1,0:T(8,128)S(1)}, f32[256,128]{1,0:T(8,128)S(1)}, u32[]{:S(2)}, u32[]{:S(2)}) collective-permute-start(f32[256,128]{1,0:T(8,128)S(1)} %get-tuple-element.83), channel_id=1, source_target_pairs={{0,4},{4,0},{8,12},{12,8},{16,20},{20,16},{24,28},{28,24},{1,5},{5... | collective-permute-start | bytes 393224 | tf_op jit(solution)/shard_map/ppermute | solution.py:126
  60.2 11.7 %collective-permute-start.28 = (f32[128,256]{1,0:T(8,128)S(1)}, f32[128,256]{1,0:T(8,128)S(1)}, u32[]{:S(2)}, u32[]{:S(2)}) collective-permute-start(f32[128,256]{1,0:T(8,128)S(1)} %add.38.refs_0_), channel_id=1, source_target_pairs={{0,4},{4,0},{8,12},{12,8},{16,20},{20,16},{24,28},{28,24},{1,5},{5... | collective-permute-start | bytes 393224 | tf_op jit(solution)/shard_map/ppermute | solution.py:126
  61.6 6.4 %collective-permute-start.25 = (f32[192,128]{1,0:T(8,128)S(1)}, f32[192,128]{1,0:T(8,128)S(1)}, u32[]{:S(2)}, u32[]{:S(2)}) collective-permute-start(f32[192,128]{1,0:T(8,128)S(1)} %get-tuple-element.92), channel_id=1, source_target_pairs={{0,3},{1,2},{2,1},{3,0},{4,7},{5,6},{6,5},{7,4},{8,11},{9,10},{10,... | collective-permute-start | bytes 294920 | tf_op jit(solution)/shard_map/ppermute | solution.py:126
  68.1 13.0 %collective-permute-start.16 = (f32[256,128]{1,0:T(8,128)S(1)}, f32[256,128]{1,0:T(8,128)S(1)}, u32[]{:S(2)}, u32[]{:S(2)}) collective-permute-start(f32[256,128]{1,0:T(8,128)S(1)} %get-tuple-element.81), channel_id=1, source_target_pairs={{0,4},{4,0},{8,12},{12,8},{16,20},{20,16},{24,28},{28,24},{1,5},{5... | collective-permute-start | bytes 393224 | tf_op jit(solution)/shard_map/ppermute | solution.py:126
  68.2 12.9 %collective-permute-start.22 = (f32[256,128]{1,0:T(8,128)S(1)}, f32[256,128]{1,0:T(8,128)S(1)}, u32[]{:S(2)}, u32[]{:S(2)}) collective-permute-start(f32[256,128]{1,0:T(8,128)S(1)} %add.35), channel_id=1, source_target_pairs={{0,24},{4,28},{8,16},{12,20},{16,8},{20,12},{24,0},{28,4},{1,25},{... | collective-permute-start | bytes 393224 | tf_op jit(solution)/shard_map/ppermute | solution.py:126
  68.9 12.3 %collective-permute-start.20 = (f32[256,128]{1,0:T(8,128)S(1)}, f32[256,128]{1,0:T(8,128)S(1)}, u32[]{:S(2)}, u32[]{:S(2)}) collective-permute-start(f32[256,128]{1,0:T(8,128)S(1)} %add.34), channel_id=1, source_target_pairs={{0,16},{4,20},{8,24},{12,28},{16,0},{20,4},{24,8},{28,12},{1,17},{... | collective-permute-start | bytes 393224 | tf_op jit(solution)/shard_map/ppermute | solution.py:126
  70.4 10.8 %collective-permute-start.18 = (f32[256,128]{1,0:T(8,128)S(1)}, f32[256,128]{1,0:T(8,128)S(1)}, u32[]{:S(2)}, u32[]{:S(2)}) collective-permute-start(f32[256,128]{1,0:T(8,128)S(1)} %add.33), channel_id=1, source_target_pairs={{0,8},{4,12},{8,0},{12,4},{16,24},{20,28},{24,16},{28,20},{1,9},{5... | collective-permute-start | bytes 393224 | tf_op jit(solution)/shard_map/ppermute | solution.py:126
  82.3 6.4 %collective-permute-start.33 = (bf16[512,128]{1,0:T(8,128)(2,1)S(1)}, bf16[512,128]{1,0:T(8,128)(2,1)S(1)}, u32[]{:S(2)}, u32[]{:S(2)}) collective-permute-start(bf16[512,128]{1,0:T(8,128)(2,1)S(1)} %get-tuple-element.102.refs_0_), channel_id=1, source_target_pairs={{0,8},{4,12},{8,0},{12,4},{16,24},{20,28},{24,16},{28,20},{1,9},{5... | collective-permute-start | bytes 393224 | tf_op jit(solution)/shard_map/ppermute | solution.py:126
  82.9 6.3 %collective-permute-start.35 = (bf16[512,128]{1,0:T(8,128)(2,1)S(1)}, bf16[512,128]{1,0:T(8,128)(2,1)S(1)}, u32[]{:S(2)}, u32[]{:S(2)}) collective-permute-start(bf16[512,128]{1,0:T(8,128)(2,1)S(1)} %get-tuple-element.102.refs_0_), channel_id=1, source_target_pairs={{0,16},{4,20},{8,24},{12,28},{16,0},{20,4},{24,8},{28,12},{1,17},{... | collective-permute-start | bytes 393224 | tf_op jit(solution)/shard_map/ppermute | solution.py:126
  83.5 7.2 %collective-permute-start.37 = (bf16[512,128]{1,0:T(8,128)(2,1)S(1)}, bf16[512,128]{1,0:T(8,128)(2,1)S(1)}, u32[]{:S(2)}, u32[]{:S(2)}) collective-permute-start(bf16[512,128]{1,0:T(8,128)(2,1)S(1)} %get-tuple-element.102.refs_0_), channel_id=1, source_target_pairs={{0,24},{4,28},{8,16},{12,20},{16,8},{20,12},{24,0},{28,4},{1,25},{... | collective-permute-start | bytes 393224 | tf_op jit(solution)/shard_map/ppermute | solution.py:126
  85.9 4.8 %collective-permute-start.32 = (bf16[512,128]{1,0:T(8,128)(2,1)S(1)}, bf16[512,128]{1,0:T(8,128)(2,1)S(1)}, u32[]{:S(2)}, u32[]{:S(2)}) collective-permute-start(bf16[512,128]{1,0:T(8,128)(2,1)S(1)} %get-tuple-element.102.refs_0_), channel_id=1, source_target_pairs={{0,4},{4,0},{8,12},{12,8},{16,20},{20,16},{24,28},{28,24},{1,5},{5... | collective-permute-start | bytes 393224 | tf_op jit(solution)/shard_map/ppermute | solution.py:126
  88.8 1.9 %collective-permute-start.34 = (bf16[512,128]{1,0:T(8,128)(2,1)S(1)}, bf16[512,128]{1,0:T(8,128)(2,1)S(1)}, u32[]{:S(2)}, u32[]{:S(2)}) collective-permute-start(bf16[512,128]{1,0:T(8,128)(2,1)S(1)} %collective-permute-done.33.refs_2_), channel_id=1, source_target_pairs={{0,4},{4,0},{8,12},{12,8},{16,20},{20,16},{24,28},{28,24},{1,5},{5... | collective-permute-start | bytes 393224 | tf_op jit(solution)/shard_map/ppermute | solution.py:126
  89.2 1.5 collective-permute-start.36
  90.7 1.3 collective-permute-start.38
  92.3 5.9 %collective-permute-start.39 = (bf16[256,128]{1,0:T(8,128)(2,1)S(1)}, bf16[256,128]{1,0:T(8,128)(2,1)S(1)}, u32[]{:S(2)}, u32[]{:S(2)}) collective-permute-start(bf16[256,128]{1,0:T(8,128)(2,1)S(1)} %get-tuple-element.104), channel_id=1, source_target_pairs={{0,1},{1,0},{2,3},{3,2},{4,5},{5,4},{6,7},{7,6},{8,9},{9,8},{10,11... | collective-permute-start | bytes 196616 | tf_op jit(solution)/shard_map/ppermute | solution.py:126
  92.4 8.6 %collective-permute-start.40 = (bf16[256,128]{1,0:T(8,128)(2,1)S(1)}, bf16[256,128]{1,0:T(8,128)(2,1)S(1)}, u32[]{:S(2)}, u32[]{:S(2)}) collective-permute-start(bf16[256,128]{1,0:T(8,128)(2,1)S(1)} %get-tuple-element.105), channel_id=1, source_target_pairs={{0,2},{1,3},{2,0},{3,1},{4,6},{5,7},{6,4},{7,5},{8,10},{9,11},{10,... | collective-permute-start | bytes 196616 | tf_op jit(solution)/shard_map/ppermute | solution.py:126
  94.4 6.7 %collective-permute-start.41 = (bf16[256,128]{1,0:T(8,128)(2,1)S(1)}, bf16[256,128]{1,0:T(8,128)(2,1)S(1)}, u32[]{:S(2)}, u32[]{:S(2)}) collective-permute-start(bf16[256,128]{1,0:T(8,128)(2,1)S(1)} %get-tuple-element.106), channel_id=1, source_target_pairs={{0,3},{1,2},{2,1},{3,0},{4,7},{5,6},{6,5},{7,4},{8,11},{9,10},{10,... | collective-permute-start | bytes 196616 | tf_op jit(solution)/shard_map/ppermute | solution.py:126
  98.2 8.9 %collective-permute-start.52 = (f32[128,256]{1,0:T(8,128)S(1)}, f32[128,256]{1,0:T(8,128)S(1)}, u32[]{:S(2)}, u32[]{:S(2)}) collective-permute-start(f32[128,256]{1,0:T(8,128)S(1)} %shard_map.136), channel_id=1, source_target_pairs={{0,1},{1,0},{2,3},{3,2},{4,5},{5,4},{6,7},{7,6},{8,9},{9,8},{10,11... | collective-permute-start | bytes 393224 | tf_op jit(solution)/shard_map/ppermute | solution.py:126
  102.6 6.3 %collective-permute-start.42 = (f32[256,128]{1,0:T(8,128)S(1)}, f32[256,128]{1,0:T(8,128)S(1)}, u32[]{:S(2)}, u32[]{:S(2)}) collective-permute-start(f32[256,128]{1,0:T(8,128)S(1)} %get-tuple-element.108), channel_id=1, source_target_pairs={{0,1},{1,0},{2,3},{3,2},{4,5},{5,4},{6,7},{7,6},{8,9},{9,8},{10,11... | collective-permute-start | bytes 393224 | tf_op jit(solution)/shard_map/ppermute | solution.py:126
  103.9 14.8 %collective-permute-start.43 = (f32[256,128]{1,0:T(8,128)S(1)}, f32[256,128]{1,0:T(8,128)S(1)}, u32[]{:S(2)}, u32[]{:S(2)}) collective-permute-start(f32[256,128]{1,0:T(8,128)S(1)} %get-tuple-element.109), channel_id=1, source_target_pairs={{0,2},{1,3},{2,0},{3,1},{4,6},{5,7},{6,4},{7,5},{8,10},{9,11},{10,... | collective-permute-start | bytes 393224 | tf_op jit(solution)/shard_map/ppermute | solution.py:126
  105.6 13.1 %collective-permute-start.44 = (f32[256,128]{1,0:T(8,128)S(1)}, f32[256,128]{1,0:T(8,128)S(1)}, u32[]{:S(2)}, u32[]{:S(2)}) collective-permute-start(f32[256,128]{1,0:T(8,128)S(1)} %get-tuple-element.110), channel_id=1, source_target_pairs={{0,3},{1,2},{2,1},{3,0},{4,7},{5,6},{6,5},{7,4},{8,11},{9,10},{10,... | collective-permute-start | bytes 393224 | tf_op jit(solution)/shard_map/ppermute | solution.py:126
  107.1 15.7 %collective-permute-start.53 = (f32[128,256]{1,0:T(8,128)S(1)}, f32[128,256]{1,0:T(8,128)S(1)}, u32[]{:S(2)}, u32[]{:S(2)}) collective-permute-start(f32[128,256]{1,0:T(8,128)S(1)} %add.42), channel_id=1, source_target_pairs={{0,2},{1,3},{2,0},{3,1},{4,6},{5,7},{6,4},{7,5},{8,10},{9,11},{10,... | collective-permute-start | bytes 393224 | tf_op jit(solution)/shard_map/ppermute | solution.py:126
  119.1 4.4 %collective-permute-start.50 = (f32[256,128]{1,0:T(8,128)S(1)}, f32[256,128]{1,0:T(8,128)S(1)}, u32[]{:S(2)}, u32[]{:S(2)}) collective-permute-start(f32[256,128]{1,0:T(8,128)S(1)} %get-tuple-element.118), channel_id=1, source_target_pairs={{0,4},{4,0},{8,12},{12,8},{16,20},{20,16},{24,28},{28,24},{1,5},{5... | collective-permute-start | bytes 393224 | tf_op jit(solution)/shard_map/ppermute | solution.py:126
  119.2 4.3 %collective-permute-start.48 = (f32[256,128]{1,0:T(8,128)S(1)}, f32[256,128]{1,0:T(8,128)S(1)}, u32[]{:S(2)}, u32[]{:S(2)}) collective-permute-start(f32[256,128]{1,0:T(8,128)S(1)} %get-tuple-element.116), channel_id=1, source_target_pairs={{0,4},{4,0},{8,12},{12,8},{16,20},{20,16},{24,28},{28,24},{1,5},{5... | collective-permute-start | bytes 393224 | tf_op jit(solution)/shard_map/ppermute | solution.py:126
  119.7 6.7 %collective-permute-start.46 = (f32[256,128]{1,0:T(8,128)S(1)}, f32[256,128]{1,0:T(8,128)S(1)}, u32[]{:S(2)}, u32[]{:S(2)}) collective-permute-start(f32[256,128]{1,0:T(8,128)S(1)} %get-tuple-element.114), channel_id=1, source_target_pairs={{0,4},{4,0},{8,12},{12,8},{16,20},{20,16},{24,28},{28,24},{1,5},{5... | collective-permute-start | bytes 393224 | tf_op jit(solution)/shard_map/ppermute | solution.py:126
  122.8 4.7 %collective-permute-start.54 = (f32[128,256]{1,0:T(8,128)S(1)}, f32[128,256]{1,0:T(8,128)S(1)}, u32[]{:S(2)}, u32[]{:S(2)}) collective-permute-start(f32[128,256]{1,0:T(8,128)S(1)} %add.43.refs_0_), channel_id=1, source_target_pairs={{0,4},{4,0},{8,12},{12,8},{16,20},{20,16},{24,28},{28,24},{1,5},{5... | collective-permute-start | bytes 393224 | tf_op jit(solution)/shard_map/ppermute | solution.py:126
  122.9 21.6 %collective-permute-start.29 = (f32[64,128]{1,0:T(8,128)S(1)}, f32[64,128]{1,0:T(8,128)S(1)}, u32[]{:S(2)}, u32[]{:S(2)}) collective-permute-start(f32[64,128]{1,0:T(8,128)S(1)} %get-tuple-element.98), channel_id=1, source_target_pairs={{0,1},{1,0},{2,3},{3,2},{4,5},{5,4},{6,7},{7,6},{8,9},{9,8},{10,11... | collective-permute-start | bytes 98312 | tf_op jit(solution)/shard_map/ppermute | solution.py:126
  123.5 13.3 %collective-permute-start.45 = (f32[256,128]{1,0:T(8,128)S(1)}, f32[256,128]{1,0:T(8,128)S(1)}, u32[]{:S(2)}, u32[]{:S(2)}) collective-permute-start(f32[256,128]{1,0:T(8,128)S(1)} %get-tuple-element.112), channel_id=1, source_target_pairs={{0,4},{4,0},{8,12},{12,8},{16,20},{20,16},{24,28},{28,24},{1,5},{5... | collective-permute-start | bytes 393224 | tf_op jit(solution)/shard_map/ppermute | solution.py:126
  123.6 15.3 %collective-permute-start.51 = (f32[256,128]{1,0:T(8,128)S(1)}, f32[256,128]{1,0:T(8,128)S(1)}, u32[]{:S(2)}, u32[]{:S(2)}) collective-permute-start(f32[256,128]{1,0:T(8,128)S(1)} %add.41), channel_id=1, source_target_pairs={{0,24},{4,28},{8,16},{12,20},{16,8},{20,12},{24,0},{28,4},{1,25},{... | collective-permute-start | bytes 393224 | tf_op jit(solution)/shard_map/ppermute | solution.py:126
  126.4 14.6 %collective-permute-start.49 = (f32[256,128]{1,0:T(8,128)S(1)}, f32[256,128]{1,0:T(8,128)S(1)}, u32[]{:S(2)}, u32[]{:S(2)}) collective-permute-start(f32[256,128]{1,0:T(8,128)S(1)} %add.40), channel_id=1, source_target_pairs={{0,16},{4,20},{8,24},{12,28},{16,0},{20,4},{24,8},{28,12},{1,17},{... | collective-permute-start | bytes 393224 | tf_op jit(solution)/shard_map/ppermute | solution.py:126
  127.5 13.5 %collective-permute-start.47 = (f32[256,128]{1,0:T(8,128)S(1)}, f32[256,128]{1,0:T(8,128)S(1)}, u32[]{:S(2)}, u32[]{:S(2)}) collective-permute-start(f32[256,128]{1,0:T(8,128)S(1)} %add.39), channel_id=1, source_target_pairs={{0,8},{4,12},{8,0},{12,4},{16,24},{20,28},{24,16},{28,20},{1,9},{5... | collective-permute-start | bytes 393224 | tf_op jit(solution)/shard_map/ppermute | solution.py:126
  136.8 9.8 %collective-permute-start.30 = (f32[64,128]{1,0:T(8,128)S(1)}, f32[64,128]{1,0:T(8,128)S(1)}, u32[]{:S(2)}, u32[]{:S(2)}) collective-permute-start(f32[64,128]{1,0:T(8,128)S(1)} %get-tuple-element.99), channel_id=1, source_target_pairs={{0,2},{1,3},{2,0},{3,1},{4,6},{5,7},{6,4},{7,5},{8,10},{9,11},{10,... | collective-permute-start | bytes 98312 | tf_op jit(solution)/shard_map/ppermute | solution.py:126
  138.9 7.7 %collective-permute-start.31 = (f32[64,128]{1,0:T(8,128)S(1)}, f32[64,128]{1,0:T(8,128)S(1)}, u32[]{:S(2)}, u32[]{:S(2)}) collective-permute-start(f32[64,128]{1,0:T(8,128)S(1)} %get-tuple-element.100), channel_id=1, source_target_pairs={{0,3},{1,2},{2,1},{3,0},{4,7},{5,6},{6,5},{7,4},{8,11},{9,10},{10,... | collective-permute-start | bytes 98312 | tf_op jit(solution)/shard_map/ppermute | solution.py:126
  142.2 5.2 %collective-permute-start.55 = (f32[64,128]{1,0:T(8,128)S(1)}, f32[64,128]{1,0:T(8,128)S(1)}, u32[]{:S(2)}, u32[]{:S(2)}) collective-permute-start(f32[64,128]{1,0:T(8,128)S(1)} %get-tuple-element.124), channel_id=1, source_target_pairs={{0,1},{1,0},{2,3},{3,2},{4,5},{5,4},{6,7},{7,6},{8,9},{9,8},{10,11... | collective-permute-start | bytes 98312 | tf_op jit(solution)/shard_map/ppermute | solution.py:126
  142.2 5.1 %collective-permute-start.56 = (f32[64,128]{1,0:T(8,128)S(1)}, f32[64,128]{1,0:T(8,128)S(1)}, u32[]{:S(2)}, u32[]{:S(2)}) collective-permute-start(f32[64,128]{1,0:T(8,128)S(1)} %get-tuple-element.125), channel_id=1, source_target_pairs={{0,2},{1,3},{2,0},{3,1},{4,6},{5,7},{6,4},{7,5},{8,10},{9,11},{10,... | collective-permute-start | bytes 98312 | tf_op jit(solution)/shard_map/ppermute | solution.py:126
  144.5 5.7 %collective-permute-start.57 = (f32[64,128]{1,0:T(8,128)S(1)}, f32[64,128]{1,0:T(8,128)S(1)}, u32[]{:S(2)}, u32[]{:S(2)}) collective-permute-start(f32[64,128]{1,0:T(8,128)S(1)} %get-tuple-element.126), channel_id=1, source_target_pairs={{0,3},{1,2},{2,1},{3,0},{4,7},{5,6},{6,5},{7,4},{8,11},{9,10},{10,... | collective-permute-start | bytes 98312 | tf_op jit(solution)/shard_map/ppermute | solution.py:126
  (3 other events, 2.0 us)
where the time goes:
time: 151 us
  waiting for transfers between devices  60.9 us (40%)
  starting transfers between devices  55.8 us (37%)
  Pallas kernels  30 us (20%)
  local copies, waits for them, and re-layouts  2.92 us (2%)
    ppermute x58, waiting for transfers between devices, swap(): return lax.ppermute(x, axis, [(i, i ^ mask) for i in range(size)])  60.9 us
    ppermute x58, starting transfers between devices, swap(): return lax.ppermute(x, axis, [(i, i ^ mask) for i in range(size)])  55.8 us
    pallas_call x21, Pallas kernels, kernel_call(): pl.pallas_call(kernel, out_shape=tuple(out_shape), in_specs=[spec] * len(...  30 us
  transfers between devices with their start and end apart: 58, of which 21 were waited for; matrix products, arithmetic and copies ran while one was open for 0% of the time, Pallas kernels for 18%

commit v1 on v0

--- a/solution.py
+++ b/solution.py
@@ -127,7 +127,10 @@
 
 
 def swaps(pieces):
-    return [pieces[0]] + [swap(pieces[d], "narrow", d) for d in range(1, len(pieces))]
+    received = list(pieces)
+    for d in reversed(range(1, len(pieces))):
+        received[d] = swap(pieces[d], "narrow", d)
+    return received
 
 
 def for_each_position(body):
@@ -196,7 +199,7 @@
     height = pieces[0].shape[0] // 3
     for d, piece in enumerate(pieces):
         rows = rows_of(d, height)
-        outputs[0][rows, :] = piece[:height]
+        outputs[0][rows, :] = piece[:height] + piece[height : 2 * height]
         outputs[1][rows, :] = piece[height : 2 * height]
         outputs[3][rows, :] = piece[2 * height :]
     outputs[2][...] = factor_ref[...] + outputs[3][...]
@@ -246,7 +249,9 @@
 
 def all_pairs(pair):
     chips = lax.axis_size("wide") // 2
-    same = [pair] + [swap(pair, "wide", 2 * m) for m in range(1, chips)]
+    same = [pair] * chips
+    for m in reversed(range(1, chips)):
+        same[m] = swap(pair, "wide", 2 * m)
     return [x for a in same for x in (a, swap(a, "wide", 1))]
 
 
@@ -316,10 +321,11 @@
         functools.partial(place_kernel, len(received)), [shape(received[0].shape)] * size,
         table, *received,
     )
-    arrived = [swap(placed[2 * m + 1], "wide", 1) for m in range(1, size // 2)]
-    terms = [placed[0], swap(placed[1], "wide", 1)]
-    for m in range(1, size // 2):
-        terms.append(swap(placed[2 * m] + arrived[m - 1], "wide", 2 * m))
+    order = [*reversed(range(1, size // 2)), 0]
+    arrived = {m: swap(placed[2 * m + 1], "wide", 1) for m in order}
+    terms = [placed[0], arrived[0]]
+    for m in order[:-1]:
+        terms.append(swap(placed[2 * m] + arrived[m], "wide", 2 * m))
     return terms
 
 
@@ -416,7 +422,7 @@
     rows = shape((rank, pieces[0].shape[1]))
     pair = shape((2 * rank, rows.shape[1]), jnp.bfloat16)
     item_rows, pair = kernel_call(functools.partial(pair_kernel, count), [rows, pair], *pieces)
-    stack = jnp.concatenate([user_factor + user_dual, user_dual, item_dual])
+    stack = jnp.concatenate([user_factor, user_dual, item_dual])
     user_shifted, udual_rows, item_shifted, idual_rows = kernel_call(
         functools.partial(assemble_kernel, count), [rows] * 4,
         item_rows, *swaps(split(stack)),

time: 151 us -> 148 us (0.980)
  waiting for transfers between devices: 60.9 us -> 58.7 us
    ppermute x58, waiting for transfers between devices: 60.9 us -> 58.7 us  [swap(): return lax.ppermute(x, axis, [(i, i ^ mask) for i in range(size)])]
  transfers between devices with their start and end apart: 58 -> 58, of which waited for: 21 -> 20; matrix products, arithmetic and copies ran while one was open for 0% -> 0% of each run, Pallas kernels for 18% -> 19%
where the time goes in v1:
time: 148 us
  waiting for transfers between devices  58.7 us (40%)
  starting transfers between devices  54.9 us (37%)
  Pallas kernels  30 us (20%)
  local copies, waits for them, and re-layouts  2.91 us (2%)
    ppermute x58, waiting for transfers between devices, swap(): return lax.ppermute(x, axis, [(i, i ^ mask) for i in range(size)])  58.7 us
    ppermute x58, starting transfers between devices, swap(): return lax.ppermute(x, axis, [(i, i ^ mask) for i in range(size)])  54.9 us
    pallas_call x21, Pallas kernels, kernel_call(): pl.pallas_call(kernel, out_shape=tuple(out_shape), in_specs=[spec] * len(...  30 us
  transfers between devices with their start and end apart: 58, of which 20 were waited for; matrix products, arithmetic and copies ran while one was open for 0% of the time, Pallas kernels for 19%

profile of v1, /device:TPU:0, one launch (start us, length us, event | category | flops | bytes accessed | tf_op | source)
XLA Modules:
  0.0 147.8 jit_solution(2367378457608183558)
XLA Ops:
  0.6 0.9 copy-done.1
  1.6 3.1 %collective-permute-start = (f32[64,128]{1,0:T(8,128)S(1)}, f32[64,128]{1,0:T(8,128)S(1)}, u32[]{:S(2)}, u32[]{:S(2)}) collective-permute-start(f32[64,128]{1,0:T(8,128)S(1)} %get-tuple-element.68), channel_id=1, source_target_pairs={{0,1},{1,0},{2,3},{3,2},{4,5},{5,4},{6,7},{7,6},{8,9},{9,8},{10,11... | collective-permute-start | bytes 98312 | tf_op jit(solution)/shard_map/ppermute | solution.py:126
  4.7 2.6 %collective-permute-start.1 = (f32[64,128]{1,0:T(8,128)S(1)}, f32[64,128]{1,0:T(8,128)S(1)}, u32[]{:S(2)}, u32[]{:S(2)}) collective-permute-start(f32[64,128]{1,0:T(8,128)S(1)} %get-tuple-element.69), channel_id=1, source_target_pairs={{0,2},{1,3},{2,0},{3,1},{4,6},{5,7},{6,4},{7,5},{8,10},{9,11},{10,... | collective-permute-start | bytes 98312 | tf_op jit(solution)/shard_map/ppermute | solution.py:126
  7.3 2.8 %collective-permute-done.1.refs_2_ = f32[64,128]{1,0:T(8,128)S(1)} collective-permute-done((f32[64,128]{1,0:T(8,128)S(1)}, f32[64,128]{1,0:T(8,128)S(1)}, u32[]{:S(2)}, u32[]{:S(2)}) %collective-permute-start.1) | collective-permute-done | bytes 32800 | tf_op jit(solution)/shard_map/ppermute | solution.py:126
  10.1 2.9 %collective-permute-done.2.refs_3_ = f32[64,128]{1,0:T(8,128)S(1)} collective-permute-done((f32[64,128]{1,0:T(8,128)S(1)}, f32[64,128]{1,0:T(8,128)S(1)}, u32[]{:S(2)}, u32[]{:S(2)}) %collective-permute-start.2) | collective-permute-done | bytes 32800 | tf_op jit(solution)/shard_map/ppermute | solution.py:126
  13.0 1.6 %collective-permute-start.4 = (bf16[512,128]{1,0:T(8,128)(2,1)S(1)}, bf16[512,128]{1,0:T(8,128)(2,1)S(1)}, u32[]{:S(2)}, u32[]{:S(2)}) collective-permute-start(bf16[512,128]{1,0:T(8,128)(2,1)S(1)} %get-tuple-element.71.refs_0_), channel_id=1, source_target_pairs={{0,8},{4,12},{8,0},{12,4},{16,24},{20,28},{24,16},{28,20},{1,9},{5... | collective-permute-start | bytes 393224 | tf_op jit(solution)/shard_map/ppermute | solution.py:126
  14.6 1.5 %collective-permute-start.6 = (bf16[512,128]{1,0:T(8,128)(2,1)S(1)}, bf16[512,128]{1,0:T(8,128)(2,1)S(1)}, u32[]{:S(2)}, u32[]{:S(2)}) collective-permute-start(bf16[512,128]{1,0:T(8,128)(2,1)S(1)} %get-tuple-element.71.refs_0_), channel_id=1, source_target_pairs={{0,16},{4,20},{8,24},{12,28},{16,0},{20,4},{24,8},{28,12},{1,17},{... | collective-permute-start | bytes 393224 | tf_op jit(solution)/shard_map/ppermute | solution.py:126
  16.6 0.7 copy-done.3
  17.2 0.7 copy-done.4
  17.9 0.7 copy-done.5
  18.6 0.6 shard_map.120
  19.7 0.6 collective-permute-done.6.refs_4_
  20.3 1.6 %collective-permute-done.8.refs_6_ = bf16[512,128]{1,0:T(8,128)(2,1)S(1)} collective-permute-done((bf16[512,128]{1,0:T(8,128)(2,1)S(1)}, bf16[512,128]{1,0:T(8,128)(2,1)S(1)}, u32[]{:S(2)}, u32[]{:S(2)}) %collective-permute-start.8) | collective-permute-done | bytes 131104 | tf_op jit(solution)/shard_map/ppermute | solution.py:126
  22.0 1.3 collective-permute-done.9.refs_7_
  23.7 0.9 collective-permute-start.11
  24.6 3.5 %collective-permute-start.12 = (bf16[256,128]{1,0:T(8,128)(2,1)S(1)}, bf16[256,128]{1,0:T(8,128)(2,1)S(1)}, u32[]{:S(2)}, u32[]{:S(2)}) collective-permute-start(bf16[256,128]{1,0:T(8,128)(2,1)S(1)} %get-tuple-element.75), channel_id=1, source_target_pairs={{0,3},{1,2},{2,1},{3,0},{4,7},{5,6},{6,5},{7,4},{8,11},{9,10},{10,... | collective-permute-start | bytes 196616 | tf_op jit(solution)/shard_map/ppermute | solution.py:126
  28.0 1.2 shard_map.128
  29.3 2.8 %collective-permute-done.11.refs_2_ = bf16[256,128]{1,0:T(8,128)(2,1)S(1)} collective-permute-done((bf16[256,128]{1,0:T(8,128)(2,1)S(1)}, bf16[256,128]{1,0:T(8,128)(2,1)S(1)}, u32[]{:S(2)}, u32[]{:S(2)}) %collective-permute-start.11) | collective-permute-done | bytes 65568 | tf_op jit(solution)/shard_map/ppermute | solution.py:126
  32.4 1.5 %shard_map.124 = (f32[256,128]{1,0:T(8,128)S(1)}, f32[256,128]{1,0:T(8,128)S(1)}, f32[256,128]{1,0:T(8,128)S(1)}, f32[256,128]{1,0:T(8,128)S(1)}) custom-call(bf16[1,8,512,512]{3,2,1,0:T(8,128)(2,1)S(1)} %copy-done, f32[8,256]{1,0:T(8,128)S(1)} %copy-done.2, bf16[256,128]{1,0:T(8,128)(2,1)S(1)} %get-tuple-element.72.refs_0_, ...), custom_call_target="tpu_custom_call" | custom-call | flops 1073741824 | bytes 4988928 | tf_op jit(solution)/shard_map/pallas_call | solution.py:109
  33.9 1.3 collective-permute-start.13
  35.2 1.8 %collective-permute-start.14 = (f32[256,128]{1,0:T(8,128)S(1)}, f32[256,128]{1,0:T(8,128)S(1)}, u32[]{:S(2)}, u32[]{:S(2)}) collective-permute-start(f32[256,128]{1,0:T(8,128)S(1)} %get-tuple-element.78), channel_id=1, source_target_pairs={{0,2},{1,3},{2,0},{3,1},{4,6},{5,7},{6,4},{7,5},{8,10},{9,11},{10,... | collective-permute-start | bytes 393224 | tf_op jit(solution)/shard_map/ppermute | solution.py:126
  37.0 1.3 collective-permute-start.15
  38.9 2.9 %collective-permute-start.23 = (f32[192,128]{1,0:T(8,128)S(1)}, f32[192,128]{1,0:T(8,128)S(1)}, u32[]{:S(2)}, u32[]{:S(2)}) collective-permute-start(f32[192,128]{1,0:T(8,128)S(1)} %get-tuple-element.90), channel_id=1, source_target_pairs={{0,1},{1,0},{2,3},{3,2},{4,5},{5,4},{6,7},{7,6},{8,9},{9,8},{10,11... | collective-permute-start | bytes 294920 | tf_op jit(solution)/shard_map/ppermute | solution.py:126
  42.0 9.6 %collective-permute-done.14.refs_2_ = f32[256,128]{1,0:T(8,128)S(1)} collective-permute-done((f32[256,128]{1,0:T(8,128)S(1)}, f32[256,128]{1,0:T(8,128)S(1)}, u32[]{:S(2)}, u32[]{:S(2)}) %collective-permute-start.14) | collective-permute-done | bytes 131104 | tf_op jit(solution)/shard_map/ppermute | solution.py:126
  52.6 4.5 %collective-permute-done.27 = f32[128,256]{1,0:T(8,128)S(1)} collective-permute-done((f32[128,256]{1,0:T(8,128)S(1)}, f32[128,256]{1,0:T(8,128)S(1)}, u32[]{:S(2)}, u32[]{:S(2)}) %collective-permute-start.27) | collective-permute-done | bytes 131104 | tf_op jit(solution)/shard_map/ppermute | solution.py:126
  57.2 0.6 collective-permute-start.28
  58.2 1.6 %collective-permute-start.25 = (f32[192,128]{1,0:T(8,128)S(1)}, f32[192,128]{1,0:T(8,128)S(1)}, u32[]{:S(2)}, u32[]{:S(2)}) collective-permute-start(f32[192,128]{1,0:T(8,128)S(1)} %get-tuple-element.92), channel_id=1, source_target_pairs={{0,3},{1,2},{2,1},{3,0},{4,7},{5,6},{6,5},{7,4},{8,11},{9,10},{10,... | collective-permute-start | bytes 294920 | tf_op jit(solution)/shard_map/ppermute | solution.py:126
  59.8 4.8 %collective-permute-done.25.refs_4_ = f32[192,128]{1,0:T(8,128)S(1)} collective-permute-done((f32[192,128]{1,0:T(8,128)S(1)}, f32[192,128]{1,0:T(8,128)S(1)}, u32[]{:S(2)}, u32[]{:S(2)}) %collective-permute-start.25) | collective-permute-done | bytes 98336 | tf_op jit(solution)/shard_map/ppermute | solution.py:126
  64.8 0.7 collective-permute-start.22
  65.5 1.2 collective-permute-start.20
  66.7 1.8 %collective-permute-start.18 = (f32[256,128]{1,0:T(8,128)S(1)}, f32[256,128]{1,0:T(8,128)S(1)}, u32[]{:S(2)}, u32[]{:S(2)}) collective-permute-start(f32[256,128]{1,0:T(8,128)S(1)} %add.30), channel_id=1, source_target_pairs={{0,24},{4,28},{8,16},{12,20},{16,8},{20,12},{24,0},{28,4},{1,25},{... | collective-permute-start | bytes 393224 | tf_op jit(solution)/shard_map/ppermute | solution.py:126
  68.5 5.0 %shard_map.129 = (f32[256,256]{1,0:T(8,128)S(1)}, f32[1,128]{1,0:T(1,128)S(1)}) custom-call(f32[8,256]{1,0:T(8,128)S(1)} %copy-done.2, f32[128,256]{1,0:T(8,128)S(1)} %add.34.refs_0_, f32[128,256]{1,0:T(8,128)S(1)} %collective-permute-done.28.refs_1_), custom_call_target="tpu_custom_call" | custom-call | flops 6000000000 | bytes 532992 | tf_op jit(solution)/shard_map/pallas_call | solution.py:109
  73.5 4.2 %shard_map.130.refs_8_ = f32[256,256]{1,0:T(8,128)S(1)} custom-call(f32[256,256]{1,0:T(8,128)S(1)} %get-tuple-element.96.half_ref), custom_call_target="tpu_custom_call" | custom-call | flops 6000000000 | bytes 524288 | tf_op jit(solution)/shard_map/pallas_call | solution.py:109
  77.8 1.2 shard_map.131
  78.9 0.7 collective-permute-start.33
  79.6 1.2 collective-permute-start.35
  80.8 1.7 %collective-permute-start.37 = (bf16[512,128]{1,0:T(8,128)(2,1)S(1)}, bf16[512,128]{1,0:T(8,128)(2,1)S(1)}, u32[]{:S(2)}, u32[]{:S(2)}) collective-permute-start(bf16[512,128]{1,0:T(8,128)(2,1)S(1)} %get-tuple-element.102.refs_0_), channel_id=1, source_target_pairs={{0,24},{4,28},{8,16},{12,20},{16,8},{20,12},{24,0},{28,4},{1,25},{... | collective-permute-start | bytes 393224 | tf_op jit(solution)/shard_map/ppermute | solution.py:126
  82.5 2.9 %collective-permute-done.33.refs_2_ = bf16[512,128]{1,0:T(8,128)(2,1)S(1)} collective-permute-done((bf16[512,128]{1,0:T(8,128)(2,1)S(1)}, bf16[512,128]{1,0:T(8,128)(2,1)S(1)}, u32[]{:S(2)}, u32[]{:S(2)}) %collective-permute-start.33) | collective-permute-done | bytes 131104 | tf_op jit(solution)/shard_map/ppermute | solution.py:126
  85.4 0.8 collective-permute-done.35.refs_4_
  86.2 1.8 %collective-permute-done.37.refs_6_ = bf16[512,128]{1,0:T(8,128)(2,1)S(1)} collective-permute-done((bf16[512,128]{1,0:T(8,128)(2,1)S(1)}, bf16[512,128]{1,0:T(8,128)(2,1)S(1)}, u32[]{:S(2)}, u32[]{:S(2)}) %collective-permute-start.37) | collective-permute-done | bytes 131104 | tf_op jit(solution)/shard_map/ppermute | solution.py:126
  88.0 1.3 collective-permute-done.38.refs_7_
  89.7 1.9 %collective-permute-start.40 = (bf16[256,128]{1,0:T(8,128)(2,1)S(1)}, bf16[256,128]{1,0:T(8,128)(2,1)S(1)}, u32[]{:S(2)}, u32[]{:S(2)}) collective-permute-start(bf16[256,128]{1,0:T(8,128)(2,1)S(1)} %get-tuple-element.105), channel_id=1, source_target_pairs={{0,2},{1,3},{2,0},{3,1},{4,6},{5,7},{6,4},{7,5},{8,10},{9,11},{10,... | collective-permute-start | bytes 196616 | tf_op jit(solution)/shard_map/ppermute | solution.py:126
  91.6 2.5 %collective-permute-start.41 = (bf16[256,128]{1,0:T(8,128)(2,1)S(1)}, bf16[256,128]{1,0:T(8,128)(2,1)S(1)}, u32[]{:S(2)}, u32[]{:S(2)}) collective-permute-start(bf16[256,128]{1,0:T(8,128)(2,1)S(1)} %get-tuple-element.106), channel_id=1, source_target_pairs={{0,3},{1,2},{2,1},{3,0},{4,7},{5,6},{6,5},{7,4},{8,11},{9,10},{10,... | collective-permute-start | bytes 196616 | tf_op jit(solution)/shard_map/ppermute | solution.py:126
  94.0 1.4 shard_map.136
  95.5 2.7 %collective-permute-done.40.refs_2_ = bf16[256,128]{1,0:T(8,128)(2,1)S(1)} collective-permute-done((bf16[256,128]{1,0:T(8,128)(2,1)S(1)}, bf16[256,128]{1,0:T(8,128)(2,1)S(1)}, u32[]{:S(2)}, u32[]{:S(2)}) %collective-permute-start.40) | collective-permute-done | bytes 65568 | tf_op jit(solution)/shard_map/ppermute | solution.py:126
  98.3 1.5 %shard_map.134 = (f32[256,128]{1,0:T(8,128)S(1)}, f32[256,128]{1,0:T(8,128)S(1)}, f32[256,128]{1,0:T(8,128)S(1)}, f32[256,128]{1,0:T(8,128)S(1)}) custom-call(bf16[1,8,512,512]{3,2,1,0:T(8,128)(2,1)S(1)} %copy-done, f32[8,256]{1,0:T(8,128)S(1)} %copy-done.2, bf16[256,128]{1,0:T(8,128)(2,1)S(1)} %get-tuple-element.103.refs_0_, ...), custom_call_target="tpu_custom_call" | custom-call | flops 1073741824 | bytes 4988928 | tf_op jit(solution)/shard_map/pallas_call | solution.py:109
  99.8 1.3 collective-permute-start.42
  101.1 1.7 %collective-permute-start.43 = (f32[256,128]{1,0:T(8,128)S(1)}, f32[256,128]{1,0:T(8,128)S(1)}, u32[]{:S(2)}, u32[]{:S(2)}) collective-permute-start(f32[256,128]{1,0:T(8,128)S(1)} %get-tuple-element.109), channel_id=1, source_target_pairs={{0,2},{1,3},{2,0},{3,1},{4,6},{5,7},{6,4},{7,5},{8,10},{9,11},{10,... | collective-permute-start | bytes 393224 | tf_op jit(solution)/shard_map/ppermute | solution.py:126
  102.9 1.4 collective-permute-start.44
  104.6 1.6 %collective-permute-done.42.refs_1_ = f32[256,128]{1,0:T(8,128)S(1)} collective-permute-done((f32[256,128]{1,0:T(8,128)S(1)}, f32[256,128]{1,0:T(8,128)S(1)}, u32[]{:S(2)}, u32[]{:S(2)}) %collective-permute-start.42) | collective-permute-done | bytes 131104 | tf_op jit(solution)/shard_map/ppermute | solution.py:126
  106.2 9.6 %collective-permute-done.43.refs_2_ = f32[256,128]{1,0:T(8,128)S(1)} collective-permute-done((f32[256,128]{1,0:T(8,128)S(1)}, f32[256,128]{1,0:T(8,128)S(1)}, u32[]{:S(2)}, u32[]{:S(2)}) %collective-permute-start.43) | collective-permute-done | bytes 131104 | tf_op jit(solution)/shard_map/ppermute | solution.py:126
  116.8 3.2 %collective-permute-done.53 = f32[128,256]{1,0:T(8,128)S(1)} collective-permute-done((f32[128,256]{1,0:T(8,128)S(1)}, f32[128,256]{1,0:T(8,128)S(1)}, u32[]{:S(2)}, u32[]{:S(2)}) %collective-permute-start.53) | collective-permute-done | bytes 131104 | tf_op jit(solution)/shard_map/ppermute | solution.py:126
  120.8 1.8 %collective-permute-start.51 = (f32[256,128]{1,0:T(8,128)S(1)}, f32[256,128]{1,0:T(8,128)S(1)}, u32[]{:S(2)}, u32[]{:S(2)}) collective-permute-start(f32[256,128]{1,0:T(8,128)S(1)} %add.37), channel_id=1, source_target_pairs={{0,8},{4,12},{8,0},{12,4},{16,24},{20,28},{24,16},{28,20},{1,9},{5... | collective-permute-start | bytes 393224 | tf_op jit(solution)/shard_map/ppermute | solution.py:126
  122.6 1.5 %collective-permute-start.49 = (f32[256,128]{1,0:T(8,128)S(1)}, f32[256,128]{1,0:T(8,128)S(1)}, u32[]{:S(2)}, u32[]{:S(2)}) collective-permute-start(f32[256,128]{1,0:T(8,128)S(1)} %add.36), channel_id=1, source_target_pairs={{0,16},{4,20},{8,24},{12,28},{16,0},{20,4},{24,8},{28,12},{1,17},{... | collective-permute-start | bytes 393224 | tf_op jit(solution)/shard_map/ppermute | solution.py:126
  124.5 5.0 %shard_map.137 = (f32[256,256]{1,0:T(8,128)S(1)}, f32[1,128]{1,0:T(1,128)S(1)}) custom-call(f32[8,256]{1,0:T(8,128)S(1)} %copy-done.2, f32[128,256]{1,0:T(8,128)S(1)} %add.39.refs_0_, f32[128,256]{1,0:T(8,128)S(1)} %collective-permute-done.54.refs_1_), custom_call_target="tpu_custom_call" | custom-call | flops 6000000000 | bytes 532992 | tf_op jit(solution)/shard_map/pallas_call | solution.py:109
  129.5 4.2 %shard_map.138.refs_8_ = f32[256,256]{1,0:T(8,128)S(1)} custom-call(f32[256,256]{1,0:T(8,128)S(1)} %get-tuple-element.122.half_ref), custom_call_target="tpu_custom_call" | custom-call | flops 6000000000 | bytes 524288 | tf_op jit(solution)/shard_map/pallas_call | solution.py:109
  133.7 2.0 %collective-permute-start.30 = (f32[64,128]{1,0:T(8,128)S(1)}, f32[64,128]{1,0:T(8,128)S(1)}, u32[]{:S(2)}, u32[]{:S(2)}) collective-permute-start(f32[64,128]{1,0:T(8,128)S(1)} %get-tuple-element.99), channel_id=1, source_target_pairs={{0,2},{1,3},{2,0},{3,1},{4,6},{5,7},{6,4},{7,5},{8,10},{9,11},{10,... | collective-permute-start | bytes 98312 | tf_op jit(solution)/shard_map/ppermute | solution.py:126
  135.8 2.1 %collective-permute-start.31 = (f32[64,128]{1,0:T(8,128)S(1)}, f32[64,128]{1,0:T(8,128)S(1)}, u32[]{:S(2)}, u32[]{:S(2)}) collective-permute-start(f32[64,128]{1,0:T(8,128)S(1)} %get-tuple-element.100), channel_id=1, source_target_pairs={{0,3},{1,2},{2,1},{3,0},{4,7},{5,6},{6,5},{7,4},{8,11},{9,10},{10,... | collective-permute-start | bytes 98312 | tf_op jit(solution)/shard_map/ppermute | solution.py:126
  137.8 1.2 shard_map.139
  139.1 2.3 %collective-permute-start.56 = (f32[64,128]{1,0:T(8,128)S(1)}, f32[64,128]{1,0:T(8,128)S(1)}, u32[]{:S(2)}, u32[]{:S(2)}) collective-permute-start(f32[64,128]{1,0:T(8,128)S(1)} %get-tuple-element.125), channel_id=1, source_target_pairs={{0,2},{1,3},{2,0},{3,1},{4,6},{5,7},{6,4},{7,5},{8,10},{9,11},{10,... | collective-permute-start | bytes 98312 | tf_op jit(solution)/shard_map/ppermute | solution.py:126
  141.4 2.1 %collective-permute-start.57 = (f32[64,128]{1,0:T(8,128)S(1)}, f32[64,128]{1,0:T(8,128)S(1)}, u32[]{:S(2)}, u32[]{:S(2)}) collective-permute-start(f32[64,128]{1,0:T(8,128)S(1)} %get-tuple-element.126), channel_id=1, source_target_pairs={{0,3},{1,2},{2,1},{3,0},{4,7},{5,6},{6,5},{7,4},{8,11},{9,10},{10,... | collective-permute-start | bytes 98312 | tf_op jit(solution)/shard_map/ppermute | solution.py:126
  143.5 0.7 shard_map.132
  144.2 2.9 %collective-permute-done.57.refs_3_ = f32[64,128]{1,0:T(8,128)S(1)} collective-permute-done((f32[64,128]{1,0:T(8,128)S(1)}, f32[64,128]{1,0:T(8,128)S(1)}, u32[]{:S(2)}, u32[]{:S(2)}) %collective-permute-start.57) | collective-permute-done | bytes 32800 | tf_op jit(solution)/shard_map/ppermute | solution.py:126
  147.1 0.7 shard_map.140
  (103 shorter events, 7.0 us)
Async XLA Ops:
  0.6 0.9 copy-start.1
  1.6 5.7 %collective-permute-start = (f32[64,128]{1,0:T(8,128)S(1)}, f32[64,128]{1,0:T(8,128)S(1)}, u32[]{:S(2)}, u32[]{:S(2)}) collective-permute-start(f32[64,128]{1,0:T(8,128)S(1)} %get-tuple-element.68), channel_id=1, source_target_pairs={{0,1},{1,0},{2,3},{3,2},{4,5},{5,4},{6,7},{7,6},{8,9},{9,8},{10,11... | collective-permute-start | bytes 98312 | tf_op jit(solution)/shard_map/ppermute | solution.py:126
  4.7 5.4 %collective-permute-start.1 = (f32[64,128]{1,0:T(8,128)S(1)}, f32[64,128]{1,0:T(8,128)S(1)}, u32[]{:S(2)}, u32[]{:S(2)}) collective-permute-start(f32[64,128]{1,0:T(8,128)S(1)} %get-tuple-element.69), channel_id=1, source_target_pairs={{0,2},{1,3},{2,0},{3,1},{4,6},{5,7},{6,4},{7,5},{8,10},{9,11},{10,... | collective-permute-start | bytes 98312 | tf_op jit(solution)/shard_map/ppermute | solution.py:126
  7.3 5.7 %collective-permute-start.2 = (f32[64,128]{1,0:T(8,128)S(1)}, f32[64,128]{1,0:T(8,128)S(1)}, u32[]{:S(2)}, u32[]{:S(2)}) collective-permute-start(f32[64,128]{1,0:T(8,128)S(1)} %get-tuple-element.70), channel_id=1, source_target_pairs={{0,3},{1,2},{2,1},{3,0},{4,7},{5,6},{6,5},{7,4},{8,11},{9,10},{10,... | collective-permute-start | bytes 98312 | tf_op jit(solution)/shard_map/ppermute | solution.py:126
  13.0 6.2 %collective-permute-start.4 = (bf16[512,128]{1,0:T(8,128)(2,1)S(1)}, bf16[512,128]{1,0:T(8,128)(2,1)S(1)}, u32[]{:S(2)}, u32[]{:S(2)}) collective-permute-start(bf16[512,128]{1,0:T(8,128)(2,1)S(1)} %get-tuple-element.71.refs_0_), channel_id=1, source_target_pairs={{0,8},{4,12},{8,0},{12,4},{16,24},{20,28},{24,16},{28,20},{1,9},{5... | collective-permute-start | bytes 393224 | tf_op jit(solution)/shard_map/ppermute | solution.py:126
  14.6 5.8 %collective-permute-start.6 = (bf16[512,128]{1,0:T(8,128)(2,1)S(1)}, bf16[512,128]{1,0:T(8,128)(2,1)S(1)}, u32[]{:S(2)}, u32[]{:S(2)}) collective-permute-start(bf16[512,128]{1,0:T(8,128)(2,1)S(1)} %get-tuple-element.71.refs_0_), channel_id=1, source_target_pairs={{0,16},{4,20},{8,24},{12,28},{16,0},{20,4},{24,8},{28,12},{1,17},{... | collective-permute-start | bytes 393224 | tf_op jit(solution)/shard_map/ppermute | solution.py:126
  16.1 5.9 %collective-permute-start.8 = (bf16[512,128]{1,0:T(8,128)(2,1)S(1)}, bf16[512,128]{1,0:T(8,128)(2,1)S(1)}, u32[]{:S(2)}, u32[]{:S(2)}) collective-permute-start(bf16[512,128]{1,0:T(8,128)(2,1)S(1)} %get-tuple-element.71.refs_0_), channel_id=1, source_target_pairs={{0,24},{4,28},{8,16},{12,20},{16,8},{20,12},{24,0},{28,4},{1,25},{... | collective-permute-start | bytes 393224 | tf_op jit(solution)/shard_map/ppermute | solution.py:126
  19.1 2.8 %collective-permute-start.3 = (bf16[512,128]{1,0:T(8,128)(2,1)S(1)}, bf16[512,128]{1,0:T(8,128)(2,1)S(1)}, u32[]{:S(2)}, u32[]{:S(2)}) collective-permute-start(bf16[512,128]{1,0:T(8,128)(2,1)S(1)} %get-tuple-element.71.refs_0_), channel_id=1, source_target_pairs={{0,4},{4,0},{8,12},{12,8},{16,20},{20,16},{24,28},{28,24},{1,5},{5... | collective-permute-start | bytes 393224 | tf_op jit(solution)/shard_map/ppermute | solution.py:126
  19.2 2.7 %collective-permute-start.5 = (bf16[512,128]{1,0:T(8,128)(2,1)S(1)}, bf16[512,128]{1,0:T(8,128)(2,1)S(1)}, u32[]{:S(2)}, u32[]{:S(2)}) collective-permute-start(bf16[512,128]{1,0:T(8,128)(2,1)S(1)} %collective-permute-done.4.refs_2_), channel_id=1, source_target_pairs={{0,4},{4,0},{8,12},{12,8},{16,20},{20,16},{24,28},{28,24},{1,5},{5... | collective-permute-start | bytes 393224 | tf_op jit(solution)/shard_map/ppermute | solution.py:126
  20.3 1.7 %collective-permute-start.7 = (bf16[512,128]{1,0:T(8,128)(2,1)S(1)}, bf16[512,128]{1,0:T(8,128)(2,1)S(1)}, u32[]{:S(2)}, u32[]{:S(2)}) collective-permute-start(bf16[512,128]{1,0:T(8,128)(2,1)S(1)} %collective-permute-done.6.refs_4_), channel_id=1, source_target_pairs={{0,4},{4,0},{8,12},{12,8},{16,20},{20,16},{24,28},{28,24},{1,5},{5... | collective-permute-start | bytes 393224 | tf_op jit(solution)/shard_map/ppermute | solution.py:126
  22.0 1.3 collective-permute-start.9
  23.6 8.8 %copy-start = (bf16[1,8,512,512]{3,2,1,0:T(8,128)(2,1)S(1)}, bf16[1,8,512,512]{3,2,1,0:T(8,128)(2,1)}, u32[]{:S(2)}) copy-start(bf16[1,8,512,512]{3,2,1,0:T(8,128)(2,1)} %activity_ref.3) | copy-start | bytes 12582916
  23.6 8.8 %copy-start.2 = (f32[8,256]{1,0:T(8,128)S(1)}, f32[8,256]{1,0:T(8,128)}, u32[]{:S(2)}) copy-start(f32[8,256]{1,0:T(8,128)} %time_ref.7) | copy-start | bytes 24580
  23.6 5.7 %collective-permute-start.10 = (bf16[256,128]{1,0:T(8,128)(2,1)S(1)}, bf16[256,128]{1,0:T(8,128)(2,1)S(1)}, u32[]{:S(2)}, u32[]{:S(2)}) collective-permute-start(bf16[256,128]{1,0:T(8,128)(2,1)S(1)} %get-tuple-element.73), channel_id=1, source_target_pairs={{0,1},{1,0},{2,3},{3,2},{4,5},{5,4},{6,7},{7,6},{8,9},{9,8},{10,11... | collective-permute-start | bytes 196616 | tf_op jit(solution)/shard_map/ppermute | solution.py:126
  23.7 8.5 %collective-permute-start.11 = (bf16[256,128]{1,0:T(8,128)(2,1)S(1)}, bf16[256,128]{1,0:T(8,128)(2,1)S(1)}, u32[]{:S(2)}, u32[]{:S(2)}) collective-permute-start(bf16[256,128]{1,0:T(8,128)(2,1)S(1)} %get-tuple-element.74), channel_id=1, source_target_pairs={{0,2},{1,3},{2,0},{3,1},{4,6},{5,7},{6,4},{7,5},{8,10},{9,11},{10,... | collective-permute-start | bytes 196616 | tf_op jit(solution)/shard_map/ppermute | solution.py:126
  24.6 14.1 %copy-start.6 = (f32[512,64]{0,1:T(8,128)S(1)}, f32[512,64]{0,1:T(8,128)}, u32[]{:S(2)}) copy-start(f32[512,64]{0,1:T(8,128)} %param.17) | copy-start | bytes 393220
  24.6 14.1 %copy-start.7 = (f32[512,64]{0,1:T(8,128)S(1)}, f32[512,64]{0,1:T(8,128)}, u32[]{:S(2)}) copy-start(f32[512,64]{0,1:T(8,128)} %param.16) | copy-start | bytes 393220
  24.6 14.1 %copy-start.8 = (f32[512,64]{0,1:T(8,128)S(1)}, f32[512,64]{0,1:T(8,128)}, u32[]{:S(2)}) copy-start(f32[512,64]{0,1:T(8,128)} %param.13) | copy-start | bytes 393220
  24.6 7.8 %collective-permute-start.12 = (bf16[256,128]{1,0:T(8,128)(2,1)S(1)}, bf16[256,128]{1,0:T(8,128)(2,1)S(1)}, u32[]{:S(2)}, u32[]{:S(2)}) collective-permute-start(bf16[256,128]{1,0:T(8,128)(2,1)S(1)} %get-tuple-element.75), channel_id=1, source_target_pairs={{0,3},{1,2},{2,1},{3,0},{4,7},{5,6},{6,5},{7,4},{8,11},{9,10},{10,... | collective-permute-start | bytes 196616 | tf_op jit(solution)/shard_map/ppermute | solution.py:126
  29.2 9.1 %collective-permute-start.26 = (f32[128,256]{1,0:T(8,128)S(1)}, f32[128,256]{1,0:T(8,128)S(1)}, u32[]{:S(2)}, u32[]{:S(2)}) collective-permute-start(f32[128,256]{1,0:T(8,128)S(1)} %shard_map.128), channel_id=1, source_target_pairs={{0,1},{1,0},{2,3},{3,2},{4,5},{5,4},{6,7},{7,6},{8,9},{9,8},{10,11... | collective-permute-start | bytes 393224 | tf_op jit(solution)/shard_map/ppermute | solution.py:126
  33.9 7.9 %collective-permute-start.13 = (f32[256,128]{1,0:T(8,128)S(1)}, f32[256,128]{1,0:T(8,128)S(1)}, u32[]{:S(2)}, u32[]{:S(2)}) collective-permute-start(f32[256,128]{1,0:T(8,128)S(1)} %get-tuple-element.77), channel_id=1, source_target_pairs={{0,1},{1,0},{2,3},{3,2},{4,5},{5,4},{6,7},{7,6},{8,9},{9,8},{10,11... | collective-permute-start | bytes 393224 | tf_op jit(solution)/shard_map/ppermute | solution.py:126
  35.2 16.5 %collective-permute-start.14 = (f32[256,128]{1,0:T(8,128)S(1)}, f32[256,128]{1,0:T(8,128)S(1)}, u32[]{:S(2)}, u32[]{:S(2)}) collective-permute-start(f32[256,128]{1,0:T(8,128)S(1)} %get-tuple-element.78), channel_id=1, source_target_pairs={{0,2},{1,3},{2,0},{3,1},{4,6},{5,7},{6,4},{7,5},{8,10},{9,11},{10,... | collective-permute-start | bytes 393224 | tf_op jit(solution)/shard_map/ppermute | solution.py:126
  37.0 14.6 %collective-permute-start.15 = (f32[256,128]{1,0:T(8,128)S(1)}, f32[256,128]{1,0:T(8,128)S(1)}, u32[]{:S(2)}, u32[]{:S(2)}) collective-permute-start(f32[256,128]{1,0:T(8,128)S(1)} %get-tuple-element.79), channel_id=1, source_target_pairs={{0,3},{1,2},{2,1},{3,0},{4,7},{5,6},{6,5},{7,4},{8,11},{9,10},{10,... | collective-permute-start | bytes 393224 | tf_op jit(solution)/shard_map/ppermute | solution.py:126
  38.4 18.8 %collective-permute-start.27 = (f32[128,256]{1,0:T(8,128)S(1)}, f32[128,256]{1,0:T(8,128)S(1)}, u32[]{:S(2)}, u32[]{:S(2)}) collective-permute-start(f32[128,256]{1,0:T(8,128)S(1)} %add.33), channel_id=1, source_target_pairs={{0,2},{1,3},{2,0},{3,1},{4,6},{5,7},{6,4},{7,5},{8,10},{9,11},{10,... | collective-permute-start | bytes 393224 | tf_op jit(solution)/shard_map/ppermute | solution.py:126
  38.9 18.3 %collective-permute-start.23 = (f32[192,128]{1,0:T(8,128)S(1)}, f32[192,128]{1,0:T(8,128)S(1)}, u32[]{:S(2)}, u32[]{:S(2)}) collective-permute-start(f32[192,128]{1,0:T(8,128)S(1)} %get-tuple-element.90), channel_id=1, source_target_pairs={{0,1},{1,0},{2,3},{3,2},{4,5},{5,4},{6,7},{7,6},{8,9},{9,8},{10,11... | collective-permute-start | bytes 294920 | tf_op jit(solution)/shard_map/ppermute | solution.py:126
  41.8 16.4 %collective-permute-start.24 = (f32[192,128]{1,0:T(8,128)S(1)}, f32[192,128]{1,0:T(8,128)S(1)}, u32[]{:S(2)}, u32[]{:S(2)}) collective-permute-start(f32[192,128]{1,0:T(8,128)S(1)} %get-tuple-element.91), channel_id=1, source_target_pairs={{0,2},{1,3},{2,0},{3,1},{4,6},{5,7},{6,4},{7,5},{8,10},{9,11},{10,... | collective-permute-start | bytes 294920 | tf_op jit(solution)/shard_map/ppermute | solution.py:126
  52.0 12.7 %collective-permute-start.21 = (f32[256,128]{1,0:T(8,128)S(1)}, f32[256,128]{1,0:T(8,128)S(1)}, u32[]{:S(2)}, u32[]{:S(2)}) collective-permute-start(f32[256,128]{1,0:T(8,128)S(1)} %get-tuple-element.87), channel_id=1, source_target_pairs={{0,4},{4,0},{8,12},{12,8},{16,20},{20,16},{24,28},{28,24},{1,5},{5... | collective-permute-start | bytes 393224 | tf_op jit(solution)/shard_map/ppermute | solution.py:126
  52.1 13.3 %collective-permute-start.19 = (f32[256,128]{1,0:T(8,128)S(1)}, f32[256,128]{1,0:T(8,128)S(1)}, u32[]{:S(2)}, u32[]{:S(2)}) collective-permute-start(f32[256,128]{1,0:T(8,128)S(1)} %get-tuple-element.85), channel_id=1, source_target_pairs={{0,4},{4,0},{8,12},{12,8},{16,20},{20,16},{24,28},{28,24},{1,5},{5... | collective-permute-start | bytes 393224 | tf_op jit(solution)/shard_map/ppermute | solution.py:126
  57.2 9.5 %collective-permute-start.17 = (f32[256,128]{1,0:T(8,128)S(1)}, f32[256,128]{1,0:T(8,128)S(1)}, u32[]{:S(2)}, u32[]{:S(2)}) collective-permute-start(f32[256,128]{1,0:T(8,128)S(1)} %get-tuple-element.83), channel_id=1, source_target_pairs={{0,4},{4,0},{8,12},{12,8},{16,20},{20,16},{24,28},{28,24},{1,5},{5... | collective-permute-start | bytes 393224 | tf_op jit(solution)/shard_map/ppermute | solution.py:126
  57.2 11.3 %collective-permute-start.28 = (f32[128,256]{1,0:T(8,128)S(1)}, f32[128,256]{1,0:T(8,128)S(1)}, u32[]{:S(2)}, u32[]{:S(2)}) collective-permute-start(f32[128,256]{1,0:T(8,128)S(1)} %add.34.refs_0_), channel_id=1, source_target_pairs={{0,4},{4,0},{8,12},{12,8},{16,20},{20,16},{24,28},{28,24},{1,5},{5... | collective-permute-start | bytes 393224 | tf_op jit(solution)/shard_map/ppermute | solution.py:126
  58.2 6.4 %collective-permute-start.25 = (f32[192,128]{1,0:T(8,128)S(1)}, f32[192,128]{1,0:T(8,128)S(1)}, u32[]{:S(2)}, u32[]{:S(2)}) collective-permute-start(f32[192,128]{1,0:T(8,128)S(1)} %get-tuple-element.92), channel_id=1, source_target_pairs={{0,3},{1,2},{2,1},{3,0},{4,7},{5,6},{6,5},{7,4},{8,11},{9,10},{10,... | collective-permute-start | bytes 294920 | tf_op jit(solution)/shard_map/ppermute | solution.py:126
  64.7 13.0 %collective-permute-start.16 = (f32[256,128]{1,0:T(8,128)S(1)}, f32[256,128]{1,0:T(8,128)S(1)}, u32[]{:S(2)}, u32[]{:S(2)}) collective-permute-start(f32[256,128]{1,0:T(8,128)S(1)} %get-tuple-element.81), channel_id=1, source_target_pairs={{0,4},{4,0},{8,12},{12,8},{16,20},{20,16},{24,28},{28,24},{1,5},{5... | collective-permute-start | bytes 393224 | tf_op jit(solution)/shard_map/ppermute | solution.py:126
  64.8 12.9 %collective-permute-start.22 = (f32[256,128]{1,0:T(8,128)S(1)}, f32[256,128]{1,0:T(8,128)S(1)}, u32[]{:S(2)}, u32[]{:S(2)}) collective-permute-start(f32[256,128]{1,0:T(8,128)S(1)} %add.32), channel_id=1, source_target_pairs={{0,8},{4,12},{8,0},{12,4},{16,24},{20,28},{24,16},{28,20},{1,9},{5... | collective-permute-start | bytes 393224 | tf_op jit(solution)/shard_map/ppermute | solution.py:126
  65.5 12.3 %collective-permute-start.20 = (f32[256,128]{1,0:T(8,128)S(1)}, f32[256,128]{1,0:T(8,128)S(1)}, u32[]{:S(2)}, u32[]{:S(2)}) collective-permute-start(f32[256,128]{1,0:T(8,128)S(1)} %add.31), channel_id=1, source_target_pairs={{0,16},{4,20},{8,24},{12,28},{16,0},{20,4},{24,8},{28,12},{1,17},{... | collective-permute-start | bytes 393224 | tf_op jit(solution)/shard_map/ppermute | solution.py:126
  66.7 11.1 %collective-permute-start.18 = (f32[256,128]{1,0:T(8,128)S(1)}, f32[256,128]{1,0:T(8,128)S(1)}, u32[]{:S(2)}, u32[]{:S(2)}) collective-permute-start(f32[256,128]{1,0:T(8,128)S(1)} %add.30), channel_id=1, source_target_pairs={{0,24},{4,28},{8,16},{12,20},{16,8},{20,12},{24,0},{28,4},{1,25},{... | collective-permute-start | bytes 393224 | tf_op jit(solution)/shard_map/ppermute | solution.py:126
  78.9 6.4 %collective-permute-start.33 = (bf16[512,128]{1,0:T(8,128)(2,1)S(1)}, bf16[512,128]{1,0:T(8,128)(2,1)S(1)}, u32[]{:S(2)}, u32[]{:S(2)}) collective-permute-start(bf16[512,128]{1,0:T(8,128)(2,1)S(1)} %get-tuple-element.102.refs_0_), channel_id=1, source_target_pairs={{0,8},{4,12},{8,0},{12,4},{16,24},{20,28},{24,16},{28,20},{1,9},{5... | collective-permute-start | bytes 393224 | tf_op jit(solution)/shard_map/ppermute | solution.py:126
  79.6 6.6 %collective-permute-start.35 = (bf16[512,128]{1,0:T(8,128)(2,1)S(1)}, bf16[512,128]{1,0:T(8,128)(2,1)S(1)}, u32[]{:S(2)}, u32[]{:S(2)}) collective-permute-start(bf16[512,128]{1,0:T(8,128)(2,1)S(1)} %get-tuple-element.102.refs_0_), channel_id=1, source_target_pairs={{0,16},{4,20},{8,24},{12,28},{16,0},{20,4},{24,8},{28,12},{1,17},{... | collective-permute-start | bytes 393224 | tf_op jit(solution)/shard_map/ppermute | solution.py:126
  80.8 7.2 %collective-permute-start.37 = (bf16[512,128]{1,0:T(8,128)(2,1)S(1)}, bf16[512,128]{1,0:T(8,128)(2,1)S(1)}, u32[]{:S(2)}, u32[]{:S(2)}) collective-permute-start(bf16[512,128]{1,0:T(8,128)(2,1)S(1)} %get-tuple-element.102.refs_0_), channel_id=1, source_target_pairs={{0,24},{4,28},{8,16},{12,20},{16,8},{20,12},{24,0},{28,4},{1,25},{... | collective-permute-start | bytes 393224 | tf_op jit(solution)/shard_map/ppermute | solution.py:126
  82.5 5.5 %collective-permute-start.32 = (bf16[512,128]{1,0:T(8,128)(2,1)S(1)}, bf16[512,128]{1,0:T(8,128)(2,1)S(1)}, u32[]{:S(2)}, u32[]{:S(2)}) collective-permute-start(bf16[512,128]{1,0:T(8,128)(2,1)S(1)} %get-tuple-element.102.refs_0_), channel_id=1, source_target_pairs={{0,4},{4,0},{8,12},{12,8},{16,20},{20,16},{24,28},{28,24},{1,5},{5... | collective-permute-start | bytes 393224 | tf_op jit(solution)/shard_map/ppermute | solution.py:126
  85.4 2.6 %collective-permute-start.34 = (bf16[512,128]{1,0:T(8,128)(2,1)S(1)}, bf16[512,128]{1,0:T(8,128)(2,1)S(1)}, u32[]{:S(2)}, u32[]{:S(2)}) collective-permute-start(bf16[512,128]{1,0:T(8,128)(2,1)S(1)} %collective-permute-done.33.refs_2_), channel_id=1, source_target_pairs={{0,4},{4,0},{8,12},{12,8},{16,20},{20,16},{24,28},{28,24},{1,5},{5... | collective-permute-start | bytes 393224 | tf_op jit(solution)/shard_map/ppermute | solution.py:126
  86.2 1.8 %collective-permute-start.36 = (bf16[512,128]{1,0:T(8,128)(2,1)S(1)}, bf16[512,128]{1,0:T(8,128)(2,1)S(1)}, u32[]{:S(2)}, u32[]{:S(2)}) collective-permute-start(bf16[512,128]{1,0:T(8,128)(2,1)S(1)} %collective-permute-done.35.refs_4_), channel_id=1, source_target_pairs={{0,4},{4,0},{8,12},{12,8},{16,20},{20,16},{24,28},{28,24},{1,5},{5... | collective-permute-start | bytes 393224 | tf_op jit(solution)/shard_map/ppermute | solution.py:126
  88.0 1.3 collective-permute-start.38
  89.6 5.9 %collective-permute-start.39 = (bf16[256,128]{1,0:T(8,128)(2,1)S(1)}, bf16[256,128]{1,0:T(8,128)(2,1)S(1)}, u32[]{:S(2)}, u32[]{:S(2)}) collective-permute-start(bf16[256,128]{1,0:T(8,128)(2,1)S(1)} %get-tuple-element.104), channel_id=1, source_target_pairs={{0,1},{1,0},{2,3},{3,2},{4,5},{5,4},{6,7},{7,6},{8,9},{9,8},{10,11... | collective-permute-start | bytes 196616 | tf_op jit(solution)/shard_map/ppermute | solution.py:126
  89.7 8.6 %collective-permute-start.40 = (bf16[256,128]{1,0:T(8,128)(2,1)S(1)}, bf16[256,128]{1,0:T(8,128)(2,1)S(1)}, u32[]{:S(2)}, u32[]{:S(2)}) collective-permute-start(bf16[256,128]{1,0:T(8,128)(2,1)S(1)} %get-tuple-element.105), channel_id=1, source_target_pairs={{0,2},{1,3},{2,0},{3,1},{4,6},{5,7},{6,4},{7,5},{8,10},{9,11},{10,... | collective-permute-start | bytes 196616 | tf_op jit(solution)/shard_map/ppermute | solution.py:126
  91.6 6.7 %collective-permute-start.41 = (bf16[256,128]{1,0:T(8,128)(2,1)S(1)}, bf16[256,128]{1,0:T(8,128)(2,1)S(1)}, u32[]{:S(2)}, u32[]{:S(2)}) collective-permute-start(bf16[256,128]{1,0:T(8,128)(2,1)S(1)} %get-tuple-element.106), channel_id=1, source_target_pairs={{0,3},{1,2},{2,1},{3,0},{4,7},{5,6},{6,5},{7,4},{8,11},{9,10},{10,... | collective-permute-start | bytes 196616 | tf_op jit(solution)/shard_map/ppermute | solution.py:126
  95.4 8.8 %collective-permute-start.52 = (f32[128,256]{1,0:T(8,128)S(1)}, f32[128,256]{1,0:T(8,128)S(1)}, u32[]{:S(2)}, u32[]{:S(2)}) collective-permute-start(f32[128,256]{1,0:T(8,128)S(1)} %shard_map.136), channel_id=1, source_target_pairs={{0,1},{1,0},{2,3},{3,2},{4,5},{5,4},{6,7},{7,6},{8,9},{9,8},{10,11... | collective-permute-start | bytes 393224 | tf_op jit(solution)/shard_map/ppermute | solution.py:126
  99.8 6.4 %collective-permute-start.42 = (f32[256,128]{1,0:T(8,128)S(1)}, f32[256,128]{1,0:T(8,128)S(1)}, u32[]{:S(2)}, u32[]{:S(2)}) collective-permute-start(f32[256,128]{1,0:T(8,128)S(1)} %get-tuple-element.108), channel_id=1, source_target_pairs={{0,1},{1,0},{2,3},{3,2},{4,5},{5,4},{6,7},{7,6},{8,9},{9,8},{10,11... | collective-permute-start | bytes 393224 | tf_op jit(solution)/shard_map/ppermute | solution.py:126
  101.1 14.6 %collective-permute-start.43 = (f32[256,128]{1,0:T(8,128)S(1)}, f32[256,128]{1,0:T(8,128)S(1)}, u32[]{:S(2)}, u32[]{:S(2)}) collective-permute-start(f32[256,128]{1,0:T(8,128)S(1)} %get-tuple-element.109), channel_id=1, source_target_pairs={{0,2},{1,3},{2,0},{3,1},{4,6},{5,7},{6,4},{7,5},{8,10},{9,11},{10,... | collective-permute-start | bytes 393224 | tf_op jit(solution)/shard_map/ppermute | solution.py:126
  102.9 12.9 %collective-permute-start.44 = (f32[256,128]{1,0:T(8,128)S(1)}, f32[256,128]{1,0:T(8,128)S(1)}, u32[]{:S(2)}, u32[]{:S(2)}) collective-permute-start(f32[256,128]{1,0:T(8,128)S(1)} %get-tuple-element.110), channel_id=1, source_target_pairs={{0,3},{1,2},{2,1},{3,0},{4,7},{5,6},{6,5},{7,4},{8,11},{9,10},{10,... | collective-permute-start | bytes 393224 | tf_op jit(solution)/shard_map/ppermute | solution.py:126
  104.3 15.8 %collective-permute-start.53 = (f32[128,256]{1,0:T(8,128)S(1)}, f32[128,256]{1,0:T(8,128)S(1)}, u32[]{:S(2)}, u32[]{:S(2)}) collective-permute-start(f32[128,256]{1,0:T(8,128)S(1)} %add.38), channel_id=1, source_target_pairs={{0,2},{1,3},{2,0},{3,1},{4,6},{5,7},{6,4},{7,5},{8,10},{9,11},{10,... | collective-permute-start | bytes 393224 | tf_op jit(solution)/shard_map/ppermute | solution.py:126
  116.2 4.5 %collective-permute-start.50 = (f32[256,128]{1,0:T(8,128)S(1)}, f32[256,128]{1,0:T(8,128)S(1)}, u32[]{:S(2)}, u32[]{:S(2)}) collective-permute-start(f32[256,128]{1,0:T(8,128)S(1)} %get-tuple-element.118), channel_id=1, source_target_pairs={{0,4},{4,0},{8,12},{12,8},{16,20},{20,16},{24,28},{28,24},{1,5},{5... | collective-permute-start | bytes 393224 | tf_op jit(solution)/shard_map/ppermute | solution.py:126
  116.3 4.5 %collective-permute-start.48 = (f32[256,128]{1,0:T(8,128)S(1)}, f32[256,128]{1,0:T(8,128)S(1)}, u32[]{:S(2)}, u32[]{:S(2)}) collective-permute-start(f32[256,128]{1,0:T(8,128)S(1)} %get-tuple-element.116), channel_id=1, source_target_pairs={{0,4},{4,0},{8,12},{12,8},{16,20},{20,16},{24,28},{28,24},{1,5},{5... | collective-permute-start | bytes 393224 | tf_op jit(solution)/shard_map/ppermute | solution.py:126
  116.8 5.8 %collective-permute-start.46 = (f32[256,128]{1,0:T(8,128)S(1)}, f32[256,128]{1,0:T(8,128)S(1)}, u32[]{:S(2)}, u32[]{:S(2)}) collective-permute-start(f32[256,128]{1,0:T(8,128)S(1)} %get-tuple-element.114), channel_id=1, source_target_pairs={{0,4},{4,0},{8,12},{12,8},{16,20},{20,16},{24,28},{28,24},{1,5},{5... | collective-permute-start | bytes 393224 | tf_op jit(solution)/shard_map/ppermute | solution.py:126
  120.1 4.1 %collective-permute-start.54 = (f32[128,256]{1,0:T(8,128)S(1)}, f32[128,256]{1,0:T(8,128)S(1)}, u32[]{:S(2)}, u32[]{:S(2)}) collective-permute-start(f32[128,256]{1,0:T(8,128)S(1)} %add.39.refs_0_), channel_id=1, source_target_pairs={{0,4},{4,0},{8,12},{12,8},{16,20},{20,16},{24,28},{28,24},{1,5},{5... | collective-permute-start | bytes 393224 | tf_op jit(solution)/shard_map/ppermute | solution.py:126
  120.2 21.2 %collective-permute-start.29 = (f32[64,128]{1,0:T(8,128)S(1)}, f32[64,128]{1,0:T(8,128)S(1)}, u32[]{:S(2)}, u32[]{:S(2)}) collective-permute-start(f32[64,128]{1,0:T(8,128)S(1)} %get-tuple-element.98), channel_id=1, source_target_pairs={{0,1},{1,0},{2,3},{3,2},{4,5},{5,4},{6,7},{7,6},{8,9},{9,8},{10,11... | collective-permute-start | bytes 98312 | tf_op jit(solution)/shard_map/ppermute | solution.py:126
  120.7 13.0 %collective-permute-start.45 = (f32[256,128]{1,0:T(8,128)S(1)}, f32[256,128]{1,0:T(8,128)S(1)}, u32[]{:S(2)}, u32[]{:S(2)}) collective-permute-start(f32[256,128]{1,0:T(8,128)S(1)} %get-tuple-element.112), channel_id=1, source_target_pairs={{0,4},{4,0},{8,12},{12,8},{16,20},{20,16},{24,28},{28,24},{1,5},{5... | collective-permute-start | bytes 393224 | tf_op jit(solution)/shard_map/ppermute | solution.py:126
  120.8 15.0 %collective-permute-start.51 = (f32[256,128]{1,0:T(8,128)S(1)}, f32[256,128]{1,0:T(8,128)S(1)}, u32[]{:S(2)}, u32[]{:S(2)}) collective-permute-start(f32[256,128]{1,0:T(8,128)S(1)} %add.37), channel_id=1, source_target_pairs={{0,8},{4,12},{8,0},{12,4},{16,24},{20,28},{24,16},{28,20},{1,9},{5... | collective-permute-start | bytes 393224 | tf_op jit(solution)/shard_map/ppermute | solution.py:126
  122.6 15.2 %collective-permute-start.49 = (f32[256,128]{1,0:T(8,128)S(1)}, f32[256,128]{1,0:T(8,128)S(1)}, u32[]{:S(2)}, u32[]{:S(2)}) collective-permute-start(f32[256,128]{1,0:T(8,128)S(1)} %add.36), channel_id=1, source_target_pairs={{0,16},{4,20},{8,24},{12,28},{16,0},{20,4},{24,8},{28,12},{1,17},{... | collective-permute-start | bytes 393224 | tf_op jit(solution)/shard_map/ppermute | solution.py:126
  124.2 13.6 %collective-permute-start.47 = (f32[256,128]{1,0:T(8,128)S(1)}, f32[256,128]{1,0:T(8,128)S(1)}, u32[]{:S(2)}, u32[]{:S(2)}) collective-permute-start(f32[256,128]{1,0:T(8,128)S(1)} %add.35), channel_id=1, source_target_pairs={{0,24},{4,28},{8,16},{12,20},{16,8},{20,12},{24,0},{28,4},{1,25},{... | collective-permute-start | bytes 393224 | tf_op jit(solution)/shard_map/ppermute | solution.py:126
  133.7 9.7 %collective-permute-start.30 = (f32[64,128]{1,0:T(8,128)S(1)}, f32[64,128]{1,0:T(8,128)S(1)}, u32[]{:S(2)}, u32[]{:S(2)}) collective-permute-start(f32[64,128]{1,0:T(8,128)S(1)} %get-tuple-element.99), channel_id=1, source_target_pairs={{0,2},{1,3},{2,0},{3,1},{4,6},{5,7},{6,4},{7,5},{8,10},{9,11},{10,... | collective-permute-start | bytes 98312 | tf_op jit(solution)/shard_map/ppermute | solution.py:126
  135.8 7.7 %collective-permute-start.31 = (f32[64,128]{1,0:T(8,128)S(1)}, f32[64,128]{1,0:T(8,128)S(1)}, u32[]{:S(2)}, u32[]{:S(2)}) collective-permute-start(f32[64,128]{1,0:T(8,128)S(1)} %get-tuple-element.100), channel_id=1, source_target_pairs={{0,3},{1,2},{2,1},{3,0},{4,7},{5,6},{6,5},{7,4},{8,11},{9,10},{10,... | collective-permute-start | bytes 98312 | tf_op jit(solution)/shard_map/ppermute | solution.py:126
  139.0 5.2 %collective-permute-start.55 = (f32[64,128]{1,0:T(8,128)S(1)}, f32[64,128]{1,0:T(8,128)S(1)}, u32[]{:S(2)}, u32[]{:S(2)}) collective-permute-start(f32[64,128]{1,0:T(8,128)S(1)} %get-tuple-element.124), channel_id=1, source_target_pairs={{0,1},{1,0},{2,3},{3,2},{4,5},{5,4},{6,7},{7,6},{8,9},{9,8},{10,11... | collective-permute-start | bytes 98312 | tf_op jit(solution)/shard_map/ppermute | solution.py:126
  139.1 5.1 %collective-permute-start.56 = (f32[64,128]{1,0:T(8,128)S(1)}, f32[64,128]{1,0:T(8,128)S(1)}, u32[]{:S(2)}, u32[]{:S(2)}) collective-permute-start(f32[64,128]{1,0:T(8,128)S(1)} %get-tuple-element.125), channel_id=1, source_target_pairs={{0,2},{1,3},{2,0},{3,1},{4,6},{5,7},{6,4},{7,5},{8,10},{9,11},{10,... | collective-permute-start | bytes 98312 | tf_op jit(solution)/shard_map/ppermute | solution.py:126
  141.4 5.7 %collective-permute-start.57 = (f32[64,128]{1,0:T(8,128)S(1)}, f32[64,128]{1,0:T(8,128)S(1)}, u32[]{:S(2)}, u32[]{:S(2)}) collective-permute-start(f32[64,128]{1,0:T(8,128)S(1)} %get-tuple-element.126), channel_id=1, source_target_pairs={{0,3},{1,2},{2,1},{3,0},{4,7},{5,6},{6,5},{7,4},{8,11},{9,10},{10,... | collective-permute-start | bytes 98312 | tf_op jit(solution)/shard_map/ppermute | solution.py:126
  (3 other events, 2.0 us)

commit v2 on v1

--- a/solution.py
+++ b/solution.py
@@ -67,10 +67,12 @@
 def first_half_kernel(panel, time_ref, *refs):
     pieces, (work_ref, penalty_ref) = refs[:-2], refs[-2:]
     rank = work_ref.shape[0]
-    half = rank // 2
+    part = rank // 4
     for r, piece in enumerate(pieces):
-        start = (lax.axis_index("wide") % 2 ^ r) * half
-        work_ref[pl.ds(pl.multiple_of(start, half), half), :] = piece[...]
+        core = lax.axis_index("wide") % 2 ^ r % 2
+        side = lax.axis_index("narrow") % 2 ^ r // 2
+        start = pl.multiple_of((core * 2 + side) * part, part)
+        work_ref[pl.ds(start, part), :] = piece[...]
     time = time_ref[...]
     times = lax.dot_general(
         time, time, (((0,), (0,)), ((), ())), precision=HIGHEST, preferred_element_type=jnp.float32
@@ -206,33 +208,41 @@
 
 
 def gram_kernel(*refs):
-    pairs, (half_ref, rows_ref) = refs[:-2], refs[-2:]
+    pairs, (far_ref, near_ref, rows_ref, half_ref) = refs[:-4], refs[-4:]
     rank = rows_ref.shape[0]
     width = pairs[0].shape[1]
     for k, pair in enumerate(pairs):
         rows_ref[:, k * width : (k + 1) * width] = pair[:rank].astype(jnp.float32) + pair[
             rank:
         ].astype(jnp.float32)
-    half = half_ref.shape[0]
+    half, part = half_ref.shape[0], near_ref.shape[0]
     start = pl.multiple_of(lax.axis_index("wide") % 2 * half, half)
     half_ref[...] = lax.dot_general(
         rows_ref[pl.ds(start, half), :], rows_ref[...], (((1,), (1,)), ((), ())),
         precision=HIGHEST, preferred_element_type=jnp.float32,
     )
+    side = lax.axis_index("narrow") % 2
+    near_ref[...] = half_ref[pl.ds(pl.multiple_of(side * part, part), part), :]
+    far_ref[...] = half_ref[pl.ds(pl.multiple_of((1 - side) * part, part), part), :]
 
 
 def joint_gram(pairs):
     rank, width = pairs[0].shape[0] // 2, pairs[0].shape[1]
-    (total,) = kernel_call(
-        gram_kernel, [shape((rank // 2, rank))], *pairs,
-        scratch=[pltpu.VMEM((rank, len(pairs) * width), jnp.float32)],
+    far, near = kernel_call(
+        gram_kernel, [shape((rank // 4, rank))] * 2, *pairs,
+        scratch=[
+            pltpu.VMEM((rank, len(pairs) * width), jnp.float32),
+            pltpu.VMEM((rank // 2, rank), jnp.float32),
+        ],
         flops=1_500_000_000,
     )
-    mask = 1
+    total = near + swap(far, "narrow", 1)
+    mask = 2
     while mask < lax.axis_size("narrow"):
         total = total + swap(total, "narrow", mask)
         mask *= 2
-    return total, swap(total, "wide", 1)
+    parts = [total, swap(total, "narrow", 1)]
+    return [x for part in parts for x in (part, swap(part, "wide", 1))]
 
 
 def pick_kernel(count, table_ref, *refs):

time: 148 us -> 141 us (0.953)
  waiting for transfers between devices: 58.7 us -> 42.3 us
  starting transfers between devices: 54.9 us -> 64.2 us
    ppermute x58 -> x62, waiting for transfers between devices: 58.7 us -> 42.3 us  [swap(): return lax.ppermute(x, axis, [(i, i ^ mask) for i in range(size)])]
    ppermute x58 -> x62, starting transfers between devices: 54.9 us -> 64.2 us  [swap(): return lax.ppermute(x, axis, [(i, i ^ mask) for i in range(size)])]
  transfers between devices with their start and end apart: 58 -> 62, of which waited for: 20 -> 18; matrix products, arithmetic and copies ran while one was open for 0% -> 0% of each run, Pallas kernels for 19% -> 18%
where the time goes in v2:
time: 141 us
  starting transfers between devices  64.2 us (46%)
  waiting for transfers between devices  42.3 us (30%)
  Pallas kernels  30.3 us (21%)
  local copies, waits for them, and re-layouts  2.92 us (2%)
    ppermute x62, starting transfers between devices, swap(): return lax.ppermute(x, axis, [(i, i ^ mask) for i in range(size)])  64.2 us
    ppermute x62, waiting for transfers between devices, swap(): return lax.ppermute(x, axis, [(i, i ^ mask) for i in range(size)])  42.3 us
    pallas_call x21, Pallas kernels, kernel_call(): pl.pallas_call(kernel, out_shape=tuple(out_shape), in_specs=[spec] * len(...  30.3 us
    unnamed x18, local copies, waits for them, and re-layouts  2.92 us
  transfers between devices with their start and end apart: 62, of which 18 were waited for; matrix products, arithmetic and copies ran while one was open for 0% of the time, Pallas kernels for 18%

profile of v2, /device:TPU:0, one launch (start us, length us, event | category | flops | bytes accessed | tf_op | source)
XLA Modules:
  0.0 140.9 jit_solution(1898865295059210044)
XLA Ops:
  0.6 0.9 copy-done.1
  1.6 3.1 %collective-permute-start = (f32[64,128]{1,0:T(8,128)S(1)}, f32[64,128]{1,0:T(8,128)S(1)}, u32[]{:S(2)}, u32[]{:S(2)}) collective-permute-start(f32[64,128]{1,0:T(8,128)S(1)} %get-tuple-element.72), channel_id=1, source_target_pairs={{0,1},{1,0},{2,3},{3,2},{4,5},{5,4},{6,7},{7,6},{8,9},{9,8},{10,11... | collective-permute-start | bytes 98312 | tf_op jit(solution)/shard_map/ppermute | solution.py:128
  4.7 2.6 %collective-permute-start.1 = (f32[64,128]{1,0:T(8,128)S(1)}, f32[64,128]{1,0:T(8,128)S(1)}, u32[]{:S(2)}, u32[]{:S(2)}) collective-permute-start(f32[64,128]{1,0:T(8,128)S(1)} %get-tuple-element.73), channel_id=1, source_target_pairs={{0,2},{1,3},{2,0},{3,1},{4,6},{5,7},{6,4},{7,5},{8,10},{9,11},{10,... | collective-permute-start | bytes 98312 | tf_op jit(solution)/shard_map/ppermute | solution.py:128
  7.3 2.8 %collective-permute-done.1.refs_2_ = f32[64,128]{1,0:T(8,128)S(1)} collective-permute-done((f32[64,128]{1,0:T(8,128)S(1)}, f32[64,128]{1,0:T(8,128)S(1)}, u32[]{:S(2)}, u32[]{:S(2)}) %collective-permute-start.1) | collective-permute-done | bytes 32800 | tf_op jit(solution)/shard_map/ppermute | solution.py:128
  10.1 2.9 %collective-permute-done.2.refs_3_ = f32[64,128]{1,0:T(8,128)S(1)} collective-permute-done((f32[64,128]{1,0:T(8,128)S(1)}, f32[64,128]{1,0:T(8,128)S(1)}, u32[]{:S(2)}, u32[]{:S(2)}) %collective-permute-start.2) | collective-permute-done | bytes 32800 | tf_op jit(solution)/shard_map/ppermute | solution.py:128
  13.0 1.6 %collective-permute-start.4 = (bf16[512,128]{1,0:T(8,128)(2,1)S(1)}, bf16[512,128]{1,0:T(8,128)(2,1)S(1)}, u32[]{:S(2)}, u32[]{:S(2)}) collective-permute-start(bf16[512,128]{1,0:T(8,128)(2,1)S(1)} %get-tuple-element.75.refs_0_), channel_id=1, source_target_pairs={{0,8},{4,12},{8,0},{12,4},{16,24},{20,28},{24,16},{28,20},{1,9},{5... | collective-permute-start | bytes 393224 | tf_op jit(solution)/shard_map/ppermute | solution.py:128
  14.6 1.5 %collective-permute-start.6 = (bf16[512,128]{1,0:T(8,128)(2,1)S(1)}, bf16[512,128]{1,0:T(8,128)(2,1)S(1)}, u32[]{:S(2)}, u32[]{:S(2)}) collective-permute-start(bf16[512,128]{1,0:T(8,128)(2,1)S(1)} %get-tuple-element.75.refs_0_), channel_id=1, source_target_pairs={{0,16},{4,20},{8,24},{12,28},{16,0},{20,4},{24,8},{28,12},{1,17},{... | collective-permute-start | bytes 393224 | tf_op jit(solution)/shard_map/ppermute | solution.py:128
  16.6 0.7 copy-done.3
  17.2 0.7 copy-done.4
  17.9 0.7 copy-done.5
  18.6 0.6 shard_map.120
  19.7 0.6 collective-permute-done.6.refs_4_
  20.3 1.6 %collective-permute-done.8.refs_6_ = bf16[512,128]{1,0:T(8,128)(2,1)S(1)} collective-permute-done((bf16[512,128]{1,0:T(8,128)(2,1)S(1)}, bf16[512,128]{1,0:T(8,128)(2,1)S(1)}, u32[]{:S(2)}, u32[]{:S(2)}) %collective-permute-start.8) | collective-permute-done | bytes 131104 | tf_op jit(solution)/shard_map/ppermute | solution.py:128
  22.0 1.3 collective-permute-done.9.refs_7_
  23.3 1.2 shard_map.128
  24.9 2.0 %collective-permute-start.10 = (bf16[256,128]{1,0:T(8,128)(2,1)S(1)}, bf16[256,128]{1,0:T(8,128)(2,1)S(1)}, u32[]{:S(2)}, u32[]{:S(2)}) collective-permute-start(bf16[256,128]{1,0:T(8,128)(2,1)S(1)} %get-tuple-element.77), channel_id=1, source_target_pairs={{0,1},{1,0},{2,3},{3,2},{4,5},{5,4},{6,7},{7,6},{8,9},{9,8},{10,11... | collective-permute-start | bytes 196616 | tf_op jit(solution)/shard_map/ppermute | solution.py:128
  27.0 2.4 %collective-permute-start.12 = (bf16[256,128]{1,0:T(8,128)(2,1)S(1)}, bf16[256,128]{1,0:T(8,128)(2,1)S(1)}, u32[]{:S(2)}, u32[]{:S(2)}) collective-permute-start(bf16[256,128]{1,0:T(8,128)(2,1)S(1)} %get-tuple-element.79), channel_id=1, source_target_pairs={{0,3},{1,2},{2,1},{3,0},{4,7},{5,6},{6,5},{7,4},{8,11},{9,10},{10,... | collective-permute-start | bytes 196616 | tf_op jit(solution)/shard_map/ppermute | solution.py:128
  29.7 1.1 collective-permute-start.23
  30.8 0.9 collective-permute-start.24
  31.7 2.5 %collective-permute-start.25 = (f32[192,128]{1,0:T(8,128)S(1)}, f32[192,128]{1,0:T(8,128)S(1)}, u32[]{:S(2)}, u32[]{:S(2)}) collective-permute-start(f32[192,128]{1,0:T(8,128)S(1)} %get-tuple-element.96), channel_id=1, source_target_pairs={{0,3},{1,2},{2,1},{3,0},{4,7},{5,6},{6,5},{7,4},{8,11},{9,10},{10,... | collective-permute-start | bytes 294920 | tf_op jit(solution)/shard_map/ppermute | solution.py:128
  34.5 1.5 %shard_map.124 = (f32[256,128]{1,0:T(8,128)S(1)}, f32[256,128]{1,0:T(8,128)S(1)}, f32[256,128]{1,0:T(8,128)S(1)}, f32[256,128]{1,0:T(8,128)S(1)}) custom-call(bf16[1,8,512,512]{3,2,1,0:T(8,128)(2,1)S(1)} %copy-done, f32[8,256]{1,0:T(8,128)S(1)} %copy-done.2, bf16[256,128]{1,0:T(8,128)(2,1)S(1)} %get-tuple-element.76.refs_0_, ...), custom_call_target="tpu_custom_call" | custom-call | flops 1073741824 | bytes 4988928 | tf_op jit(solution)/shard_map/pallas_call | solution.py:111
  36.1 7.6 %collective-permute-start.13 = (f32[256,128]{1,0:T(8,128)S(1)}, f32[256,128]{1,0:T(8,128)S(1)}, u32[]{:S(2)}, u32[]{:S(2)}) collective-permute-start(f32[256,128]{1,0:T(8,128)S(1)} %get-tuple-element.81), channel_id=1, source_target_pairs={{0,1},{1,0},{2,3},{3,2},{4,5},{5,4},{6,7},{7,6},{8,9},{9,8},{10,11... | collective-permute-start | bytes 393224 | tf_op jit(solution)/shard_map/ppermute | solution.py:128
  43.7 6.3 %collective-permute-done.27 = f32[64,256]{1,0:T(8,128)S(1)} collective-permute-done((f32[64,256]{1,0:T(8,128)S(1)}, f32[64,256]{1,0:T(8,128)S(1)}, u32[]{:S(2)}, u32[]{:S(2)}) %collective-permute-start.27) | collective-permute-done | bytes 65568 | tf_op jit(solution)/shard_map/ppermute | solution.py:128
  50.1 5.0 %collective-permute-done.29.refs_2_ = f32[64,256]{1,0:T(8,128)S(1)} collective-permute-done((f32[64,256]{1,0:T(8,128)S(1)}, f32[64,256]{1,0:T(8,128)S(1)}, u32[]{:S(2)}, u32[]{:S(2)}) %collective-permute-start.29) | collective-permute-done | bytes 65568 | tf_op jit(solution)/shard_map/ppermute | solution.py:128
  55.2 1.6 %collective-permute-done.15.refs_3_ = f32[256,128]{1,0:T(8,128)S(1)} collective-permute-done((f32[256,128]{1,0:T(8,128)S(1)}, f32[256,128]{1,0:T(8,128)S(1)}, u32[]{:S(2)}, u32[]{:S(2)}) %collective-permute-start.15) | collective-permute-done | bytes 131104 | tf_op jit(solution)/shard_map/ppermute | solution.py:128
  58.3 4.9 %shard_map.129 = (f32[256,256]{1,0:T(8,128)S(1)}, f32[1,128]{1,0:T(1,128)S(1)}) custom-call(f32[8,256]{1,0:T(8,128)S(1)} %copy-done.2, f32[64,256]{1,0:T(8,128)S(1)} %add.34.refs_0_, f32[64,256]{1,0:T(8,128)S(1)} %collective-permute-done.28.refs_1_, f32[64,256]{1,0:T(8,128)S(1)} %collective-permute-done.29.refs_2_, f32[64,256]{1,0:T(8,128)S(1)} %collective-permute-done.30.refs_3_), custom_call_target="tpu_custom_call" | custom-call | flops 6000000000 | bytes 532992 | tf_op jit(solution)/shard_map/pallas_call | solution.py:111
  63.3 0.6 collective-permute-start.22
  63.9 0.6 collective-permute-start.20
  64.5 2.5 %collective-permute-start.18 = (f32[256,128]{1,0:T(8,128)S(1)}, f32[256,128]{1,0:T(8,128)S(1)}, u32[]{:S(2)}, u32[]{:S(2)}) collective-permute-start(f32[256,128]{1,0:T(8,128)S(1)} %add.30), channel_id=1, source_target_pairs={{0,24},{4,28},{8,16},{12,20},{16,8},{20,12},{24,0},{28,4},{1,25},{... | collective-permute-start | bytes 393224 | tf_op jit(solution)/shard_map/ppermute | solution.py:128
  67.0 4.2 %shard_map.130.refs_8_ = f32[256,256]{1,0:T(8,128)S(1)} custom-call(f32[256,256]{1,0:T(8,128)S(1)} %get-tuple-element.102.half_ref), custom_call_target="tpu_custom_call" | custom-call | flops 6000000000 | bytes 524288 | tf_op jit(solution)/shard_map/pallas_call | solution.py:111
  71.3 0.8 collective-permute-done.18.refs_2_
  72.0 1.4 shard_map.131
  73.4 1.5 %collective-permute-start.35 = (bf16[512,128]{1,0:T(8,128)(2,1)S(1)}, bf16[512,128]{1,0:T(8,128)(2,1)S(1)}, u32[]{:S(2)}, u32[]{:S(2)}) collective-permute-start(bf16[512,128]{1,0:T(8,128)(2,1)S(1)} %get-tuple-element.108.refs_0_), channel_id=1, source_target_pairs={{0,8},{4,12},{8,0},{12,4},{16,24},{20,28},{24,16},{28,20},{1,9},{5... | collective-permute-start | bytes 393224 | tf_op jit(solution)/shard_map/ppermute | solution.py:128
  74.9 1.0 collective-permute-start.37
  75.9 1.1 collective-permute-start.39
  77.0 2.5 %collective-permute-done.35.refs_2_ = bf16[512,128]{1,0:T(8,128)(2,1)S(1)} collective-permute-done((bf16[512,128]{1,0:T(8,128)(2,1)S(1)}, bf16[512,128]{1,0:T(8,128)(2,1)S(1)}, u32[]{:S(2)}, u32[]{:S(2)}) %collective-permute-start.35) | collective-permute-done | bytes 131104 | tf_op jit(solution)/shard_map/ppermute | solution.py:128
  79.5 2.4 %collective-permute-done.37.refs_4_ = bf16[512,128]{1,0:T(8,128)(2,1)S(1)} collective-permute-done((bf16[512,128]{1,0:T(8,128)(2,1)S(1)}, bf16[512,128]{1,0:T(8,128)(2,1)S(1)}, u32[]{:S(2)}, u32[]{:S(2)}) %collective-permute-start.37) | collective-permute-done | bytes 131104 | tf_op jit(solution)/shard_map/ppermute | solution.py:128
  82.4 0.8 collective-permute-done.38.refs_5_
  83.4 1.2 shard_map.136
  84.6 1.7 %collective-permute-start.54 = (f32[64,256]{1,0:T(8,128)S(1)}, f32[64,256]{1,0:T(8,128)S(1)}, u32[]{:S(2)}, u32[]{:S(2)}) collective-permute-start(f32[64,256]{1,0:T(8,128)S(1)} %get-tuple-element.128), channel_id=1, source_target_pairs={{0,1},{1,0},{2,3},{3,2},{4,5},{5,4},{6,7},{7,6},{8,9},{9,8},{10,11... | collective-permute-start | bytes 196616 | tf_op jit(solution)/shard_map/ppermute | solution.py:128
  87.0 2.0 %collective-permute-start.42 = (bf16[256,128]{1,0:T(8,128)(2,1)S(1)}, bf16[256,128]{1,0:T(8,128)(2,1)S(1)}, u32[]{:S(2)}, u32[]{:S(2)}) collective-permute-start(bf16[256,128]{1,0:T(8,128)(2,1)S(1)} %get-tuple-element.111), channel_id=1, source_target_pairs={{0,2},{1,3},{2,0},{3,1},{4,6},{5,7},{6,4},{7,5},{8,10},{9,11},{10,... | collective-permute-start | bytes 196616 | tf_op jit(solution)/shard_map/ppermute | solution.py:128
  89.0 2.0 %collective-permute-start.43 = (bf16[256,128]{1,0:T(8,128)(2,1)S(1)}, bf16[256,128]{1,0:T(8,128)(2,1)S(1)}, u32[]{:S(2)}, u32[]{:S(2)}) collective-permute-start(bf16[256,128]{1,0:T(8,128)(2,1)S(1)} %get-tuple-element.112), channel_id=1, source_target_pairs={{0,3},{1,2},{2,1},{3,0},{4,7},{5,6},{6,5},{7,4},{8,11},{9,10},{10,... | collective-permute-start | bytes 196616 | tf_op jit(solution)/shard_map/ppermute | solution.py:128
  91.0 0.7 collective-permute-start.55
  91.7 5.3 %collective-permute-done.42.refs_2_ = bf16[256,128]{1,0:T(8,128)(2,1)S(1)} collective-permute-done((bf16[256,128]{1,0:T(8,128)(2,1)S(1)}, bf16[256,128]{1,0:T(8,128)(2,1)S(1)}, u32[]{:S(2)}, u32[]{:S(2)}) %collective-permute-start.42) | collective-permute-done | bytes 65568 | tf_op jit(solution)/shard_map/ppermute | solution.py:128
  97.0 1.5 %shard_map.134 = (f32[256,128]{1,0:T(8,128)S(1)}, f32[256,128]{1,0:T(8,128)S(1)}, f32[256,128]{1,0:T(8,128)S(1)}, f32[256,128]{1,0:T(8,128)S(1)}) custom-call(bf16[1,8,512,512]{3,2,1,0:T(8,128)(2,1)S(1)} %copy-done, f32[8,256]{1,0:T(8,128)S(1)} %copy-done.2, bf16[256,128]{1,0:T(8,128)(2,1)S(1)} %get-tuple-element.109.refs_0_, ...), custom_call_target="tpu_custom_call" | custom-call | flops 1073741824 | bytes 4988928 | tf_op jit(solution)/shard_map/pallas_call | solution.py:111
  98.5 2.0 %collective-permute-start.44 = (f32[256,128]{1,0:T(8,128)S(1)}, f32[256,128]{1,0:T(8,128)S(1)}, u32[]{:S(2)}, u32[]{:S(2)}) collective-permute-start(f32[256,128]{1,0:T(8,128)S(1)} %get-tuple-element.114), channel_id=1, source_target_pairs={{0,1},{1,0},{2,3},{3,2},{4,5},{5,4},{6,7},{7,6},{8,9},{9,8},{10,11... | collective-permute-start | bytes 393224 | tf_op jit(solution)/shard_map/ppermute | solution.py:128
  100.5 0.8 collective-permute-start.45
  101.2 1.7 %collective-permute-start.46 = (f32[256,128]{1,0:T(8,128)S(1)}, f32[256,128]{1,0:T(8,128)S(1)}, u32[]{:S(2)}, u32[]{:S(2)}) collective-permute-start(f32[256,128]{1,0:T(8,128)S(1)} %get-tuple-element.116), channel_id=1, source_target_pairs={{0,3},{1,2},{2,1},{3,0},{4,7},{5,6},{6,5},{7,4},{8,11},{9,10},{10,... | collective-permute-start | bytes 393224 | tf_op jit(solution)/shard_map/ppermute | solution.py:128
  103.0 1.1 collective-permute-start.57
  104.0 4.7 %collective-permute-done.57.refs_2_ = f32[64,256]{1,0:T(8,128)S(1)} collective-permute-done((f32[64,256]{1,0:T(8,128)S(1)}, f32[64,256]{1,0:T(8,128)S(1)}, u32[]{:S(2)}, u32[]{:S(2)}) %collective-permute-start.57) | collective-permute-done | bytes 65568 | tf_op jit(solution)/shard_map/ppermute | solution.py:128
  108.8 2.5 %collective-permute-start.31 = (f32[64,128]{1,0:T(8,128)S(1)}, f32[64,128]{1,0:T(8,128)S(1)}, u32[]{:S(2)}, u32[]{:S(2)}) collective-permute-start(f32[64,128]{1,0:T(8,128)S(1)} %get-tuple-element.104), channel_id=1, source_target_pairs={{0,1},{1,0},{2,3},{3,2},{4,5},{5,4},{6,7},{7,6},{8,9},{9,8},{10,11... | collective-permute-start | bytes 98312 | tf_op jit(solution)/shard_map/ppermute | solution.py:128
  113.0 4.9 %shard_map.137 = (f32[256,256]{1,0:T(8,128)S(1)}, f32[1,128]{1,0:T(1,128)S(1)}) custom-call(f32[8,256]{1,0:T(8,128)S(1)} %copy-done.2, f32[64,256]{1,0:T(8,128)S(1)} %add.39.refs_0_, f32[64,256]{1,0:T(8,128)S(1)} %collective-permute-done.56.refs_1_, f32[64,256]{1,0:T(8,128)S(1)} %collective-permute-done.57.refs_2_, f32[64,256]{1,0:T(8,128)S(1)} %collective-permute-done.58.refs_3_), custom_call_target="tpu_custom_call" | custom-call | flops 6000000000 | bytes 532992 | tf_op jit(solution)/shard_map/pallas_call | solution.py:111
  118.0 1.1 collective-permute-start.53
  119.1 1.2 collective-permute-start.51
  120.3 1.4 collective-permute-start.49
  121.7 4.5 %shard_map.138.refs_8_ = f32[256,256]{1,0:T(8,128)S(1)} custom-call(f32[256,256]{1,0:T(8,128)S(1)} %get-tuple-element.130.half_ref), custom_call_target="tpu_custom_call" | custom-call | flops 6000000000 | bytes 524288 | tf_op jit(solution)/shard_map/pallas_call | solution.py:111
  126.2 2.6 %collective-permute-start.32 = (f32[64,128]{1,0:T(8,128)S(1)}, f32[64,128]{1,0:T(8,128)S(1)}, u32[]{:S(2)}, u32[]{:S(2)}) collective-permute-start(f32[64,128]{1,0:T(8,128)S(1)} %get-tuple-element.105), channel_id=1, source_target_pairs={{0,2},{1,3},{2,0},{3,1},{4,6},{5,7},{6,4},{7,5},{8,10},{9,11},{10,... | collective-permute-start | bytes 98312 | tf_op jit(solution)/shard_map/ppermute | solution.py:128
  128.9 2.1 %collective-permute-start.33 = (f32[64,128]{1,0:T(8,128)S(1)}, f32[64,128]{1,0:T(8,128)S(1)}, u32[]{:S(2)}, u32[]{:S(2)}) collective-permute-start(f32[64,128]{1,0:T(8,128)S(1)} %get-tuple-element.106), channel_id=1, source_target_pairs={{0,3},{1,2},{2,1},{3,0},{4,7},{5,6},{6,5},{7,4},{8,11},{9,10},{10,... | collective-permute-start | bytes 98312 | tf_op jit(solution)/shard_map/ppermute | solution.py:128
  131.0 1.2 shard_map.139
  132.2 2.3 %collective-permute-start.60 = (f32[64,128]{1,0:T(8,128)S(1)}, f32[64,128]{1,0:T(8,128)S(1)}, u32[]{:S(2)}, u32[]{:S(2)}) collective-permute-start(f32[64,128]{1,0:T(8,128)S(1)} %get-tuple-element.133), channel_id=1, source_target_pairs={{0,2},{1,3},{2,0},{3,1},{4,6},{5,7},{6,4},{7,5},{8,10},{9,11},{10,... | collective-permute-start | bytes 98312 | tf_op jit(solution)/shard_map/ppermute | solution.py:128
  134.5 2.1 %collective-permute-start.61 = (f32[64,128]{1,0:T(8,128)S(1)}, f32[64,128]{1,0:T(8,128)S(1)}, u32[]{:S(2)}, u32[]{:S(2)}) collective-permute-start(f32[64,128]{1,0:T(8,128)S(1)} %get-tuple-element.134), channel_id=1, source_target_pairs={{0,3},{1,2},{2,1},{3,0},{4,7},{5,6},{6,5},{7,4},{8,11},{9,10},{10,... | collective-permute-start | bytes 98312 | tf_op jit(solution)/shard_map/ppermute | solution.py:128
  136.6 0.7 shard_map.132
  137.3 2.9 %collective-permute-done.61.refs_3_ = f32[64,128]{1,0:T(8,128)S(1)} collective-permute-done((f32[64,128]{1,0:T(8,128)S(1)}, f32[64,128]{1,0:T(8,128)S(1)}, u32[]{:S(2)}, u32[]{:S(2)}) %collective-permute-start.61) | collective-permute-done | bytes 32800 | tf_op jit(solution)/shard_map/ppermute | solution.py:128
  140.2 0.7 shard_map.140
  (111 shorter events, 7.2 us)
Async XLA Ops:
  1.6 5.7 %collective-permute-start = (f32[64,128]{1,0:T(8,128)S(1)}, f32[64,128]{1,0:T(8,128)S(1)}, u32[]{:S(2)}, u32[]{:S(2)}) collective-permute-start(f32[64,128]{1,0:T(8,128)S(1)} %get-tuple-element.72), channel_id=1, source_target_pairs={{0,1},{1,0},{2,3},{3,2},{4,5},{5,4},{6,7},{7,6},{8,9},{9,8},{10,11... | collective-permute-start | bytes 98312 | tf_op jit(solution)/shard_map/ppermute | solution.py:128
  4.7 5.4 %collective-permute-start.1 = (f32[64,128]{1,0:T(8,128)S(1)}, f32[64,128]{1,0:T(8,128)S(1)}, u32[]{:S(2)}, u32[]{:S(2)}) collective-permute-start(f32[64,128]{1,0:T(8,128)S(1)} %get-tuple-element.73), channel_id=1, source_target_pairs={{0,2},{1,3},{2,0},{3,1},{4,6},{5,7},{6,4},{7,5},{8,10},{9,11},{10,... | collective-permute-start | bytes 98312 | tf_op jit(solution)/shard_map/ppermute | solution.py:128
  7.3 5.7 %collective-permute-start.2 = (f32[64,128]{1,0:T(8,128)S(1)}, f32[64,128]{1,0:T(8,128)S(1)}, u32[]{:S(2)}, u32[]{:S(2)}) collective-permute-start(f32[64,128]{1,0:T(8,128)S(1)} %get-tuple-element.74), channel_id=1, source_target_pairs={{0,3},{1,2},{2,1},{3,0},{4,7},{5,6},{6,5},{7,4},{8,11},{9,10},{10,... | collective-permute-start | bytes 98312 | tf_op jit(solution)/shard_map/ppermute | solution.py:128
  13.0 6.2 %collective-permute-start.4 = (bf16[512,128]{1,0:T(8,128)(2,1)S(1)}, bf16[512,128]{1,0:T(8,128)(2,1)S(1)}, u32[]{:S(2)}, u32[]{:S(2)}) collective-permute-start(bf16[512,128]{1,0:T(8,128)(2,1)S(1)} %get-tuple-element.75.refs_0_), channel_id=1, source_target_pairs={{0,8},{4,12},{8,0},{12,4},{16,24},{20,28},{24,16},{28,20},{1,9},{5... | collective-permute-start | bytes 393224 | tf_op jit(solution)/shard_map/ppermute | solution.py:128
  14.6 5.8 %collective-permute-start.6 = (bf16[512,128]{1,0:T(8,128)(2,1)S(1)}, bf16[512,128]{1,0:T(8,128)(2,1)S(1)}, u32[]{:S(2)}, u32[]{:S(2)}) collective-permute-start(bf16[512,128]{1,0:T(8,128)(2,1)S(1)} %get-tuple-element.75.refs_0_), channel_id=1, source_target_pairs={{0,16},{4,20},{8,24},{12,28},{16,0},{20,4},{24,8},{28,12},{1,17},{... | collective-permute-start | bytes 393224 | tf_op jit(solution)/shard_map/ppermute | solution.py:128
  16.1 5.9 %collective-permute-start.8 = (bf16[512,128]{1,0:T(8,128)(2,1)S(1)}, bf16[512,128]{1,0:T(8,128)(2,1)S(1)}, u32[]{:S(2)}, u32[]{:S(2)}) collective-permute-start(bf16[512,128]{1,0:T(8,128)(2,1)S(1)} %get-tuple-element.75.refs_0_), channel_id=1, source_target_pairs={{0,24},{4,28},{8,16},{12,20},{16,8},{20,12},{24,0},{28,4},{1,25},{... | collective-permute-start | bytes 393224 | tf_op jit(solution)/shard_map/ppermute | solution.py:128
  19.1 2.8 %collective-permute-start.3 = (bf16[512,128]{1,0:T(8,128)(2,1)S(1)}, bf16[512,128]{1,0:T(8,128)(2,1)S(1)}, u32[]{:S(2)}, u32[]{:S(2)}) collective-permute-start(bf16[512,128]{1,0:T(8,128)(2,1)S(1)} %get-tuple-element.75.refs_0_), channel_id=1, source_target_pairs={{0,4},{4,0},{8,12},{12,8},{16,20},{20,16},{24,28},{28,24},{1,5},{5... | collective-permute-start | bytes 393224 | tf_op jit(solution)/shard_map/ppermute | solution.py:128
  19.2 2.7 %collective-permute-start.5 = (bf16[512,128]{1,0:T(8,128)(2,1)S(1)}, bf16[512,128]{1,0:T(8,128)(2,1)S(1)}, u32[]{:S(2)}, u32[]{:S(2)}) collective-permute-start(bf16[512,128]{1,0:T(8,128)(2,1)S(1)} %collective-permute-done.4.refs_2_), channel_id=1, source_target_pairs={{0,4},{4,0},{8,12},{12,8},{16,20},{20,16},{24,28},{28,24},{1,5},{5... | collective-permute-start | bytes 393224 | tf_op jit(solution)/shard_map/ppermute | solution.py:128
  20.3 1.7 %collective-permute-start.7 = (bf16[512,128]{1,0:T(8,128)(2,1)S(1)}, bf16[512,128]{1,0:T(8,128)(2,1)S(1)}, u32[]{:S(2)}, u32[]{:S(2)}) collective-permute-start(bf16[512,128]{1,0:T(8,128)(2,1)S(1)} %collective-permute-done.6.refs_4_), channel_id=1, source_target_pairs={{0,4},{4,0},{8,12},{12,8},{16,20},{20,16},{24,28},{28,24},{1,5},{5... | collective-permute-start | bytes 393224 | tf_op jit(solution)/shard_map/ppermute | solution.py:128
  22.0 1.3 collective-permute-start.9
  24.5 6.3 %collective-permute-start.26 = (f32[64,256]{1,0:T(8,128)S(1)}, f32[64,256]{1,0:T(8,128)S(1)}, u32[]{:S(2)}, u32[]{:S(2)}) collective-permute-start(f32[64,256]{1,0:T(8,128)S(1)} %get-tuple-element.100), channel_id=1, source_target_pairs={{0,1},{1,0},{2,3},{3,2},{4,5},{5,4},{6,7},{7,6},{8,9},{9,8},{10,11... | collective-permute-start | bytes 196616 | tf_op jit(solution)/shard_map/ppermute | solution.py:128
  24.6 9.9 %copy-start = (bf16[1,8,512,512]{3,2,1,0:T(8,128)(2,1)S(1)}, bf16[1,8,512,512]{3,2,1,0:T(8,128)(2,1)}, u32[]{:S(2)}) copy-start(bf16[1,8,512,512]{3,2,1,0:T(8,128)(2,1)} %activity_ref.3) | copy-start | bytes 12582916
  24.6 9.9 %copy-start.2 = (f32[8,256]{1,0:T(8,128)S(1)}, f32[8,256]{1,0:T(8,128)}, u32[]{:S(2)}) copy-start(f32[8,256]{1,0:T(8,128)} %time_ref.7) | copy-start | bytes 24580
  24.9 6.8 %collective-permute-start.10 = (bf16[256,128]{1,0:T(8,128)(2,1)S(1)}, bf16[256,128]{1,0:T(8,128)(2,1)S(1)}, u32[]{:S(2)}, u32[]{:S(2)}) collective-permute-start(bf16[256,128]{1,0:T(8,128)(2,1)S(1)} %get-tuple-element.77), channel_id=1, source_target_pairs={{0,1},{1,0},{2,3},{3,2},{4,5},{5,4},{6,7},{7,6},{8,9},{9,8},{10,11... | collective-permute-start | bytes 196616 | tf_op jit(solution)/shard_map/ppermute | solution.py:128
  27.0 7.6 %collective-permute-start.11 = (bf16[256,128]{1,0:T(8,128)(2,1)S(1)}, bf16[256,128]{1,0:T(8,128)(2,1)S(1)}, u32[]{:S(2)}, u32[]{:S(2)}) collective-permute-start(bf16[256,128]{1,0:T(8,128)(2,1)S(1)} %get-tuple-element.78), channel_id=1, source_target_pairs={{0,2},{1,3},{2,0},{3,1},{4,6},{5,7},{6,4},{7,5},{8,10},{9,11},{10,... | collective-permute-start | bytes 196616 | tf_op jit(solution)/shard_map/ppermute | solution.py:128
  27.0 7.6 %collective-permute-start.12 = (bf16[256,128]{1,0:T(8,128)(2,1)S(1)}, bf16[256,128]{1,0:T(8,128)(2,1)S(1)}, u32[]{:S(2)}, u32[]{:S(2)}) collective-permute-start(bf16[256,128]{1,0:T(8,128)(2,1)S(1)} %get-tuple-element.79), channel_id=1, source_target_pairs={{0,3},{1,2},{2,1},{3,0},{4,7},{5,6},{6,5},{7,4},{8,11},{9,10},{10,... | collective-permute-start | bytes 196616 | tf_op jit(solution)/shard_map/ppermute | solution.py:128
  29.7 14.0 %collective-permute-start.23 = (f32[192,128]{1,0:T(8,128)S(1)}, f32[192,128]{1,0:T(8,128)S(1)}, u32[]{:S(2)}, u32[]{:S(2)}) collective-permute-start(f32[192,128]{1,0:T(8,128)S(1)} %get-tuple-element.94), channel_id=1, source_target_pairs={{0,1},{1,0},{2,3},{3,2},{4,5},{5,4},{6,7},{7,6},{8,9},{9,8},{10,11... | collective-permute-start | bytes 294920 | tf_op jit(solution)/shard_map/ppermute | solution.py:128
  30.8 19.2 %collective-permute-start.24 = (f32[192,128]{1,0:T(8,128)S(1)}, f32[192,128]{1,0:T(8,128)S(1)}, u32[]{:S(2)}, u32[]{:S(2)}) collective-permute-start(f32[192,128]{1,0:T(8,128)S(1)} %get-tuple-element.95), channel_id=1, source_target_pairs={{0,2},{1,3},{2,0},{3,1},{4,6},{5,7},{6,4},{7,5},{8,10},{9,11},{10,... | collective-permute-start | bytes 294920 | tf_op jit(solution)/shard_map/ppermute | solution.py:128
  31.7 18.3 %collective-permute-start.25 = (f32[192,128]{1,0:T(8,128)S(1)}, f32[192,128]{1,0:T(8,128)S(1)}, u32[]{:S(2)}, u32[]{:S(2)}) collective-permute-start(f32[192,128]{1,0:T(8,128)S(1)} %get-tuple-element.96), channel_id=1, source_target_pairs={{0,3},{1,2},{2,1},{3,0},{4,7},{5,6},{6,5},{7,4},{8,11},{9,10},{10,... | collective-permute-start | bytes 294920 | tf_op jit(solution)/shard_map/ppermute | solution.py:128
  34.5 15.4 %collective-permute-start.27 = (f32[64,256]{1,0:T(8,128)S(1)}, f32[64,256]{1,0:T(8,128)S(1)}, u32[]{:S(2)}, u32[]{:S(2)}) collective-permute-start(f32[64,256]{1,0:T(8,128)S(1)} %add.33), channel_id=1, source_target_pairs={{0,2},{1,3},{2,0},{3,1},{4,6},{5,7},{6,4},{7,5},{8,10},{9,11},{10,... | collective-permute-start | bytes 196616 | tf_op jit(solution)/shard_map/ppermute | solution.py:128
  36.1 19.1 %collective-permute-start.13 = (f32[256,128]{1,0:T(8,128)S(1)}, f32[256,128]{1,0:T(8,128)S(1)}, u32[]{:S(2)}, u32[]{:S(2)}) collective-permute-start(f32[256,128]{1,0:T(8,128)S(1)} %get-tuple-element.81), channel_id=1, source_target_pairs={{0,1},{1,0},{2,3},{3,2},{4,5},{5,4},{6,7},{7,6},{8,9},{9,8},{10,11... | collective-permute-start | bytes 393224 | tf_op jit(solution)/shard_map/ppermute | solution.py:128
  43.7 11.5 %collective-permute-start.14 = (f32[256,128]{1,0:T(8,128)S(1)}, f32[256,128]{1,0:T(8,128)S(1)}, u32[]{:S(2)}, u32[]{:S(2)}) collective-permute-start(f32[256,128]{1,0:T(8,128)S(1)} %get-tuple-element.82), channel_id=1, source_target_pairs={{0,2},{1,3},{2,0},{3,1},{4,6},{5,7},{6,4},{7,5},{8,10},{9,11},{10,... | collective-permute-start | bytes 393224 | tf_op jit(solution)/shard_map/ppermute | solution.py:128
  49.9 6.9 %collective-permute-start.15 = (f32[256,128]{1,0:T(8,128)S(1)}, f32[256,128]{1,0:T(8,128)S(1)}, u32[]{:S(2)}, u32[]{:S(2)}) collective-permute-start(f32[256,128]{1,0:T(8,128)S(1)} %get-tuple-element.83), channel_id=1, source_target_pairs={{0,3},{1,2},{2,1},{3,0},{4,7},{5,6},{6,5},{7,4},{8,11},{9,10},{10,... | collective-permute-start | bytes 393224 | tf_op jit(solution)/shard_map/ppermute | solution.py:128
  50.0 5.2 %collective-permute-start.29 = (f32[64,256]{1,0:T(8,128)S(1)}, f32[64,256]{1,0:T(8,128)S(1)}, u32[]{:S(2)}, u32[]{:S(2)}) collective-permute-start(f32[64,256]{1,0:T(8,128)S(1)} %add.34.refs_0_), channel_id=1, source_target_pairs={{0,1},{1,0},{2,3},{3,2},{4,5},{5,4},{6,7},{7,6},{8,9},{9,8},{10,11... | collective-permute-start | bytes 196616 | tf_op jit(solution)/shard_map/ppermute | solution.py:128
  50.0 7.8 %collective-permute-start.28 = (f32[64,256]{1,0:T(8,128)S(1)}, f32[64,256]{1,0:T(8,128)S(1)}, u32[]{:S(2)}, u32[]{:S(2)}) collective-permute-start(f32[64,256]{1,0:T(8,128)S(1)} %add.34.refs_0_), channel_id=1, source_target_pairs={{0,4},{4,0},{8,12},{12,8},{16,20},{20,16},{24,28},{28,24},{1,5},{5... | collective-permute-start | bytes 196616 | tf_op jit(solution)/shard_map/ppermute | solution.py:128
  55.2 3.1 %collective-permute-start.30 = (f32[64,256]{1,0:T(8,128)S(1)}, f32[64,256]{1,0:T(8,128)S(1)}, u32[]{:S(2)}, u32[]{:S(2)}) collective-permute-start(f32[64,256]{1,0:T(8,128)S(1)} %collective-permute-done.29.refs_2_), channel_id=1, source_target_pairs={{0,4},{4,0},{8,12},{12,8},{16,20},{20,16},{24,28},{28,24},{1,5},{5... | collective-permute-start | bytes 196616 | tf_op jit(solution)/shard_map/ppermute | solution.py:128
  57.2 6.0 %collective-permute-start.21 = (f32[256,128]{1,0:T(8,128)S(1)}, f32[256,128]{1,0:T(8,128)S(1)}, u32[]{:S(2)}, u32[]{:S(2)}) collective-permute-start(f32[256,128]{1,0:T(8,128)S(1)} %get-tuple-element.91), channel_id=1, source_target_pairs={{0,4},{4,0},{8,12},{12,8},{16,20},{20,16},{24,28},{28,24},{1,5},{5... | collective-permute-start | bytes 393224 | tf_op jit(solution)/shard_map/ppermute | solution.py:128
  57.3 6.6 %collective-permute-start.19 = (f32[256,128]{1,0:T(8,128)S(1)}, f32[256,128]{1,0:T(8,128)S(1)}, u32[]{:S(2)}, u32[]{:S(2)}) collective-permute-start(f32[256,128]{1,0:T(8,128)S(1)} %get-tuple-element.89), channel_id=1, source_target_pairs={{0,4},{4,0},{8,12},{12,8},{16,20},{20,16},{24,28},{28,24},{1,5},{5... | collective-permute-start | bytes 393224 | tf_op jit(solution)/shard_map/ppermute | solution.py:128
  57.8 6.7 %collective-permute-start.17 = (f32[256,128]{1,0:T(8,128)S(1)}, f32[256,128]{1,0:T(8,128)S(1)}, u32[]{:S(2)}, u32[]{:S(2)}) collective-permute-start(f32[256,128]{1,0:T(8,128)S(1)} %get-tuple-element.87), channel_id=1, source_target_pairs={{0,4},{4,0},{8,12},{12,8},{16,20},{20,16},{24,28},{28,24},{1,5},{5... | collective-permute-start | bytes 393224 | tf_op jit(solution)/shard_map/ppermute | solution.py:128
  57.9 13.4 %collective-permute-start.16 = (f32[256,128]{1,0:T(8,128)S(1)}, f32[256,128]{1,0:T(8,128)S(1)}, u32[]{:S(2)}, u32[]{:S(2)}) collective-permute-start(f32[256,128]{1,0:T(8,128)S(1)} %get-tuple-element.85), channel_id=1, source_target_pairs={{0,4},{4,0},{8,12},{12,8},{16,20},{20,16},{24,28},{28,24},{1,5},{5... | collective-permute-start | bytes 393224 | tf_op jit(solution)/shard_map/ppermute | solution.py:128
  63.3 8.0 %collective-permute-start.22 = (f32[256,128]{1,0:T(8,128)S(1)}, f32[256,128]{1,0:T(8,128)S(1)}, u32[]{:S(2)}, u32[]{:S(2)}) collective-permute-start(f32[256,128]{1,0:T(8,128)S(1)} %add.32), channel_id=1, source_target_pairs={{0,8},{4,12},{8,0},{12,4},{16,24},{20,28},{24,16},{28,20},{1,9},{5... | collective-permute-start | bytes 393224 | tf_op jit(solution)/shard_map/ppermute | solution.py:128
  63.9 7.4 %collective-permute-start.20 = (f32[256,128]{1,0:T(8,128)S(1)}, f32[256,128]{1,0:T(8,128)S(1)}, u32[]{:S(2)}, u32[]{:S(2)}) collective-permute-start(f32[256,128]{1,0:T(8,128)S(1)} %add.31), channel_id=1, source_target_pairs={{0,16},{4,20},{8,24},{12,28},{16,0},{20,4},{24,8},{28,12},{1,17},{... | collective-permute-start | bytes 393224 | tf_op jit(solution)/shard_map/ppermute | solution.py:128
  64.5 7.5 %collective-permute-start.18 = (f32[256,128]{1,0:T(8,128)S(1)}, f32[256,128]{1,0:T(8,128)S(1)}, u32[]{:S(2)}, u32[]{:S(2)}) collective-permute-start(f32[256,128]{1,0:T(8,128)S(1)} %add.30), channel_id=1, source_target_pairs={{0,24},{4,28},{8,16},{12,20},{16,8},{20,12},{24,0},{28,4},{1,25},{... | collective-permute-start | bytes 393224 | tf_op jit(solution)/shard_map/ppermute | solution.py:128
  73.4 6.1 %collective-permute-start.35 = (bf16[512,128]{1,0:T(8,128)(2,1)S(1)}, bf16[512,128]{1,0:T(8,128)(2,1)S(1)}, u32[]{:S(2)}, u32[]{:S(2)}) collective-permute-start(bf16[512,128]{1,0:T(8,128)(2,1)S(1)} %get-tuple-element.108.refs_0_), channel_id=1, source_target_pairs={{0,8},{4,12},{8,0},{12,4},{16,24},{20,28},{24,16},{28,20},{1,9},{5... | collective-permute-start | bytes 393224 | tf_op jit(solution)/shard_map/ppermute | solution.py:128
  74.9 7.0 %collective-permute-start.37 = (bf16[512,128]{1,0:T(8,128)(2,1)S(1)}, bf16[512,128]{1,0:T(8,128)(2,1)S(1)}, u32[]{:S(2)}, u32[]{:S(2)}) collective-permute-start(bf16[512,128]{1,0:T(8,128)(2,1)S(1)} %get-tuple-element.108.refs_0_), channel_id=1, source_target_pairs={{0,16},{4,20},{8,24},{12,28},{16,0},{20,4},{24,8},{28,12},{1,17},{... | collective-permute-start | bytes 393224 | tf_op jit(solution)/shard_map/ppermute | solution.py:128
  75.9 6.0 %collective-permute-start.39 = (bf16[512,128]{1,0:T(8,128)(2,1)S(1)}, bf16[512,128]{1,0:T(8,128)(2,1)S(1)}, u32[]{:S(2)}, u32[]{:S(2)}) collective-permute-start(bf16[512,128]{1,0:T(8,128)(2,1)S(1)} %get-tuple-element.108.refs_0_), channel_id=1, source_target_pairs={{0,24},{4,28},{8,16},{12,20},{16,8},{20,12},{24,0},{28,4},{1,25},{... | collective-permute-start | bytes 393224 | tf_op jit(solution)/shard_map/ppermute | solution.py:128
  77.0 5.4 %collective-permute-start.34 = (bf16[512,128]{1,0:T(8,128)(2,1)S(1)}, bf16[512,128]{1,0:T(8,128)(2,1)S(1)}, u32[]{:S(2)}, u32[]{:S(2)}) collective-permute-start(bf16[512,128]{1,0:T(8,128)(2,1)S(1)} %get-tuple-element.108.refs_0_), channel_id=1, source_target_pairs={{0,4},{4,0},{8,12},{12,8},{16,20},{20,16},{24,28},{28,24},{1,5},{5... | collective-permute-start | bytes 393224 | tf_op jit(solution)/shard_map/ppermute | solution.py:128
  79.5 2.9 %collective-permute-start.36 = (bf16[512,128]{1,0:T(8,128)(2,1)S(1)}, bf16[512,128]{1,0:T(8,128)(2,1)S(1)}, u32[]{:S(2)}, u32[]{:S(2)}) collective-permute-start(bf16[512,128]{1,0:T(8,128)(2,1)S(1)} %collective-permute-done.35.refs_2_), channel_id=1, source_target_pairs={{0,4},{4,0},{8,12},{12,8},{16,20},{20,16},{24,28},{28,24},{1,5},{5... | collective-permute-start | bytes 393224 | tf_op jit(solution)/shard_map/ppermute | solution.py:128
  81.9 1.3 collective-permute-start.38
  81.9 1.5 %collective-permute-start.40 = (bf16[512,128]{1,0:T(8,128)(2,1)S(1)}, bf16[512,128]{1,0:T(8,128)(2,1)S(1)}, u32[]{:S(2)}, u32[]{:S(2)}) collective-permute-start(bf16[512,128]{1,0:T(8,128)(2,1)S(1)} %collective-permute-done.39.refs_6_), channel_id=1, source_target_pairs={{0,4},{4,0},{8,12},{12,8},{16,20},{20,16},{24,28},{28,24},{1,5},{5... | collective-permute-start | bytes 393224 | tf_op jit(solution)/shard_map/ppermute | solution.py:128
  84.6 6.4 %collective-permute-start.54 = (f32[64,256]{1,0:T(8,128)S(1)}, f32[64,256]{1,0:T(8,128)S(1)}, u32[]{:S(2)}, u32[]{:S(2)}) collective-permute-start(f32[64,256]{1,0:T(8,128)S(1)} %get-tuple-element.128), channel_id=1, source_target_pairs={{0,1},{1,0},{2,3},{3,2},{4,5},{5,4},{6,7},{7,6},{8,9},{9,8},{10,11... | collective-permute-start | bytes 196616 | tf_op jit(solution)/shard_map/ppermute | solution.py:128
  86.6 5.1 %collective-permute-start.41 = (bf16[256,128]{1,0:T(8,128)(2,1)S(1)}, bf16[256,128]{1,0:T(8,128)(2,1)S(1)}, u32[]{:S(2)}, u32[]{:S(2)}) collective-permute-start(bf16[256,128]{1,0:T(8,128)(2,1)S(1)} %get-tuple-element.110), channel_id=1, source_target_pairs={{0,1},{1,0},{2,3},{3,2},{4,5},{5,4},{6,7},{7,6},{8,9},{9,8},{10,11... | collective-permute-start | bytes 196616 | tf_op jit(solution)/shard_map/ppermute | solution.py:128
  87.0 9.9 %collective-permute-start.42 = (bf16[256,128]{1,0:T(8,128)(2,1)S(1)}, bf16[256,128]{1,0:T(8,128)(2,1)S(1)}, u32[]{:S(2)}, u32[]{:S(2)}) collective-permute-start(bf16[256,128]{1,0:T(8,128)(2,1)S(1)} %get-tuple-element.111), channel_id=1, source_target_pairs={{0,2},{1,3},{2,0},{3,1},{4,6},{5,7},{6,4},{7,5},{8,10},{9,11},{10,... | collective-permute-start | bytes 196616 | tf_op jit(solution)/shard_map/ppermute | solution.py:128
  89.0 8.0 %collective-permute-start.43 = (bf16[256,128]{1,0:T(8,128)(2,1)S(1)}, bf16[256,128]{1,0:T(8,128)(2,1)S(1)}, u32[]{:S(2)}, u32[]{:S(2)}) collective-permute-start(bf16[256,128]{1,0:T(8,128)(2,1)S(1)} %get-tuple-element.112), channel_id=1, source_target_pairs={{0,3},{1,2},{2,1},{3,0},{4,7},{5,6},{6,5},{7,4},{8,11},{9,10},{10,... | collective-permute-start | bytes 196616 | tf_op jit(solution)/shard_map/ppermute | solution.py:128
  91.0 11.9 %collective-permute-start.55 = (f32[64,256]{1,0:T(8,128)S(1)}, f32[64,256]{1,0:T(8,128)S(1)}, u32[]{:S(2)}, u32[]{:S(2)}) collective-permute-start(f32[64,256]{1,0:T(8,128)S(1)} %add.38), channel_id=1, source_target_pairs={{0,2},{1,3},{2,0},{3,1},{4,6},{5,7},{6,4},{7,5},{8,10},{9,11},{10,... | collective-permute-start | bytes 196616 | tf_op jit(solution)/shard_map/ppermute | solution.py:128
  98.5 10.3 %collective-permute-start.44 = (f32[256,128]{1,0:T(8,128)S(1)}, f32[256,128]{1,0:T(8,128)S(1)}, u32[]{:S(2)}, u32[]{:S(2)}) collective-permute-start(f32[256,128]{1,0:T(8,128)S(1)} %get-tuple-element.114), channel_id=1, source_target_pairs={{0,1},{1,0},{2,3},{3,2},{4,5},{5,4},{6,7},{7,6},{8,9},{9,8},{10,11... | collective-permute-start | bytes 393224 | tf_op jit(solution)/shard_map/ppermute | solution.py:128
  100.5 11.1 %collective-permute-start.45 = (f32[256,128]{1,0:T(8,128)S(1)}, f32[256,128]{1,0:T(8,128)S(1)}, u32[]{:S(2)}, u32[]{:S(2)}) collective-permute-start(f32[256,128]{1,0:T(8,128)S(1)} %get-tuple-element.115), channel_id=1, source_target_pairs={{0,2},{1,3},{2,0},{3,1},{4,6},{5,7},{6,4},{7,5},{8,10},{9,11},{10,... | collective-permute-start | bytes 393224 | tf_op jit(solution)/shard_map/ppermute | solution.py:128
  101.2 10.3 %collective-permute-start.46 = (f32[256,128]{1,0:T(8,128)S(1)}, f32[256,128]{1,0:T(8,128)S(1)}, u32[]{:S(2)}, u32[]{:S(2)}) collective-permute-start(f32[256,128]{1,0:T(8,128)S(1)} %get-tuple-element.116), channel_id=1, source_target_pairs={{0,3},{1,2},{2,1},{3,0},{4,7},{5,6},{6,5},{7,4},{8,11},{9,10},{10,... | collective-permute-start | bytes 393224 | tf_op jit(solution)/shard_map/ppermute | solution.py:128
  103.0 5.8 %collective-permute-start.57 = (f32[64,256]{1,0:T(8,128)S(1)}, f32[64,256]{1,0:T(8,128)S(1)}, u32[]{:S(2)}, u32[]{:S(2)}) collective-permute-start(f32[64,256]{1,0:T(8,128)S(1)} %add.39.refs_0_), channel_id=1, source_target_pairs={{0,1},{1,0},{2,3},{3,2},{4,5},{5,4},{6,7},{7,6},{8,9},{9,8},{10,11... | collective-permute-start | bytes 196616 | tf_op jit(solution)/shard_map/ppermute | solution.py:128
  104.0 8.5 %collective-permute-start.56 = (f32[64,256]{1,0:T(8,128)S(1)}, f32[64,256]{1,0:T(8,128)S(1)}, u32[]{:S(2)}, u32[]{:S(2)}) collective-permute-start(f32[64,256]{1,0:T(8,128)S(1)} %add.39.refs_0_), channel_id=1, source_target_pairs={{0,4},{4,0},{8,12},{12,8},{16,20},{20,16},{24,28},{28,24},{1,5},{5... | collective-permute-start | bytes 196616 | tf_op jit(solution)/shard_map/ppermute | solution.py:128
  108.8 3.8 %collective-permute-start.58 = (f32[64,256]{1,0:T(8,128)S(1)}, f32[64,256]{1,0:T(8,128)S(1)}, u32[]{:S(2)}, u32[]{:S(2)}) collective-permute-start(f32[64,256]{1,0:T(8,128)S(1)} %collective-permute-done.57.refs_2_), channel_id=1, source_target_pairs={{0,4},{4,0},{8,12},{12,8},{16,20},{20,16},{24,28},{28,24},{1,5},{5... | collective-permute-start | bytes 196616 | tf_op jit(solution)/shard_map/ppermute | solution.py:128
  108.8 25.7 %collective-permute-start.31 = (f32[64,128]{1,0:T(8,128)S(1)}, f32[64,128]{1,0:T(8,128)S(1)}, u32[]{:S(2)}, u32[]{:S(2)}) collective-permute-start(f32[64,128]{1,0:T(8,128)S(1)} %get-tuple-element.104), channel_id=1, source_target_pairs={{0,1},{1,0},{2,3},{3,2},{4,5},{5,4},{6,7},{7,6},{8,9},{9,8},{10,11... | collective-permute-start | bytes 98312 | tf_op jit(solution)/shard_map/ppermute | solution.py:128
  111.9 6.0 %collective-permute-start.52 = (f32[256,128]{1,0:T(8,128)S(1)}, f32[256,128]{1,0:T(8,128)S(1)}, u32[]{:S(2)}, u32[]{:S(2)}) collective-permute-start(f32[256,128]{1,0:T(8,128)S(1)} %get-tuple-element.124), channel_id=1, source_target_pairs={{0,4},{4,0},{8,12},{12,8},{16,20},{20,16},{24,28},{28,24},{1,5},{5... | collective-permute-start | bytes 393224 | tf_op jit(solution)/shard_map/ppermute | solution.py:128
  112.0 7.1 %collective-permute-start.50 = (f32[256,128]{1,0:T(8,128)S(1)}, f32[256,128]{1,0:T(8,128)S(1)}, u32[]{:S(2)}, u32[]{:S(2)}) collective-permute-start(f32[256,128]{1,0:T(8,128)S(1)} %get-tuple-element.122), channel_id=1, source_target_pairs={{0,4},{4,0},{8,12},{12,8},{16,20},{20,16},{24,28},{28,24},{1,5},{5... | collective-permute-start | bytes 393224 | tf_op jit(solution)/shard_map/ppermute | solution.py:128
  112.5 7.8 %collective-permute-start.48 = (f32[256,128]{1,0:T(8,128)S(1)}, f32[256,128]{1,0:T(8,128)S(1)}, u32[]{:S(2)}, u32[]{:S(2)}) collective-permute-start(f32[256,128]{1,0:T(8,128)S(1)} %get-tuple-element.120), channel_id=1, source_target_pairs={{0,4},{4,0},{8,12},{12,8},{16,20},{20,16},{24,28},{28,24},{1,5},{5... | collective-permute-start | bytes 393224 | tf_op jit(solution)/shard_map/ppermute | solution.py:128
  112.6 13.6 %collective-permute-start.47 = (f32[256,128]{1,0:T(8,128)S(1)}, f32[256,128]{1,0:T(8,128)S(1)}, u32[]{:S(2)}, u32[]{:S(2)}) collective-permute-start(f32[256,128]{1,0:T(8,128)S(1)} %get-tuple-element.118), channel_id=1, source_target_pairs={{0,4},{4,0},{8,12},{12,8},{16,20},{20,16},{24,28},{28,24},{1,5},{5... | collective-permute-start | bytes 393224 | tf_op jit(solution)/shard_map/ppermute | solution.py:128
  118.0 10.9 %collective-permute-start.53 = (f32[256,128]{1,0:T(8,128)S(1)}, f32[256,128]{1,0:T(8,128)S(1)}, u32[]{:S(2)}, u32[]{:S(2)}) collective-permute-start(f32[256,128]{1,0:T(8,128)S(1)} %add.37), channel_id=1, source_target_pairs={{0,8},{4,12},{8,0},{12,4},{16,24},{20,28},{24,16},{28,20},{1,9},{5... | collective-permute-start | bytes 393224 | tf_op jit(solution)/shard_map/ppermute | solution.py:128
  119.1 11.8 %collective-permute-start.51 = (f32[256,128]{1,0:T(8,128)S(1)}, f32[256,128]{1,0:T(8,128)S(1)}, u32[]{:S(2)}, u32[]{:S(2)}) collective-permute-start(f32[256,128]{1,0:T(8,128)S(1)} %add.36), channel_id=1, source_target_pairs={{0,16},{4,20},{8,24},{12,28},{16,0},{20,4},{24,8},{28,12},{1,17},{... | collective-permute-start | bytes 393224 | tf_op jit(solution)/shard_map/ppermute | solution.py:128
  120.3 10.6 %collective-permute-start.49 = (f32[256,128]{1,0:T(8,128)S(1)}, f32[256,128]{1,0:T(8,128)S(1)}, u32[]{:S(2)}, u32[]{:S(2)}) collective-permute-start(f32[256,128]{1,0:T(8,128)S(1)} %add.35), channel_id=1, source_target_pairs={{0,24},{4,28},{8,16},{12,20},{16,8},{20,12},{24,0},{28,4},{1,25},{... | collective-permute-start | bytes 393224 | tf_op jit(solution)/shard_map/ppermute | solution.py:128
  126.2 10.4 %collective-permute-start.32 = (f32[64,128]{1,0:T(8,128)S(1)}, f32[64,128]{1,0:T(8,128)S(1)}, u32[]{:S(2)}, u32[]{:S(2)}) collective-permute-start(f32[64,128]{1,0:T(8,128)S(1)} %get-tuple-element.105), channel_id=1, source_target_pairs={{0,2},{1,3},{2,0},{3,1},{4,6},{5,7},{6,4},{7,5},{8,10},{9,11},{10,... | collective-permute-start | bytes 98312 | tf_op jit(solution)/shard_map/ppermute | solution.py:128
  128.9 7.7 %collective-permute-start.33 = (f32[64,128]{1,0:T(8,128)S(1)}, f32[64,128]{1,0:T(8,128)S(1)}, u32[]{:S(2)}, u32[]{:S(2)}) collective-permute-start(f32[64,128]{1,0:T(8,128)S(1)} %get-tuple-element.106), channel_id=1, source_target_pairs={{0,3},{1,2},{2,1},{3,0},{4,7},{5,6},{6,5},{7,4},{8,11},{9,10},{10,... | collective-permute-start | bytes 98312 | tf_op jit(solution)/shard_map/ppermute | solution.py:128
  132.1 5.2 %collective-permute-start.59 = (f32[64,128]{1,0:T(8,128)S(1)}, f32[64,128]{1,0:T(8,128)S(1)}, u32[]{:S(2)}, u32[]{:S(2)}) collective-permute-start(f32[64,128]{1,0:T(8,128)S(1)} %get-tuple-element.132), channel_id=1, source_target_pairs={{0,1},{1,0},{2,3},{3,2},{4,5},{5,4},{6,7},{7,6},{8,9},{9,8},{10,11... | collective-permute-start | bytes 98312 | tf_op jit(solution)/shard_map/ppermute | solution.py:128
  132.2 5.1 %collective-permute-start.60 = (f32[64,128]{1,0:T(8,128)S(1)}, f32[64,128]{1,0:T(8,128)S(1)}, u32[]{:S(2)}, u32[]{:S(2)}) collective-permute-start(f32[64,128]{1,0:T(8,128)S(1)} %get-tuple-element.133), channel_id=1, source_target_pairs={{0,2},{1,3},{2,0},{3,1},{4,6},{5,7},{6,4},{7,5},{8,10},{9,11},{10,... | collective-permute-start | bytes 98312 | tf_op jit(solution)/shard_map/ppermute | solution.py:128
  134.5 5.7 %collective-permute-start.61 = (f32[64,128]{1,0:T(8,128)S(1)}, f32[64,128]{1,0:T(8,128)S(1)}, u32[]{:S(2)}, u32[]{:S(2)}) collective-permute-start(f32[64,128]{1,0:T(8,128)S(1)} %get-tuple-element.134), channel_id=1, source_target_pairs={{0,3},{1,2},{2,1},{3,0},{4,7},{5,6},{6,5},{7,4},{8,11},{9,10},{10,... | collective-permute-start | bytes 98312 | tf_op jit(solution)/shard_map/ppermute | solution.py:128
  (7 other events, 17.3 us)

commit v3 on v1

--- a/solution.py
+++ b/solution.py
@@ -207,25 +207,25 @@
 
 def gram_kernel(*refs):
     pairs, (half_ref, rows_ref) = refs[:-2], refs[-2:]
-    rank = rows_ref.shape[0]
+    half, rank = half_ref.shape
     width = pairs[0].shape[1]
     for k, pair in enumerate(pairs):
-        rows_ref[:, k * width : (k + 1) * width] = pair[:rank].astype(jnp.float32) + pair[
-            rank:
-        ].astype(jnp.float32)
-    half = half_ref.shape[0]
+        rows_ref[:, k * width : (k + 1) * width] = pair[...]
     start = pl.multiple_of(lax.axis_index("wide") % 2 * half, half)
-    half_ref[...] = lax.dot_general(
-        rows_ref[pl.ds(start, half), :], rows_ref[...], (((1,), (1,)), ((), ())),
-        precision=HIGHEST, preferred_element_type=jnp.float32,
-    )
+    mine = jnp.concatenate([rows_ref[pl.ds(start + k * rank, half), :] for k in range(2)])
+    products = lax.dot_general(
+        mine, rows_ref[...], (((1,), (1,)), ((), ())), preferred_element_type=jnp.float32
+    )
+    rounded = products[:half, :rank]
+    mixed = products[:half, rank:] + products[half:, :rank]
+    half_ref[...] = rounded + (mixed + products[half:, rank:])
 
 
 def joint_gram(pairs):
     rank, width = pairs[0].shape[0] // 2, pairs[0].shape[1]
     (total,) = kernel_call(
         gram_kernel, [shape((rank // 2, rank))], *pairs,
-        scratch=[pltpu.VMEM((rank, len(pairs) * width), jnp.float32)],
+        scratch=[pltpu.VMEM((2 * rank, len(pairs) * width), jnp.bfloat16)],
         flops=1_500_000_000,
     )
     mask = 1

time: 148 us -> 148 us (level)
  Pallas kernels: 30 us -> 28.5 us
    pallas_call x21, Pallas kernels: 30 us -> 28.5 us  [kernel_call(): pl.pallas_call(kernel, out_shape=tuple(out_shape), in_specs=[spec] * len(...]
  transfers between devices with their start and end apart: 58 -> 58, of which waited for: 20 -> 21; matrix products, arithmetic and copies ran while one was open for 0% -> 0% of each run, Pallas kernels for 19% -> 18%
where the time goes in v3:
time: 148 us
  waiting for transfers between devices  59.7 us (40%)
  starting transfers between devices  55.6 us (38%)
  Pallas kernels  28.5 us (19%)
  local copies, waits for them, and re-layouts  2.91 us (2%)
    ppermute x58, waiting for transfers between devices, swap(): return lax.ppermute(x, axis, [(i, i ^ mask) for i in range(size)])  59.7 us
    ppermute x58, starting transfers between devices, swap(): return lax.ppermute(x, axis, [(i, i ^ mask) for i in range(size)])  55.6 us
    pallas_call x21, Pallas kernels, kernel_call(): pl.pallas_call(kernel, out_shape=tuple(out_shape), in_specs=[spec] * len(...  28.5 us
  transfers between devices with their start and end apart: 58, of which 21 were waited for; matrix products, arithmetic and copies ran while one was open for 0% of the time, Pallas kernels for 18%

profile of v3, /device:TPU:0, one launch (start us, length us, event | category | flops | bytes accessed | tf_op | source)
XLA Modules:
  0.0 148.0 jit_solution(10171795898233491820)
XLA Ops:
  0.6 0.9 copy-done.1
  1.6 3.1 %collective-permute-start = (f32[64,128]{1,0:T(8,128)S(1)}, f32[64,128]{1,0:T(8,128)S(1)}, u32[]{:S(2)}, u32[]{:S(2)}) collective-permute-start(f32[64,128]{1,0:T(8,128)S(1)} %get-tuple-element.68), channel_id=1, source_target_pairs={{0,1},{1,0},{2,3},{3,2},{4,5},{5,4},{6,7},{7,6},{8,9},{9,8},{10,11... | collective-permute-start | bytes 98312 | tf_op jit(solution)/shard_map/ppermute | solution.py:126
  4.7 2.6 %collective-permute-start.1 = (f32[64,128]{1,0:T(8,128)S(1)}, f32[64,128]{1,0:T(8,128)S(1)}, u32[]{:S(2)}, u32[]{:S(2)}) collective-permute-start(f32[64,128]{1,0:T(8,128)S(1)} %get-tuple-element.69), channel_id=1, source_target_pairs={{0,2},{1,3},{2,0},{3,1},{4,6},{5,7},{6,4},{7,5},{8,10},{9,11},{10,... | collective-permute-start | bytes 98312 | tf_op jit(solution)/shard_map/ppermute | solution.py:126
  7.3 2.8 %collective-permute-done.1.refs_2_ = f32[64,128]{1,0:T(8,128)S(1)} collective-permute-done((f32[64,128]{1,0:T(8,128)S(1)}, f32[64,128]{1,0:T(8,128)S(1)}, u32[]{:S(2)}, u32[]{:S(2)}) %collective-permute-start.1) | collective-permute-done | bytes 32800 | tf_op jit(solution)/shard_map/ppermute | solution.py:126
  10.1 2.9 %collective-permute-done.2.refs_3_ = f32[64,128]{1,0:T(8,128)S(1)} collective-permute-done((f32[64,128]{1,0:T(8,128)S(1)}, f32[64,128]{1,0:T(8,128)S(1)}, u32[]{:S(2)}, u32[]{:S(2)}) %collective-permute-start.2) | collective-permute-done | bytes 32800 | tf_op jit(solution)/shard_map/ppermute | solution.py:126
  13.0 1.6 %collective-permute-start.4 = (bf16[512,128]{1,0:T(8,128)(2,1)S(1)}, bf16[512,128]{1,0:T(8,128)(2,1)S(1)}, u32[]{:S(2)}, u32[]{:S(2)}) collective-permute-start(bf16[512,128]{1,0:T(8,128)(2,1)S(1)} %get-tuple-element.71.refs_0_), channel_id=1, source_target_pairs={{0,8},{4,12},{8,0},{12,4},{16,24},{20,28},{24,16},{28,20},{1,9},{5... | collective-permute-start | bytes 393224 | tf_op jit(solution)/shard_map/ppermute | solution.py:126
  14.6 1.5 %collective-permute-start.6 = (bf16[512,128]{1,0:T(8,128)(2,1)S(1)}, bf16[512,128]{1,0:T(8,128)(2,1)S(1)}, u32[]{:S(2)}, u32[]{:S(2)}) collective-permute-start(bf16[512,128]{1,0:T(8,128)(2,1)S(1)} %get-tuple-element.71.refs_0_), channel_id=1, source_target_pairs={{0,16},{4,20},{8,24},{12,28},{16,0},{20,4},{24,8},{28,12},{1,17},{... | collective-permute-start | bytes 393224 | tf_op jit(solution)/shard_map/ppermute | solution.py:126
  16.6 0.7 copy-done.3
  17.2 0.7 copy-done.4
  17.9 0.7 copy-done.5
  18.6 0.6 shard_map.120
  19.7 0.6 collective-permute-done.6.refs_4_
  20.3 1.6 %collective-permute-done.8.refs_6_ = bf16[512,128]{1,0:T(8,128)(2,1)S(1)} collective-permute-done((bf16[512,128]{1,0:T(8,128)(2,1)S(1)}, bf16[512,128]{1,0:T(8,128)(2,1)S(1)}, u32[]{:S(2)}, u32[]{:S(2)}) %collective-permute-start.8) | collective-permute-done | bytes 131104 | tf_op jit(solution)/shard_map/ppermute | solution.py:126
  22.0 1.3 collective-permute-done.9.refs_7_
  23.7 0.9 collective-permute-start.11
  24.6 3.5 %collective-permute-start.12 = (bf16[256,128]{1,0:T(8,128)(2,1)S(1)}, bf16[256,128]{1,0:T(8,128)(2,1)S(1)}, u32[]{:S(2)}, u32[]{:S(2)}) collective-permute-start(bf16[256,128]{1,0:T(8,128)(2,1)S(1)} %get-tuple-element.75), channel_id=1, source_target_pairs={{0,3},{1,2},{2,1},{3,0},{4,7},{5,6},{6,5},{7,4},{8,11},{9,10},{10,... | collective-permute-start | bytes 196616 | tf_op jit(solution)/shard_map/ppermute | solution.py:126
  28.0 0.6 shard_map.128
  28.8 3.4 %collective-permute-done.11.refs_2_ = bf16[256,128]{1,0:T(8,128)(2,1)S(1)} collective-permute-done((bf16[256,128]{1,0:T(8,128)(2,1)S(1)}, bf16[256,128]{1,0:T(8,128)(2,1)S(1)}, u32[]{:S(2)}, u32[]{:S(2)}) %collective-permute-start.11) | collective-permute-done | bytes 65568 | tf_op jit(solution)/shard_map/ppermute | solution.py:126
  32.4 1.5 %shard_map.124 = (f32[256,128]{1,0:T(8,128)S(1)}, f32[256,128]{1,0:T(8,128)S(1)}, f32[256,128]{1,0:T(8,128)S(1)}, f32[256,128]{1,0:T(8,128)S(1)}) custom-call(bf16[1,8,512,512]{3,2,1,0:T(8,128)(2,1)S(1)} %copy-done, f32[8,256]{1,0:T(8,128)S(1)} %copy-done.2, bf16[256,128]{1,0:T(8,128)(2,1)S(1)} %get-tuple-element.72.refs_0_, ...), custom_call_target="tpu_custom_call" | custom-call | flops 1073741824 | bytes 4988928 | tf_op jit(solution)/shard_map/pallas_call | solution.py:109
  33.9 1.3 collective-permute-start.13
  35.2 1.8 %collective-permute-start.14 = (f32[256,128]{1,0:T(8,128)S(1)}, f32[256,128]{1,0:T(8,128)S(1)}, u32[]{:S(2)}, u32[]{:S(2)}) collective-permute-start(f32[256,128]{1,0:T(8,128)S(1)} %get-tuple-element.78), channel_id=1, source_target_pairs={{0,2},{1,3},{2,0},{3,1},{4,6},{5,7},{6,4},{7,5},{8,10},{9,11},{10,... | collective-permute-start | bytes 393224 | tf_op jit(solution)/shard_map/ppermute | solution.py:126
  37.0 1.4 collective-permute-start.15
  38.9 2.9 %collective-permute-start.23 = (f32[192,128]{1,0:T(8,128)S(1)}, f32[192,128]{1,0:T(8,128)S(1)}, u32[]{:S(2)}, u32[]{:S(2)}) collective-permute-start(f32[192,128]{1,0:T(8,128)S(1)} %get-tuple-element.90), channel_id=1, source_target_pairs={{0,1},{1,0},{2,3},{3,2},{4,5},{5,4},{6,7},{7,6},{8,9},{9,8},{10,11... | collective-permute-start | bytes 294920 | tf_op jit(solution)/shard_map/ppermute | solution.py:126
  42.0 9.6 %collective-permute-done.14.refs_2_ = f32[256,128]{1,0:T(8,128)S(1)} collective-permute-done((f32[256,128]{1,0:T(8,128)S(1)}, f32[256,128]{1,0:T(8,128)S(1)}, u32[]{:S(2)}, u32[]{:S(2)}) %collective-permute-start.14) | collective-permute-done | bytes 131104 | tf_op jit(solution)/shard_map/ppermute | solution.py:126
  52.6 4.5 %collective-permute-done.27 = f32[128,256]{1,0:T(8,128)S(1)} collective-permute-done((f32[128,256]{1,0:T(8,128)S(1)}, f32[128,256]{1,0:T(8,128)S(1)}, u32[]{:S(2)}, u32[]{:S(2)}) %collective-permute-start.27) | collective-permute-done | bytes 131104 | tf_op jit(solution)/shard_map/ppermute | solution.py:126
  57.2 0.6 collective-permute-start.28
  58.2 1.6 %collective-permute-start.25 = (f32[192,128]{1,0:T(8,128)S(1)}, f32[192,128]{1,0:T(8,128)S(1)}, u32[]{:S(2)}, u32[]{:S(2)}) collective-permute-start(f32[192,128]{1,0:T(8,128)S(1)} %get-tuple-element.92), channel_id=1, source_target_pairs={{0,3},{1,2},{2,1},{3,0},{4,7},{5,6},{6,5},{7,4},{8,11},{9,10},{10,... | collective-permute-start | bytes 294920 | tf_op jit(solution)/shard_map/ppermute | solution.py:126
  59.8 4.8 %collective-permute-done.25.refs_4_ = f32[192,128]{1,0:T(8,128)S(1)} collective-permute-done((f32[192,128]{1,0:T(8,128)S(1)}, f32[192,128]{1,0:T(8,128)S(1)}, u32[]{:S(2)}, u32[]{:S(2)}) %collective-permute-start.25) | collective-permute-done | bytes 98336 | tf_op jit(solution)/shard_map/ppermute | solution.py:126
  64.8 0.7 collective-permute-start.22
  65.5 1.2 collective-permute-start.20
  66.7 1.9 %collective-permute-start.18 = (f32[256,128]{1,0:T(8,128)S(1)}, f32[256,128]{1,0:T(8,128)S(1)}, u32[]{:S(2)}, u32[]{:S(2)}) collective-permute-start(f32[256,128]{1,0:T(8,128)S(1)} %add.30), channel_id=1, source_target_pairs={{0,24},{4,28},{8,16},{12,20},{16,8},{20,12},{24,0},{28,4},{1,25},{... | collective-permute-start | bytes 393224 | tf_op jit(solution)/shard_map/ppermute | solution.py:126
  68.5 5.0 %shard_map.129 = (f32[256,256]{1,0:T(8,128)S(1)}, f32[1,128]{1,0:T(1,128)S(1)}) custom-call(f32[8,256]{1,0:T(8,128)S(1)} %copy-done.2, f32[128,256]{1,0:T(8,128)S(1)} %add.34.refs_0_, f32[128,256]{1,0:T(8,128)S(1)} %collective-permute-done.28.refs_1_), custom_call_target="tpu_custom_call" | custom-call | flops 6000000000 | bytes 532992 | tf_op jit(solution)/shard_map/pallas_call | solution.py:109
  73.5 4.2 %shard_map.130.refs_8_ = f32[256,256]{1,0:T(8,128)S(1)} custom-call(f32[256,256]{1,0:T(8,128)S(1)} %get-tuple-element.96.half_ref), custom_call_target="tpu_custom_call" | custom-call | flops 6000000000 | bytes 524288 | tf_op jit(solution)/shard_map/pallas_call | solution.py:109
  77.8 1.2 shard_map.131
  78.9 0.7 collective-permute-start.33
  79.6 1.1 collective-permute-start.35
  80.7 1.8 %collective-permute-start.37 = (bf16[512,128]{1,0:T(8,128)(2,1)S(1)}, bf16[512,128]{1,0:T(8,128)(2,1)S(1)}, u32[]{:S(2)}, u32[]{:S(2)}) collective-permute-start(bf16[512,128]{1,0:T(8,128)(2,1)S(1)} %get-tuple-element.102.refs_0_), channel_id=1, source_target_pairs={{0,24},{4,28},{8,16},{12,20},{16,8},{20,12},{24,0},{28,4},{1,25},{... | collective-permute-start | bytes 393224 | tf_op jit(solution)/shard_map/ppermute | solution.py:126
  82.5 2.9 %collective-permute-done.33.refs_2_ = bf16[512,128]{1,0:T(8,128)(2,1)S(1)} collective-permute-done((bf16[512,128]{1,0:T(8,128)(2,1)S(1)}, bf16[512,128]{1,0:T(8,128)(2,1)S(1)}, u32[]{:S(2)}, u32[]{:S(2)}) %collective-permute-start.33) | collective-permute-done | bytes 131104 | tf_op jit(solution)/shard_map/ppermute | solution.py:126
  85.9 2.1 %collective-permute-done.37.refs_6_ = bf16[512,128]{1,0:T(8,128)(2,1)S(1)} collective-permute-done((bf16[512,128]{1,0:T(8,128)(2,1)S(1)}, bf16[512,128]{1,0:T(8,128)(2,1)S(1)}, u32[]{:S(2)}, u32[]{:S(2)}) %collective-permute-start.37) | collective-permute-done | bytes 131104 | tf_op jit(solution)/shard_map/ppermute | solution.py:126
  88.0 1.3 collective-permute-done.38.refs_7_
  89.6 1.9 %collective-permute-start.40 = (bf16[256,128]{1,0:T(8,128)(2,1)S(1)}, bf16[256,128]{1,0:T(8,128)(2,1)S(1)}, u32[]{:S(2)}, u32[]{:S(2)}) collective-permute-start(bf16[256,128]{1,0:T(8,128)(2,1)S(1)} %get-tuple-element.105), channel_id=1, source_target_pairs={{0,2},{1,3},{2,0},{3,1},{4,6},{5,7},{6,4},{7,5},{8,10},{9,11},{10,... | collective-permute-start | bytes 196616 | tf_op jit(solution)/shard_map/ppermute | solution.py:126
  91.6 2.4 %collective-permute-start.41 = (bf16[256,128]{1,0:T(8,128)(2,1)S(1)}, bf16[256,128]{1,0:T(8,128)(2,1)S(1)}, u32[]{:S(2)}, u32[]{:S(2)}) collective-permute-start(bf16[256,128]{1,0:T(8,128)(2,1)S(1)} %get-tuple-element.106), channel_id=1, source_target_pairs={{0,3},{1,2},{2,1},{3,0},{4,7},{5,6},{6,5},{7,4},{8,11},{9,10},{10,... | collective-permute-start | bytes 196616 | tf_op jit(solution)/shard_map/ppermute | solution.py:126
  94.0 0.5 shard_map.136
  94.9 3.3 %collective-permute-done.40.refs_2_ = bf16[256,128]{1,0:T(8,128)(2,1)S(1)} collective-permute-done((bf16[256,128]{1,0:T(8,128)(2,1)S(1)}, bf16[256,128]{1,0:T(8,128)(2,1)S(1)}, u32[]{:S(2)}, u32[]{:S(2)}) %collective-permute-start.40) | collective-permute-done | bytes 65568 | tf_op jit(solution)/shard_map/ppermute | solution.py:126
  98.4 1.5 %shard_map.134 = (f32[256,128]{1,0:T(8,128)S(1)}, f32[256,128]{1,0:T(8,128)S(1)}, f32[256,128]{1,0:T(8,128)S(1)}, f32[256,128]{1,0:T(8,128)S(1)}) custom-call(bf16[1,8,512,512]{3,2,1,0:T(8,128)(2,1)S(1)} %copy-done, f32[8,256]{1,0:T(8,128)S(1)} %copy-done.2, bf16[256,128]{1,0:T(8,128)(2,1)S(1)} %get-tuple-element.103.refs_0_, ...), custom_call_target="tpu_custom_call" | custom-call | flops 1073741824 | bytes 4988928 | tf_op jit(solution)/shard_map/pallas_call | solution.py:109
  99.9 1.3 collective-permute-start.42
  101.1 1.8 %collective-permute-start.43 = (f32[256,128]{1,0:T(8,128)S(1)}, f32[256,128]{1,0:T(8,128)S(1)}, u32[]{:S(2)}, u32[]{:S(2)}) collective-permute-start(f32[256,128]{1,0:T(8,128)S(1)} %get-tuple-element.109), channel_id=1, source_target_pairs={{0,2},{1,3},{2,0},{3,1},{4,6},{5,7},{6,4},{7,5},{8,10},{9,11},{10,... | collective-permute-start | bytes 393224 | tf_op jit(solution)/shard_map/ppermute | solution.py:126
  103.0 1.4 collective-permute-start.44
  104.6 1.4 collective-permute-done.42.refs_1_
  106.0 9.8 %collective-permute-done.43.refs_2_ = f32[256,128]{1,0:T(8,128)S(1)} collective-permute-done((f32[256,128]{1,0:T(8,128)S(1)}, f32[256,128]{1,0:T(8,128)S(1)}, u32[]{:S(2)}, u32[]{:S(2)}) %collective-permute-start.43) | collective-permute-done | bytes 131104 | tf_op jit(solution)/shard_map/ppermute | solution.py:126
  116.9 3.0 %collective-permute-done.53 = f32[128,256]{1,0:T(8,128)S(1)} collective-permute-done((f32[128,256]{1,0:T(8,128)S(1)}, f32[128,256]{1,0:T(8,128)S(1)}, u32[]{:S(2)}, u32[]{:S(2)}) %collective-permute-start.53) | collective-permute-done | bytes 131104 | tf_op jit(solution)/shard_map/ppermute | solution.py:126
  120.1 0.6 collective-permute-start.29
  120.7 1.8 %collective-permute-start.51 = (f32[256,128]{1,0:T(8,128)S(1)}, f32[256,128]{1,0:T(8,128)S(1)}, u32[]{:S(2)}, u32[]{:S(2)}) collective-permute-start(f32[256,128]{1,0:T(8,128)S(1)} %add.37), channel_id=1, source_target_pairs={{0,8},{4,12},{8,0},{12,4},{16,24},{20,28},{24,16},{28,20},{1,9},{5... | collective-permute-start | bytes 393224 | tf_op jit(solution)/shard_map/ppermute | solution.py:126
  122.6 1.6 %collective-permute-start.49 = (f32[256,128]{1,0:T(8,128)S(1)}, f32[256,128]{1,0:T(8,128)S(1)}, u32[]{:S(2)}, u32[]{:S(2)}) collective-permute-start(f32[256,128]{1,0:T(8,128)S(1)} %add.36), channel_id=1, source_target_pairs={{0,16},{4,20},{8,24},{12,28},{16,0},{20,4},{24,8},{28,12},{1,17},{... | collective-permute-start | bytes 393224 | tf_op jit(solution)/shard_map/ppermute | solution.py:126
  124.5 5.0 %shard_map.137 = (f32[256,256]{1,0:T(8,128)S(1)}, f32[1,128]{1,0:T(1,128)S(1)}) custom-call(f32[8,256]{1,0:T(8,128)S(1)} %copy-done.2, f32[128,256]{1,0:T(8,128)S(1)} %add.39.refs_0_, f32[128,256]{1,0:T(8,128)S(1)} %collective-permute-done.54.refs_1_), custom_call_target="tpu_custom_call" | custom-call | flops 6000000000 | bytes 532992 | tf_op jit(solution)/shard_map/pallas_call | solution.py:109
  129.4 4.2 %shard_map.138.refs_8_ = f32[256,256]{1,0:T(8,128)S(1)} custom-call(f32[256,256]{1,0:T(8,128)S(1)} %get-tuple-element.122.half_ref), custom_call_target="tpu_custom_call" | custom-call | flops 6000000000 | bytes 524288 | tf_op jit(solution)/shard_map/pallas_call | solution.py:109
  133.7 2.2 %collective-permute-start.30 = (f32[64,128]{1,0:T(8,128)S(1)}, f32[64,128]{1,0:T(8,128)S(1)}, u32[]{:S(2)}, u32[]{:S(2)}) collective-permute-start(f32[64,128]{1,0:T(8,128)S(1)} %get-tuple-element.99), channel_id=1, source_target_pairs={{0,2},{1,3},{2,0},{3,1},{4,6},{5,7},{6,4},{7,5},{8,10},{9,11},{10,... | collective-permute-start | bytes 98312 | tf_op jit(solution)/shard_map/ppermute | solution.py:126
  135.9 1.8 %collective-permute-start.31 = (f32[64,128]{1,0:T(8,128)S(1)}, f32[64,128]{1,0:T(8,128)S(1)}, u32[]{:S(2)}, u32[]{:S(2)}) collective-permute-start(f32[64,128]{1,0:T(8,128)S(1)} %get-tuple-element.100), channel_id=1, source_target_pairs={{0,3},{1,2},{2,1},{3,0},{4,7},{5,6},{6,5},{7,4},{8,11},{9,10},{10,... | collective-permute-start | bytes 98312 | tf_op jit(solution)/shard_map/ppermute | solution.py:126
  137.7 1.2 shard_map.139
  139.0 2.5 %collective-permute-start.56 = (f32[64,128]{1,0:T(8,128)S(1)}, f32[64,128]{1,0:T(8,128)S(1)}, u32[]{:S(2)}, u32[]{:S(2)}) collective-permute-start(f32[64,128]{1,0:T(8,128)S(1)} %get-tuple-element.125), channel_id=1, source_target_pairs={{0,2},{1,3},{2,0},{3,1},{4,6},{5,7},{6,4},{7,5},{8,10},{9,11},{10,... | collective-permute-start | bytes 98312 | tf_op jit(solution)/shard_map/ppermute | solution.py:126
  141.5 1.8 %collective-permute-start.57 = (f32[64,128]{1,0:T(8,128)S(1)}, f32[64,128]{1,0:T(8,128)S(1)}, u32[]{:S(2)}, u32[]{:S(2)}) collective-permute-start(f32[64,128]{1,0:T(8,128)S(1)} %get-tuple-element.126), channel_id=1, source_target_pairs={{0,3},{1,2},{2,1},{3,0},{4,7},{5,6},{6,5},{7,4},{8,11},{9,10},{10,... | collective-permute-start | bytes 98312 | tf_op jit(solution)/shard_map/ppermute | solution.py:126
  143.3 0.7 shard_map.132
  144.1 3.1 %collective-permute-done.57.refs_3_ = f32[64,128]{1,0:T(8,128)S(1)} collective-permute-done((f32[64,128]{1,0:T(8,128)S(1)}, f32[64,128]{1,0:T(8,128)S(1)}, u32[]{:S(2)}, u32[]{:S(2)}) %collective-permute-start.57) | collective-permute-done | bytes 32800 | tf_op jit(solution)/shard_map/ppermute | solution.py:126
  147.2 0.7 shard_map.140
  (103 shorter events, 7.4 us)
Async XLA Ops:
  0.6 0.9 copy-start.1
  1.6 5.7 %collective-permute-start = (f32[64,128]{1,0:T(8,128)S(1)}, f32[64,128]{1,0:T(8,128)S(1)}, u32[]{:S(2)}, u32[]{:S(2)}) collective-permute-start(f32[64,128]{1,0:T(8,128)S(1)} %get-tuple-element.68), channel_id=1, source_target_pairs={{0,1},{1,0},{2,3},{3,2},{4,5},{5,4},{6,7},{7,6},{8,9},{9,8},{10,11... | collective-permute-start | bytes 98312 | tf_op jit(solution)/shard_map/ppermute | solution.py:126
  4.7 5.4 %collective-permute-start.1 = (f32[64,128]{1,0:T(8,128)S(1)}, f32[64,128]{1,0:T(8,128)S(1)}, u32[]{:S(2)}, u32[]{:S(2)}) collective-permute-start(f32[64,128]{1,0:T(8,128)S(1)} %get-tuple-element.69), channel_id=1, source_target_pairs={{0,2},{1,3},{2,0},{3,1},{4,6},{5,7},{6,4},{7,5},{8,10},{9,11},{10,... | collective-permute-start | bytes 98312 | tf_op jit(solution)/shard_map/ppermute | solution.py:126
  7.3 5.7 %collective-permute-start.2 = (f32[64,128]{1,0:T(8,128)S(1)}, f32[64,128]{1,0:T(8,128)S(1)}, u32[]{:S(2)}, u32[]{:S(2)}) collective-permute-start(f32[64,128]{1,0:T(8,128)S(1)} %get-tuple-element.70), channel_id=1, source_target_pairs={{0,3},{1,2},{2,1},{3,0},{4,7},{5,6},{6,5},{7,4},{8,11},{9,10},{10,... | collective-permute-start | bytes 98312 | tf_op jit(solution)/shard_map/ppermute | solution.py:126
  13.0 6.2 %collective-permute-start.4 = (bf16[512,128]{1,0:T(8,128)(2,1)S(1)}, bf16[512,128]{1,0:T(8,128)(2,1)S(1)}, u32[]{:S(2)}, u32[]{:S(2)}) collective-permute-start(bf16[512,128]{1,0:T(8,128)(2,1)S(1)} %get-tuple-element.71.refs_0_), channel_id=1, source_target_pairs={{0,8},{4,12},{8,0},{12,4},{16,24},{20,28},{24,16},{28,20},{1,9},{5... | collective-permute-start | bytes 393224 | tf_op jit(solution)/shard_map/ppermute | solution.py:126
  14.6 5.8 %collective-permute-start.6 = (bf16[512,128]{1,0:T(8,128)(2,1)S(1)}, bf16[512,128]{1,0:T(8,128)(2,1)S(1)}, u32[]{:S(2)}, u32[]{:S(2)}) collective-permute-start(bf16[512,128]{1,0:T(8,128)(2,1)S(1)} %get-tuple-element.71.refs_0_), channel_id=1, source_target_pairs={{0,16},{4,20},{8,24},{12,28},{16,0},{20,4},{24,8},{28,12},{1,17},{... | collective-permute-start | bytes 393224 | tf_op jit(solution)/shard_map/ppermute | solution.py:126
  16.1 5.9 %collective-permute-start.8 = (bf16[512,128]{1,0:T(8,128)(2,1)S(1)}, bf16[512,128]{1,0:T(8,128)(2,1)S(1)}, u32[]{:S(2)}, u32[]{:S(2)}) collective-permute-start(bf16[512,128]{1,0:T(8,128)(2,1)S(1)} %get-tuple-element.71.refs_0_), channel_id=1, source_target_pairs={{0,24},{4,28},{8,16},{12,20},{16,8},{20,12},{24,0},{28,4},{1,25},{... | collective-permute-start | bytes 393224 | tf_op jit(solution)/shard_map/ppermute | solution.py:126
  19.1 2.8 %collective-permute-start.3 = (bf16[512,128]{1,0:T(8,128)(2,1)S(1)}, bf16[512,128]{1,0:T(8,128)(2,1)S(1)}, u32[]{:S(2)}, u32[]{:S(2)}) collective-permute-start(bf16[512,128]{1,0:T(8,128)(2,1)S(1)} %get-tuple-element.71.refs_0_), channel_id=1, source_target_pairs={{0,4},{4,0},{8,12},{12,8},{16,20},{20,16},{24,28},{28,24},{1,5},{5... | collective-permute-start | bytes 393224 | tf_op jit(solution)/shard_map/ppermute | solution.py:126
  19.2 2.7 %collective-permute-start.5 = (bf16[512,128]{1,0:T(8,128)(2,1)S(1)}, bf16[512,128]{1,0:T(8,128)(2,1)S(1)}, u32[]{:S(2)}, u32[]{:S(2)}) collective-permute-start(bf16[512,128]{1,0:T(8,128)(2,1)S(1)} %collective-permute-done.4.refs_2_), channel_id=1, source_target_pairs={{0,4},{4,0},{8,12},{12,8},{16,20},{20,16},{24,28},{28,24},{1,5},{5... | collective-permute-start | bytes 393224 | tf_op jit(solution)/shard_map/ppermute | solution.py:126
  20.3 1.7 %collective-permute-start.7 = (bf16[512,128]{1,0:T(8,128)(2,1)S(1)}, bf16[512,128]{1,0:T(8,128)(2,1)S(1)}, u32[]{:S(2)}, u32[]{:S(2)}) collective-permute-start(bf16[512,128]{1,0:T(8,128)(2,1)S(1)} %collective-permute-done.6.refs_4_), channel_id=1, source_target_pairs={{0,4},{4,0},{8,12},{12,8},{16,20},{20,16},{24,28},{28,24},{1,5},{5... | collective-permute-start | bytes 393224 | tf_op jit(solution)/shard_map/ppermute | solution.py:126
  22.0 1.3 collective-permute-start.9
  23.6 8.8 %copy-start = (bf16[1,8,512,512]{3,2,1,0:T(8,128)(2,1)S(1)}, bf16[1,8,512,512]{3,2,1,0:T(8,128)(2,1)}, u32[]{:S(2)}) copy-start(bf16[1,8,512,512]{3,2,1,0:T(8,128)(2,1)} %activity_ref.3) | copy-start | bytes 12582916
  23.6 8.8 %copy-start.2 = (f32[8,256]{1,0:T(8,128)S(1)}, f32[8,256]{1,0:T(8,128)}, u32[]{:S(2)}) copy-start(f32[8,256]{1,0:T(8,128)} %time_ref.7) | copy-start | bytes 24580
  23.6 5.2 %collective-permute-start.10 = (bf16[256,128]{1,0:T(8,128)(2,1)S(1)}, bf16[256,128]{1,0:T(8,128)(2,1)S(1)}, u32[]{:S(2)}, u32[]{:S(2)}) collective-permute-start(bf16[256,128]{1,0:T(8,128)(2,1)S(1)} %get-tuple-element.73), channel_id=1, source_target_pairs={{0,1},{1,0},{2,3},{3,2},{4,5},{5,4},{6,7},{7,6},{8,9},{9,8},{10,11... | collective-permute-start | bytes 196616 | tf_op jit(solution)/shard_map/ppermute | solution.py:126
  23.7 8.5 %collective-permute-start.11 = (bf16[256,128]{1,0:T(8,128)(2,1)S(1)}, bf16[256,128]{1,0:T(8,128)(2,1)S(1)}, u32[]{:S(2)}, u32[]{:S(2)}) collective-permute-start(bf16[256,128]{1,0:T(8,128)(2,1)S(1)} %get-tuple-element.74), channel_id=1, source_target_pairs={{0,2},{1,3},{2,0},{3,1},{4,6},{5,7},{6,4},{7,5},{8,10},{9,11},{10,... | collective-permute-start | bytes 196616 | tf_op jit(solution)/shard_map/ppermute | solution.py:126
  24.6 14.1 %copy-start.6 = (f32[512,64]{0,1:T(8,128)S(1)}, f32[512,64]{0,1:T(8,128)}, u32[]{:S(2)}) copy-start(f32[512,64]{0,1:T(8,128)} %param.17) | copy-start | bytes 393220
  24.6 14.1 %copy-start.7 = (f32[512,64]{0,1:T(8,128)S(1)}, f32[512,64]{0,1:T(8,128)}, u32[]{:S(2)}) copy-start(f32[512,64]{0,1:T(8,128)} %param.16) | copy-start | bytes 393220
  24.6 14.1 %copy-start.8 = (f32[512,64]{0,1:T(8,128)S(1)}, f32[512,64]{0,1:T(8,128)}, u32[]{:S(2)}) copy-start(f32[512,64]{0,1:T(8,128)} %param.13) | copy-start | bytes 393220
  24.6 7.8 %collective-permute-start.12 = (bf16[256,128]{1,0:T(8,128)(2,1)S(1)}, bf16[256,128]{1,0:T(8,128)(2,1)S(1)}, u32[]{:S(2)}, u32[]{:S(2)}) collective-permute-start(bf16[256,128]{1,0:T(8,128)(2,1)S(1)} %get-tuple-element.75), channel_id=1, source_target_pairs={{0,3},{1,2},{2,1},{3,0},{4,7},{5,6},{6,5},{7,4},{8,11},{9,10},{10,... | collective-permute-start | bytes 196616 | tf_op jit(solution)/shard_map/ppermute | solution.py:126
  28.6 9.8 %collective-permute-start.26 = (f32[128,256]{1,0:T(8,128)S(1)}, f32[128,256]{1,0:T(8,128)S(1)}, u32[]{:S(2)}, u32[]{:S(2)}) collective-permute-start(f32[128,256]{1,0:T(8,128)S(1)} %shard_map.128), channel_id=1, source_target_pairs={{0,1},{1,0},{2,3},{3,2},{4,5},{5,4},{6,7},{7,6},{8,9},{9,8},{10,11... | collective-permute-start | bytes 393224 | tf_op jit(solution)/shard_map/ppermute | solution.py:126
  33.9 7.9 %collective-permute-start.13 = (f32[256,128]{1,0:T(8,128)S(1)}, f32[256,128]{1,0:T(8,128)S(1)}, u32[]{:S(2)}, u32[]{:S(2)}) collective-permute-start(f32[256,128]{1,0:T(8,128)S(1)} %get-tuple-element.77), channel_id=1, source_target_pairs={{0,1},{1,0},{2,3},{3,2},{4,5},{5,4},{6,7},{7,6},{8,9},{9,8},{10,11... | collective-permute-start | bytes 393224 | tf_op jit(solution)/shard_map/ppermute | solution.py:126
  35.2 16.5 %collective-permute-start.14 = (f32[256,128]{1,0:T(8,128)S(1)}, f32[256,128]{1,0:T(8,128)S(1)}, u32[]{:S(2)}, u32[]{:S(2)}) collective-permute-start(f32[256,128]{1,0:T(8,128)S(1)} %get-tuple-element.78), channel_id=1, source_target_pairs={{0,2},{1,3},{2,0},{3,1},{4,6},{5,7},{6,4},{7,5},{8,10},{9,11},{10,... | collective-permute-start | bytes 393224 | tf_op jit(solution)/shard_map/ppermute | solution.py:126
  37.0 14.6 %collective-permute-start.15 = (f32[256,128]{1,0:T(8,128)S(1)}, f32[256,128]{1,0:T(8,128)S(1)}, u32[]{:S(2)}, u32[]{:S(2)}) collective-permute-start(f32[256,128]{1,0:T(8,128)S(1)} %get-tuple-element.79), channel_id=1, source_target_pairs={{0,3},{1,2},{2,1},{3,0},{4,7},{5,6},{6,5},{7,4},{8,11},{9,10},{10,... | collective-permute-start | bytes 393224 | tf_op jit(solution)/shard_map/ppermute | solution.py:126
  38.4 18.8 %collective-permute-start.27 = (f32[128,256]{1,0:T(8,128)S(1)}, f32[128,256]{1,0:T(8,128)S(1)}, u32[]{:S(2)}, u32[]{:S(2)}) collective-permute-start(f32[128,256]{1,0:T(8,128)S(1)} %add.33), channel_id=1, source_target_pairs={{0,2},{1,3},{2,0},{3,1},{4,6},{5,7},{6,4},{7,5},{8,10},{9,11},{10,... | collective-permute-start | bytes 393224 | tf_op jit(solution)/shard_map/ppermute | solution.py:126
  38.9 18.3 %collective-permute-start.23 = (f32[192,128]{1,0:T(8,128)S(1)}, f32[192,128]{1,0:T(8,128)S(1)}, u32[]{:S(2)}, u32[]{:S(2)}) collective-permute-start(f32[192,128]{1,0:T(8,128)S(1)} %get-tuple-element.90), channel_id=1, source_target_pairs={{0,1},{1,0},{2,3},{3,2},{4,5},{5,4},{6,7},{7,6},{8,9},{9,8},{10,11... | collective-permute-start | bytes 294920 | tf_op jit(solution)/shard_map/ppermute | solution.py:126
  41.8 16.4 %collective-permute-start.24 = (f32[192,128]{1,0:T(8,128)S(1)}, f32[192,128]{1,0:T(8,128)S(1)}, u32[]{:S(2)}, u32[]{:S(2)}) collective-permute-start(f32[192,128]{1,0:T(8,128)S(1)} %get-tuple-element.91), channel_id=1, source_target_pairs={{0,2},{1,3},{2,0},{3,1},{4,6},{5,7},{6,4},{7,5},{8,10},{9,11},{10,... | collective-permute-start | bytes 294920 | tf_op jit(solution)/shard_map/ppermute | solution.py:126
  52.0 12.7 %collective-permute-start.21 = (f32[256,128]{1,0:T(8,128)S(1)}, f32[256,128]{1,0:T(8,128)S(1)}, u32[]{:S(2)}, u32[]{:S(2)}) collective-permute-start(f32[256,128]{1,0:T(8,128)S(1)} %get-tuple-element.87), channel_id=1, source_target_pairs={{0,4},{4,0},{8,12},{12,8},{16,20},{20,16},{24,28},{28,24},{1,5},{5... | collective-permute-start | bytes 393224 | tf_op jit(solution)/shard_map/ppermute | solution.py:126
  52.1 13.3 %collective-permute-start.19 = (f32[256,128]{1,0:T(8,128)S(1)}, f32[256,128]{1,0:T(8,128)S(1)}, u32[]{:S(2)}, u32[]{:S(2)}) collective-permute-start(f32[256,128]{1,0:T(8,128)S(1)} %get-tuple-element.85), channel_id=1, source_target_pairs={{0,4},{4,0},{8,12},{12,8},{16,20},{20,16},{24,28},{28,24},{1,5},{5... | collective-permute-start | bytes 393224 | tf_op jit(solution)/shard_map/ppermute | solution.py:126
  57.2 9.5 %collective-permute-start.17 = (f32[256,128]{1,0:T(8,128)S(1)}, f32[256,128]{1,0:T(8,128)S(1)}, u32[]{:S(2)}, u32[]{:S(2)}) collective-permute-start(f32[256,128]{1,0:T(8,128)S(1)} %get-tuple-element.83), channel_id=1, source_target_pairs={{0,4},{4,0},{8,12},{12,8},{16,20},{20,16},{24,28},{28,24},{1,5},{5... | collective-permute-start | bytes 393224 | tf_op jit(solution)/shard_map/ppermute | solution.py:126
  57.2 11.3 %collective-permute-start.28 = (f32[128,256]{1,0:T(8,128)S(1)}, f32[128,256]{1,0:T(8,128)S(1)}, u32[]{:S(2)}, u32[]{:S(2)}) collective-permute-start(f32[128,256]{1,0:T(8,128)S(1)} %add.34.refs_0_), channel_id=1, source_target_pairs={{0,4},{4,0},{8,12},{12,8},{16,20},{20,16},{24,28},{28,24},{1,5},{5... | collective-permute-start | bytes 393224 | tf_op jit(solution)/shard_map/ppermute | solution.py:126
  58.2 6.4 %collective-permute-start.25 = (f32[192,128]{1,0:T(8,128)S(1)}, f32[192,128]{1,0:T(8,128)S(1)}, u32[]{:S(2)}, u32[]{:S(2)}) collective-permute-start(f32[192,128]{1,0:T(8,128)S(1)} %get-tuple-element.92), channel_id=1, source_target_pairs={{0,3},{1,2},{2,1},{3,0},{4,7},{5,6},{6,5},{7,4},{8,11},{9,10},{10,... | collective-permute-start | bytes 294920 | tf_op jit(solution)/shard_map/ppermute | solution.py:126
  64.7 13.0 %collective-permute-start.16 = (f32[256,128]{1,0:T(8,128)S(1)}, f32[256,128]{1,0:T(8,128)S(1)}, u32[]{:S(2)}, u32[]{:S(2)}) collective-permute-start(f32[256,128]{1,0:T(8,128)S(1)} %get-tuple-element.81), channel_id=1, source_target_pairs={{0,4},{4,0},{8,12},{12,8},{16,20},{20,16},{24,28},{28,24},{1,5},{5... | collective-permute-start | bytes 393224 | tf_op jit(solution)/shard_map/ppermute | solution.py:126
  64.8 12.9 %collective-permute-start.22 = (f32[256,128]{1,0:T(8,128)S(1)}, f32[256,128]{1,0:T(8,128)S(1)}, u32[]{:S(2)}, u32[]{:S(2)}) collective-permute-start(f32[256,128]{1,0:T(8,128)S(1)} %add.32), channel_id=1, source_target_pairs={{0,8},{4,12},{8,0},{12,4},{16,24},{20,28},{24,16},{28,20},{1,9},{5... | collective-permute-start | bytes 393224 | tf_op jit(solution)/shard_map/ppermute | solution.py:126
  65.5 12.3 %collective-permute-start.20 = (f32[256,128]{1,0:T(8,128)S(1)}, f32[256,128]{1,0:T(8,128)S(1)}, u32[]{:S(2)}, u32[]{:S(2)}) collective-permute-start(f32[256,128]{1,0:T(8,128)S(1)} %add.31), channel_id=1, source_target_pairs={{0,16},{4,20},{8,24},{12,28},{16,0},{20,4},{24,8},{28,12},{1,17},{... | collective-permute-start | bytes 393224 | tf_op jit(solution)/shard_map/ppermute | solution.py:126
  66.7 11.1 %collective-permute-start.18 = (f32[256,128]{1,0:T(8,128)S(1)}, f32[256,128]{1,0:T(8,128)S(1)}, u32[]{:S(2)}, u32[]{:S(2)}) collective-permute-start(f32[256,128]{1,0:T(8,128)S(1)} %add.30), channel_id=1, source_target_pairs={{0,24},{4,28},{8,16},{12,20},{16,8},{20,12},{24,0},{28,4},{1,25},{... | collective-permute-start | bytes 393224 | tf_op jit(solution)/shard_map/ppermute | solution.py:126
  78.9 6.4 %collective-permute-start.33 = (bf16[512,128]{1,0:T(8,128)(2,1)S(1)}, bf16[512,128]{1,0:T(8,128)(2,1)S(1)}, u32[]{:S(2)}, u32[]{:S(2)}) collective-permute-start(bf16[512,128]{1,0:T(8,128)(2,1)S(1)} %get-tuple-element.102.refs_0_), channel_id=1, source_target_pairs={{0,8},{4,12},{8,0},{12,4},{16,24},{20,28},{24,16},{28,20},{1,9},{5... | collective-permute-start | bytes 393224 | tf_op jit(solution)/shard_map/ppermute | solution.py:126
  79.6 5.8 %collective-permute-start.35 = (bf16[512,128]{1,0:T(8,128)(2,1)S(1)}, bf16[512,128]{1,0:T(8,128)(2,1)S(1)}, u32[]{:S(2)}, u32[]{:S(2)}) collective-permute-start(bf16[512,128]{1,0:T(8,128)(2,1)S(1)} %get-tuple-element.102.refs_0_), channel_id=1, source_target_pairs={{0,16},{4,20},{8,24},{12,28},{16,0},{20,4},{24,8},{28,12},{1,17},{... | collective-permute-start | bytes 393224 | tf_op jit(solution)/shard_map/ppermute | solution.py:126
  80.7 7.2 %collective-permute-start.37 = (bf16[512,128]{1,0:T(8,128)(2,1)S(1)}, bf16[512,128]{1,0:T(8,128)(2,1)S(1)}, u32[]{:S(2)}, u32[]{:S(2)}) collective-permute-start(bf16[512,128]{1,0:T(8,128)(2,1)S(1)} %get-tuple-element.102.refs_0_), channel_id=1, source_target_pairs={{0,24},{4,28},{8,16},{12,20},{16,8},{20,12},{24,0},{28,4},{1,25},{... | collective-permute-start | bytes 393224 | tf_op jit(solution)/shard_map/ppermute | solution.py:126
  82.5 5.5 %collective-permute-start.32 = (bf16[512,128]{1,0:T(8,128)(2,1)S(1)}, bf16[512,128]{1,0:T(8,128)(2,1)S(1)}, u32[]{:S(2)}, u32[]{:S(2)}) collective-permute-start(bf16[512,128]{1,0:T(8,128)(2,1)S(1)} %get-tuple-element.102.refs_0_), channel_id=1, source_target_pairs={{0,4},{4,0},{8,12},{12,8},{16,20},{20,16},{24,28},{28,24},{1,5},{5... | collective-permute-start | bytes 393224 | tf_op jit(solution)/shard_map/ppermute | solution.py:126
  85.4 2.6 %collective-permute-start.34 = (bf16[512,128]{1,0:T(8,128)(2,1)S(1)}, bf16[512,128]{1,0:T(8,128)(2,1)S(1)}, u32[]{:S(2)}, u32[]{:S(2)}) collective-permute-start(bf16[512,128]{1,0:T(8,128)(2,1)S(1)} %collective-permute-done.33.refs_2_), channel_id=1, source_target_pairs={{0,4},{4,0},{8,12},{12,8},{16,20},{20,16},{24,28},{28,24},{1,5},{5... | collective-permute-start | bytes 393224 | tf_op jit(solution)/shard_map/ppermute | solution.py:126
  85.4 2.6 %collective-permute-start.36 = (bf16[512,128]{1,0:T(8,128)(2,1)S(1)}, bf16[512,128]{1,0:T(8,128)(2,1)S(1)}, u32[]{:S(2)}, u32[]{:S(2)}) collective-permute-start(bf16[512,128]{1,0:T(8,128)(2,1)S(1)} %collective-permute-done.35.refs_4_), channel_id=1, source_target_pairs={{0,4},{4,0},{8,12},{12,8},{16,20},{20,16},{24,28},{28,24},{1,5},{5... | collective-permute-start | bytes 393224 | tf_op jit(solution)/shard_map/ppermute | solution.py:126
  87.9 1.3 collective-permute-start.38
  89.6 5.3 %collective-permute-start.39 = (bf16[256,128]{1,0:T(8,128)(2,1)S(1)}, bf16[256,128]{1,0:T(8,128)(2,1)S(1)}, u32[]{:S(2)}, u32[]{:S(2)}) collective-permute-start(bf16[256,128]{1,0:T(8,128)(2,1)S(1)} %get-tuple-element.104), channel_id=1, source_target_pairs={{0,1},{1,0},{2,3},{3,2},{4,5},{5,4},{6,7},{7,6},{8,9},{9,8},{10,11... | collective-permute-start | bytes 196616 | tf_op jit(solution)/shard_map/ppermute | solution.py:126
  89.6 8.5 %collective-permute-start.40 = (bf16[256,128]{1,0:T(8,128)(2,1)S(1)}, bf16[256,128]{1,0:T(8,128)(2,1)S(1)}, u32[]{:S(2)}, u32[]{:S(2)}) collective-permute-start(bf16[256,128]{1,0:T(8,128)(2,1)S(1)} %get-tuple-element.105), channel_id=1, source_target_pairs={{0,2},{1,3},{2,0},{3,1},{4,6},{5,7},{6,4},{7,5},{8,10},{9,11},{10,... | collective-permute-start | bytes 196616 | tf_op jit(solution)/shard_map/ppermute | solution.py:126
  91.6 6.8 %collective-permute-start.41 = (bf16[256,128]{1,0:T(8,128)(2,1)S(1)}, bf16[256,128]{1,0:T(8,128)(2,1)S(1)}, u32[]{:S(2)}, u32[]{:S(2)}) collective-permute-start(bf16[256,128]{1,0:T(8,128)(2,1)S(1)} %get-tuple-element.106), channel_id=1, source_target_pairs={{0,3},{1,2},{2,1},{3,0},{4,7},{5,6},{6,5},{7,4},{8,11},{9,10},{10,... | collective-permute-start | bytes 196616 | tf_op jit(solution)/shard_map/ppermute | solution.py:126
  94.6 9.8 %collective-permute-start.52 = (f32[128,256]{1,0:T(8,128)S(1)}, f32[128,256]{1,0:T(8,128)S(1)}, u32[]{:S(2)}, u32[]{:S(2)}) collective-permute-start(f32[128,256]{1,0:T(8,128)S(1)} %shard_map.136), channel_id=1, source_target_pairs={{0,1},{1,0},{2,3},{3,2},{4,5},{5,4},{6,7},{7,6},{8,9},{9,8},{10,11... | collective-permute-start | bytes 393224 | tf_op jit(solution)/shard_map/ppermute | solution.py:126
  99.9 6.2 %collective-permute-start.42 = (f32[256,128]{1,0:T(8,128)S(1)}, f32[256,128]{1,0:T(8,128)S(1)}, u32[]{:S(2)}, u32[]{:S(2)}) collective-permute-start(f32[256,128]{1,0:T(8,128)S(1)} %get-tuple-element.108), channel_id=1, source_target_pairs={{0,1},{1,0},{2,3},{3,2},{4,5},{5,4},{6,7},{7,6},{8,9},{9,8},{10,11... | collective-permute-start | bytes 393224 | tf_op jit(solution)/shard_map/ppermute | solution.py:126
  101.1 14.7 %collective-permute-start.43 = (f32[256,128]{1,0:T(8,128)S(1)}, f32[256,128]{1,0:T(8,128)S(1)}, u32[]{:S(2)}, u32[]{:S(2)}) collective-permute-start(f32[256,128]{1,0:T(8,128)S(1)} %get-tuple-element.109), channel_id=1, source_target_pairs={{0,2},{1,3},{2,0},{3,1},{4,6},{5,7},{6,4},{7,5},{8,10},{9,11},{10,... | collective-permute-start | bytes 393224 | tf_op jit(solution)/shard_map/ppermute | solution.py:126
  103.0 12.9 %collective-permute-start.44 = (f32[256,128]{1,0:T(8,128)S(1)}, f32[256,128]{1,0:T(8,128)S(1)}, u32[]{:S(2)}, u32[]{:S(2)}) collective-permute-start(f32[256,128]{1,0:T(8,128)S(1)} %get-tuple-element.110), channel_id=1, source_target_pairs={{0,3},{1,2},{2,1},{3,0},{4,7},{5,6},{6,5},{7,4},{8,11},{9,10},{10,... | collective-permute-start | bytes 393224 | tf_op jit(solution)/shard_map/ppermute | solution.py:126
  104.3 15.6 %collective-permute-start.53 = (f32[128,256]{1,0:T(8,128)S(1)}, f32[128,256]{1,0:T(8,128)S(1)}, u32[]{:S(2)}, u32[]{:S(2)}) collective-permute-start(f32[128,256]{1,0:T(8,128)S(1)} %add.38), channel_id=1, source_target_pairs={{0,2},{1,3},{2,0},{3,1},{4,6},{5,7},{6,4},{7,5},{8,10},{9,11},{10,... | collective-permute-start | bytes 393224 | tf_op jit(solution)/shard_map/ppermute | solution.py:126
  116.3 4.4 %collective-permute-start.50 = (f32[256,128]{1,0:T(8,128)S(1)}, f32[256,128]{1,0:T(8,128)S(1)}, u32[]{:S(2)}, u32[]{:S(2)}) collective-permute-start(f32[256,128]{1,0:T(8,128)S(1)} %get-tuple-element.118), channel_id=1, source_target_pairs={{0,4},{4,0},{8,12},{12,8},{16,20},{20,16},{24,28},{28,24},{1,5},{5... | collective-permute-start | bytes 393224 | tf_op jit(solution)/shard_map/ppermute | solution.py:126
  116.3 4.4 %collective-permute-start.48 = (f32[256,128]{1,0:T(8,128)S(1)}, f32[256,128]{1,0:T(8,128)S(1)}, u32[]{:S(2)}, u32[]{:S(2)}) collective-permute-start(f32[256,128]{1,0:T(8,128)S(1)} %get-tuple-element.116), channel_id=1, source_target_pairs={{0,4},{4,0},{8,12},{12,8},{16,20},{20,16},{24,28},{28,24},{1,5},{5... | collective-permute-start | bytes 393224 | tf_op jit(solution)/shard_map/ppermute | solution.py:126
  116.8 5.7 %collective-permute-start.46 = (f32[256,128]{1,0:T(8,128)S(1)}, f32[256,128]{1,0:T(8,128)S(1)}, u32[]{:S(2)}, u32[]{:S(2)}) collective-permute-start(f32[256,128]{1,0:T(8,128)S(1)} %get-tuple-element.114), channel_id=1, source_target_pairs={{0,4},{4,0},{8,12},{12,8},{16,20},{20,16},{24,28},{28,24},{1,5},{5... | collective-permute-start | bytes 393224 | tf_op jit(solution)/shard_map/ppermute | solution.py:126
  120.0 4.2 %collective-permute-start.54 = (f32[128,256]{1,0:T(8,128)S(1)}, f32[128,256]{1,0:T(8,128)S(1)}, u32[]{:S(2)}, u32[]{:S(2)}) collective-permute-start(f32[128,256]{1,0:T(8,128)S(1)} %add.39.refs_0_), channel_id=1, source_target_pairs={{0,4},{4,0},{8,12},{12,8},{16,20},{20,16},{24,28},{28,24},{1,5},{5... | collective-permute-start | bytes 393224 | tf_op jit(solution)/shard_map/ppermute | solution.py:126
  120.1 21.4 %collective-permute-start.29 = (f32[64,128]{1,0:T(8,128)S(1)}, f32[64,128]{1,0:T(8,128)S(1)}, u32[]{:S(2)}, u32[]{:S(2)}) collective-permute-start(f32[64,128]{1,0:T(8,128)S(1)} %get-tuple-element.98), channel_id=1, source_target_pairs={{0,1},{1,0},{2,3},{3,2},{4,5},{5,4},{6,7},{7,6},{8,9},{9,8},{10,11... | collective-permute-start | bytes 98312 | tf_op jit(solution)/shard_map/ppermute | solution.py:126
  120.7 13.0 %collective-permute-start.45 = (f32[256,128]{1,0:T(8,128)S(1)}, f32[256,128]{1,0:T(8,128)S(1)}, u32[]{:S(2)}, u32[]{:S(2)}) collective-permute-start(f32[256,128]{1,0:T(8,128)S(1)} %get-tuple-element.112), channel_id=1, source_target_pairs={{0,4},{4,0},{8,12},{12,8},{16,20},{20,16},{24,28},{28,24},{1,5},{5... | collective-permute-start | bytes 393224 | tf_op jit(solution)/shard_map/ppermute | solution.py:126
  120.7 15.1 %collective-permute-start.51 = (f32[256,128]{1,0:T(8,128)S(1)}, f32[256,128]{1,0:T(8,128)S(1)}, u32[]{:S(2)}, u32[]{:S(2)}) collective-permute-start(f32[256,128]{1,0:T(8,128)S(1)} %add.37), channel_id=1, source_target_pairs={{0,8},{4,12},{8,0},{12,4},{16,24},{20,28},{24,16},{28,20},{1,9},{5... | collective-permute-start | bytes 393224 | tf_op jit(solution)/shard_map/ppermute | solution.py:126
  122.6 15.1 %collective-permute-start.49 = (f32[256,128]{1,0:T(8,128)S(1)}, f32[256,128]{1,0:T(8,128)S(1)}, u32[]{:S(2)}, u32[]{:S(2)}) collective-permute-start(f32[256,128]{1,0:T(8,128)S(1)} %add.36), channel_id=1, source_target_pairs={{0,16},{4,20},{8,24},{12,28},{16,0},{20,4},{24,8},{28,12},{1,17},{... | collective-permute-start | bytes 393224 | tf_op jit(solution)/shard_map/ppermute | solution.py:126
  124.2 13.5 %collective-permute-start.47 = (f32[256,128]{1,0:T(8,128)S(1)}, f32[256,128]{1,0:T(8,128)S(1)}, u32[]{:S(2)}, u32[]{:S(2)}) collective-permute-start(f32[256,128]{1,0:T(8,128)S(1)} %add.35), channel_id=1, source_target_pairs={{0,24},{4,28},{8,16},{12,20},{16,8},{20,12},{24,0},{28,4},{1,25},{... | collective-permute-start | bytes 393224 | tf_op jit(solution)/shard_map/ppermute | solution.py:126
  133.7 9.7 %collective-permute-start.30 = (f32[64,128]{1,0:T(8,128)S(1)}, f32[64,128]{1,0:T(8,128)S(1)}, u32[]{:S(2)}, u32[]{:S(2)}) collective-permute-start(f32[64,128]{1,0:T(8,128)S(1)} %get-tuple-element.99), channel_id=1, source_target_pairs={{0,2},{1,3},{2,0},{3,1},{4,6},{5,7},{6,4},{7,5},{8,10},{9,11},{10,... | collective-permute-start | bytes 98312 | tf_op jit(solution)/shard_map/ppermute | solution.py:126
  135.9 7.5 %collective-permute-start.31 = (f32[64,128]{1,0:T(8,128)S(1)}, f32[64,128]{1,0:T(8,128)S(1)}, u32[]{:S(2)}, u32[]{:S(2)}) collective-permute-start(f32[64,128]{1,0:T(8,128)S(1)} %get-tuple-element.100), channel_id=1, source_target_pairs={{0,3},{1,2},{2,1},{3,0},{4,7},{5,6},{6,5},{7,4},{8,11},{9,10},{10,... | collective-permute-start | bytes 98312 | tf_op jit(solution)/shard_map/ppermute | solution.py:126
  138.9 5.2 %collective-permute-start.55 = (f32[64,128]{1,0:T(8,128)S(1)}, f32[64,128]{1,0:T(8,128)S(1)}, u32[]{:S(2)}, u32[]{:S(2)}) collective-permute-start(f32[64,128]{1,0:T(8,128)S(1)} %get-tuple-element.124), channel_id=1, source_target_pairs={{0,1},{1,0},{2,3},{3,2},{4,5},{5,4},{6,7},{7,6},{8,9},{9,8},{10,11... | collective-permute-start | bytes 98312 | tf_op jit(solution)/shard_map/ppermute | solution.py:126
  139.0 5.1 %collective-permute-start.56 = (f32[64,128]{1,0:T(8,128)S(1)}, f32[64,128]{1,0:T(8,128)S(1)}, u32[]{:S(2)}, u32[]{:S(2)}) collective-permute-start(f32[64,128]{1,0:T(8,128)S(1)} %get-tuple-element.125), channel_id=1, source_target_pairs={{0,2},{1,3},{2,0},{3,1},{4,6},{5,7},{6,4},{7,5},{8,10},{9,11},{10,... | collective-permute-start | bytes 98312 | tf_op jit(solution)/shard_map/ppermute | solution.py:126
  141.5 5.7 %collective-permute-start.57 = (f32[64,128]{1,0:T(8,128)S(1)}, f32[64,128]{1,0:T(8,128)S(1)}, u32[]{:S(2)}, u32[]{:S(2)}) collective-permute-start(f32[64,128]{1,0:T(8,128)S(1)} %get-tuple-element.126), channel_id=1, source_target_pairs={{0,3},{1,2},{2,1},{3,0},{4,7},{5,6},{6,5},{7,4},{8,11},{9,10},{10,... | collective-permute-start | bytes 98312 | tf_op jit(solution)/shard_map/ppermute | solution.py:126
  (3 other events, 2.0 us)

commit v4 on v3

--- a/solution.py
+++ b/solution.py
@@ -68,9 +68,12 @@
     pieces, (work_ref, penalty_ref) = refs[:-2], refs[-2:]
     rank = work_ref.shape[0]
     half = rank // 2
-    for r, piece in enumerate(pieces):
-        start = (lax.axis_index("wide") % 2 ^ r) * half
-        work_ref[pl.ds(pl.multiple_of(start, half), half), :] = piece[...]
+    mine, other = (piece[...] for piece in pieces)
+    first = jnp.broadcast_to(lax.axis_index("wide") % 2 == 0, mine.shape)
+    quadrants = unpack(jnp.where(first, mine, other), jnp.where(first, other, mine))
+    for k, quadrant in enumerate(quadrants):
+        row, col = k // 2 * half, k % 2 * half
+        work_ref[row : row + half, col : col + half] = quadrant
     time = time_ref[...]
     times = lax.dot_general(
         time, time, (((0,), (0,)), ((), ())), precision=HIGHEST, preferred_element_type=jnp.float32
@@ -205,9 +208,49 @@
     outputs[2][...] = factor_ref[...] + outputs[3][...]
 
 
+def pack(core, rows):
+    half = rows.shape[0]
+    part = half // 2
+    left = lax.broadcasted_iota(jnp.int32, (1, half), 1) < part
+    own = rows[:, core * half : (core + 1) * half]
+    other = rows[:, (1 - core) * half : (2 - core) * half]
+    first, second = (other[:part], other[part:]) if core == 0 else (other[part:], other[:part])
+    turned = pltpu.roll(second[part // 2 :], part, 1)
+    return jnp.concatenate(
+        [
+            own[:part],
+            jnp.where(left, first, own[part:]),
+            jnp.where(left, turned, second[: part // 2]),
+        ]
+    )
+
+
+def unpack(a, b):
+    half = a.shape[1]
+    part = half // 2
+    left = lax.broadcasted_iota(jnp.int32, (1, half), 1) < part
+
+    def last(x):
+        return jnp.concatenate([x[half:], pltpu.roll(x[half:], part, 1)])
+
+    a_turned, b_turned = a[:half].T, b[:half].T
+    b_last = last(b)
+    b_last_turned = jnp.concatenate([b_last, b_last]).T
+    upper_left = jnp.concatenate([a[:part], a_turned[part:]])
+    lower_right = jnp.concatenate([b[:part], b_turned[part:]])
+    upper_right = jnp.concatenate(
+        [
+            jnp.where(left, a[part:half], b_turned[:part]),
+            jnp.where(left, b_last_turned[part:], last(a)),
+        ]
+    )
+    return upper_left, upper_right, upper_right.T, lower_right
+
+
 def gram_kernel(*refs):
-    pairs, (half_ref, rows_ref) = refs[:-2], refs[-2:]
-    half, rank = half_ref.shape
+    pairs, (packed_ref, rows_ref) = refs[:-2], refs[-2:]
+    rank = rows_ref.shape[0] // 2
+    half = rank // 2
     width = pairs[0].shape[1]
     for k, pair in enumerate(pairs):
         rows_ref[:, k * width : (k + 1) * width] = pair[...]
@@ -218,13 +261,18 @@
     )
     rounded = products[:half, :rank]
     mixed = products[:half, rank:] + products[half:, :rank]
-    half_ref[...] = rounded + (mixed + products[half:, rank:])
+    gram = rounded + (mixed + products[half:, rank:])
+    for core in range(2):
+
+        @pl.when(lax.axis_index("wide") % 2 == core)
+        def _(core=core):
+            packed_ref[...] = pack(core, gram)
 
 
 def joint_gram(pairs):
     rank, width = pairs[0].shape[0] // 2, pairs[0].shape[1]
     (total,) = kernel_call(
-        gram_kernel, [shape((rank // 2, rank))], *pairs,
+        gram_kernel, [shape((rank // 2 + rank // 8, rank // 2))], *pairs,
         scratch=[pltpu.VMEM((2 * rank, len(pairs) * width), jnp.bfloat16)],
         flops=1_500_000_000,
     )

time: 148 us -> 142 us (0.959)
  waiting for transfers between devices: 59.7 us -> 43.5 us
  starting transfers between devices: 55.6 us -> 65 us
    ppermute x58, waiting for transfers between devices: 59.7 us -> 43.5 us  [swap(): return lax.ppermute(x, axis, [(i, i ^ mask) for i in range(size)])]
    ppermute x58, starting transfers between devices: 55.6 us -> 65 us  [swap(): return lax.ppermute(x, axis, [(i, i ^ mask) for i in range(size)])]
  transfers between devices with their start and end apart: 58 -> 58, of which waited for: 21 -> 18; matrix products, arithmetic and copies ran while one was open for 0% -> 0% of each run, Pallas kernels for 18% -> 18%
where the time goes in v4:
time: 142 us; the launch traced here: 141 us
  starting transfers between devices  65 us (46%)
  waiting for transfers between devices  43.5 us (31%)
  Pallas kernels  28.7 us (20%)
  local copies, waits for them, and re-layouts  2.92 us (2%)
    ppermute x58, starting transfers between devices, swap(): return lax.ppermute(x, axis, [(i, i ^ mask) for i in range(size)])  65 us
    ppermute x58, waiting for transfers between devices, swap(): return lax.ppermute(x, axis, [(i, i ^ mask) for i in range(size)])  43.5 us
    pallas_call x21, Pallas kernels, kernel_call(): pl.pallas_call(kernel, out_shape=tuple(out_shape), in_specs=[spec] * len(...  28.7 us
    unnamed x18, local copies, waits for them, and re-layouts  2.92 us
  transfers between devices with their start and end apart: 58, of which 18 were waited for; matrix products, arithmetic and copies ran while one was open for 0% of the time, Pallas kernels for 18%

profile of v4, /device:TPU:0, one launch (start us, length us, event | category | flops | bytes accessed | tf_op | source)
XLA Modules:
  0.0 141.4 jit_solution(13065410394793736063)
XLA Ops:
  0.6 0.9 copy-done.1
  1.6 3.1 %collective-permute-start = (f32[64,128]{1,0:T(8,128)S(1)}, f32[64,128]{1,0:T(8,128)S(1)}, u32[]{:S(2)}, u32[]{:S(2)}) collective-permute-start(f32[64,128]{1,0:T(8,128)S(1)} %get-tuple-element.68), channel_id=1, source_target_pairs={{0,1},{1,0},{2,3},{3,2},{4,5},{5,4},{6,7},{7,6},{8,9},{9,8},{10,11... | collective-permute-start | bytes 98312 | tf_op jit(solution)/shard_map/ppermute | solution.py:129
  4.7 2.6 %collective-permute-start.1 = (f32[64,128]{1,0:T(8,128)S(1)}, f32[64,128]{1,0:T(8,128)S(1)}, u32[]{:S(2)}, u32[]{:S(2)}) collective-permute-start(f32[64,128]{1,0:T(8,128)S(1)} %get-tuple-element.69), channel_id=1, source_target_pairs={{0,2},{1,3},{2,0},{3,1},{4,6},{5,7},{6,4},{7,5},{8,10},{9,11},{10,... | collective-permute-start | bytes 98312 | tf_op jit(solution)/shard_map/ppermute | solution.py:129
  7.3 2.8 %collective-permute-done.1.refs_2_ = f32[64,128]{1,0:T(8,128)S(1)} collective-permute-done((f32[64,128]{1,0:T(8,128)S(1)}, f32[64,128]{1,0:T(8,128)S(1)}, u32[]{:S(2)}, u32[]{:S(2)}) %collective-permute-start.1) | collective-permute-done | bytes 32800 | tf_op jit(solution)/shard_map/ppermute | solution.py:129
  10.1 2.9 %collective-permute-done.2.refs_3_ = f32[64,128]{1,0:T(8,128)S(1)} collective-permute-done((f32[64,128]{1,0:T(8,128)S(1)}, f32[64,128]{1,0:T(8,128)S(1)}, u32[]{:S(2)}, u32[]{:S(2)}) %collective-permute-start.2) | collective-permute-done | bytes 32800 | tf_op jit(solution)/shard_map/ppermute | solution.py:129
  13.0 1.6 %collective-permute-start.4 = (bf16[512,128]{1,0:T(8,128)(2,1)S(1)}, bf16[512,128]{1,0:T(8,128)(2,1)S(1)}, u32[]{:S(2)}, u32[]{:S(2)}) collective-permute-start(bf16[512,128]{1,0:T(8,128)(2,1)S(1)} %get-tuple-element.71.refs_0_), channel_id=1, source_target_pairs={{0,8},{4,12},{8,0},{12,4},{16,24},{20,28},{24,16},{28,20},{1,9},{5... | collective-permute-start | bytes 393224 | tf_op jit(solution)/shard_map/ppermute | solution.py:129
  14.6 1.5 %collective-permute-start.6 = (bf16[512,128]{1,0:T(8,128)(2,1)S(1)}, bf16[512,128]{1,0:T(8,128)(2,1)S(1)}, u32[]{:S(2)}, u32[]{:S(2)}) collective-permute-start(bf16[512,128]{1,0:T(8,128)(2,1)S(1)} %get-tuple-element.71.refs_0_), channel_id=1, source_target_pairs={{0,16},{4,20},{8,24},{12,28},{16,0},{20,4},{24,8},{28,12},{1,17},{... | collective-permute-start | bytes 393224 | tf_op jit(solution)/shard_map/ppermute | solution.py:129
  16.6 0.7 copy-done.3
  17.2 0.7 copy-done.4
  17.9 0.7 copy-done.5
  18.6 0.6 shard_map.120
  19.7 0.6 collective-permute-done.6.refs_4_
  20.3 1.6 %collective-permute-done.8.refs_6_ = bf16[512,128]{1,0:T(8,128)(2,1)S(1)} collective-permute-done((bf16[512,128]{1,0:T(8,128)(2,1)S(1)}, bf16[512,128]{1,0:T(8,128)(2,1)S(1)}, u32[]{:S(2)}, u32[]{:S(2)}) %collective-permute-start.8) | collective-permute-done | bytes 131104 | tf_op jit(solution)/shard_map/ppermute | solution.py:129
  22.0 1.3 collective-permute-done.9.refs_7_
  23.3 0.6 shard_map.128
  24.3 2.0 %collective-permute-start.10 = (bf16[256,128]{1,0:T(8,128)(2,1)S(1)}, bf16[256,128]{1,0:T(8,128)(2,1)S(1)}, u32[]{:S(2)}, u32[]{:S(2)}) collective-permute-start(bf16[256,128]{1,0:T(8,128)(2,1)S(1)} %get-tuple-element.73), channel_id=1, source_target_pairs={{0,1},{1,0},{2,3},{3,2},{4,5},{5,4},{6,7},{7,6},{8,9},{9,8},{10,11... | collective-permute-start | bytes 196616 | tf_op jit(solution)/shard_map/ppermute | solution.py:129
  26.3 2.4 %collective-permute-start.12 = (bf16[256,128]{1,0:T(8,128)(2,1)S(1)}, bf16[256,128]{1,0:T(8,128)(2,1)S(1)}, u32[]{:S(2)}, u32[]{:S(2)}) collective-permute-start(bf16[256,128]{1,0:T(8,128)(2,1)S(1)} %get-tuple-element.75), channel_id=1, source_target_pairs={{0,3},{1,2},{2,1},{3,0},{4,7},{5,6},{6,5},{7,4},{8,11},{9,10},{10,... | collective-permute-start | bytes 196616 | tf_op jit(solution)/shard_map/ppermute | solution.py:129
  28.8 1.1 collective-permute-start.23
  30.0 0.9 collective-permute-start.24
  30.9 2.1 %collective-permute-start.27 = (f32[160,128]{1,0:T(8,128)S(1)}, f32[160,128]{1,0:T(8,128)S(1)}, u32[]{:S(2)}, u32[]{:S(2)}) collective-permute-start(f32[160,128]{1,0:T(8,128)S(1)} %add.33), channel_id=1, source_target_pairs={{0,2},{1,3},{2,0},{3,1},{4,6},{5,7},{6,4},{7,5},{8,10},{9,11},{10,... | collective-permute-start | bytes 245768 | tf_op jit(solution)/shard_map/ppermute | solution.py:129
  33.0 0.9 collective-permute-done.11.refs_2_
  33.9 1.5 %shard_map.124 = (f32[256,128]{1,0:T(8,128)S(1)}, f32[256,128]{1,0:T(8,128)S(1)}, f32[256,128]{1,0:T(8,128)S(1)}, f32[256,128]{1,0:T(8,128)S(1)}) custom-call(bf16[1,8,512,512]{3,2,1,0:T(8,128)(2,1)S(1)} %copy-done, f32[8,256]{1,0:T(8,128)S(1)} %copy-done.2, bf16[256,128]{1,0:T(8,128)(2,1)S(1)} %get-tuple-element.72.refs_0_, ...), custom_call_target="tpu_custom_call" | custom-call | flops 1073741824 | bytes 4988928 | tf_op jit(solution)/shard_map/pallas_call | solution.py:112
  35.4 5.9 %collective-permute-start.13 = (f32[256,128]{1,0:T(8,128)S(1)}, f32[256,128]{1,0:T(8,128)S(1)}, u32[]{:S(2)}, u32[]{:S(2)}) collective-permute-start(f32[256,128]{1,0:T(8,128)S(1)} %get-tuple-element.77), channel_id=1, source_target_pairs={{0,1},{1,0},{2,3},{3,2},{4,5},{5,4},{6,7},{7,6},{8,9},{9,8},{10,11... | collective-permute-start | bytes 393224 | tf_op jit(solution)/shard_map/ppermute | solution.py:129
  41.3 2.4 %collective-permute-start.15 = (f32[256,128]{1,0:T(8,128)S(1)}, f32[256,128]{1,0:T(8,128)S(1)}, u32[]{:S(2)}, u32[]{:S(2)}) collective-permute-start(f32[256,128]{1,0:T(8,128)S(1)} %get-tuple-element.79), channel_id=1, source_target_pairs={{0,3},{1,2},{2,1},{3,0},{4,7},{5,6},{6,5},{7,4},{8,11},{9,10},{10,... | collective-permute-start | bytes 393224 | tf_op jit(solution)/shard_map/ppermute | solution.py:129
  43.7 4.9 %collective-permute-done.27 = f32[160,128]{1,0:T(8,128)S(1)} collective-permute-done((f32[160,128]{1,0:T(8,128)S(1)}, f32[160,128]{1,0:T(8,128)S(1)}, u32[]{:S(2)}, u32[]{:S(2)}) %collective-permute-start.27) | collective-permute-done | bytes 81952 | tf_op jit(solution)/shard_map/ppermute | solution.py:129
  48.8 6.4 %collective-permute-done.25.refs_4_ = f32[192,128]{1,0:T(8,128)S(1)} collective-permute-done((f32[192,128]{1,0:T(8,128)S(1)}, f32[192,128]{1,0:T(8,128)S(1)}, u32[]{:S(2)}, u32[]{:S(2)}) %collective-permute-start.25) | collective-permute-done | bytes 98336 | tf_op jit(solution)/shard_map/ppermute | solution.py:129
  56.8 5.0 %shard_map.129 = (f32[256,256]{1,0:T(8,128)S(1)}, f32[1,128]{1,0:T(1,128)S(1)}) custom-call(f32[8,256]{1,0:T(8,128)S(1)} %copy-done.2, f32[160,128]{1,0:T(8,128)S(1)} %add.34.refs_0_, f32[160,128]{1,0:T(8,128)S(1)} %collective-permute-done.28.refs_1_), custom_call_target="tpu_custom_call" | custom-call | flops 6000000000 | bytes 434688 | tf_op jit(solution)/shard_map/pallas_call | solution.py:112
  61.8 0.6 collective-permute-start.22
  62.9 2.6 %collective-permute-start.18 = (f32[256,128]{1,0:T(8,128)S(1)}, f32[256,128]{1,0:T(8,128)S(1)}, u32[]{:S(2)}, u32[]{:S(2)}) collective-permute-start(f32[256,128]{1,0:T(8,128)S(1)} %add.30), channel_id=1, source_target_pairs={{0,24},{4,28},{8,16},{12,20},{16,8},{20,12},{24,0},{28,4},{1,25},{... | collective-permute-start | bytes 393224 | tf_op jit(solution)/shard_map/ppermute | solution.py:129
  65.5 4.2 %shard_map.130.refs_8_ = f32[256,256]{1,0:T(8,128)S(1)} custom-call(f32[256,256]{1,0:T(8,128)S(1)} %get-tuple-element.96.half_ref), custom_call_target="tpu_custom_call" | custom-call | flops 6000000000 | bytes 524288 | tf_op jit(solution)/shard_map/pallas_call | solution.py:112
  69.8 0.7 collective-permute-done.18.refs_2_
  70.5 1.2 shard_map.131
  71.7 1.6 %collective-permute-start.33 = (bf16[512,128]{1,0:T(8,128)(2,1)S(1)}, bf16[512,128]{1,0:T(8,128)(2,1)S(1)}, u32[]{:S(2)}, u32[]{:S(2)}) collective-permute-start(bf16[512,128]{1,0:T(8,128)(2,1)S(1)} %get-tuple-element.102.refs_0_), channel_id=1, source_target_pairs={{0,8},{4,12},{8,0},{12,4},{16,24},{20,28},{24,16},{28,20},{1,9},{5... | collective-permute-start | bytes 393224 | tf_op jit(solution)/shard_map/ppermute | solution.py:129
  73.2 0.9 collective-permute-start.35
  74.1 1.1 collective-permute-start.37
  75.2 2.5 %collective-permute-done.33.refs_2_ = bf16[512,128]{1,0:T(8,128)(2,1)S(1)} collective-permute-done((bf16[512,128]{1,0:T(8,128)(2,1)S(1)}, bf16[512,128]{1,0:T(8,128)(2,1)S(1)}, u32[]{:S(2)}, u32[]{:S(2)}) %collective-permute-start.33) | collective-permute-done | bytes 131104 | tf_op jit(solution)/shard_map/ppermute | solution.py:129
  77.7 2.5 %collective-permute-done.35.refs_4_ = bf16[512,128]{1,0:T(8,128)(2,1)S(1)} collective-permute-done((bf16[512,128]{1,0:T(8,128)(2,1)S(1)}, bf16[512,128]{1,0:T(8,128)(2,1)S(1)}, u32[]{:S(2)}, u32[]{:S(2)}) %collective-permute-start.35) | collective-permute-done | bytes 131104 | tf_op jit(solution)/shard_map/ppermute | solution.py:129
  80.2 0.5 collective-permute-start.38
  80.7 0.8 collective-permute-done.36.refs_5_
  81.7 0.7 shard_map.136
  82.5 5.0 %collective-permute-start.52 = (f32[160,128]{1,0:T(8,128)S(1)}, f32[160,128]{1,0:T(8,128)S(1)}, u32[]{:S(2)}, u32[]{:S(2)}) collective-permute-start(f32[160,128]{1,0:T(8,128)S(1)} %shard_map.136), channel_id=1, source_target_pairs={{0,1},{1,0},{2,3},{3,2},{4,5},{5,4},{6,7},{7,6},{8,9},{9,8},{10,11... | collective-permute-start | bytes 245768 | tf_op jit(solution)/shard_map/ppermute | solution.py:129
  87.8 1.1 collective-permute-start.40
  89.0 3.2 %collective-permute-start.41 = (bf16[256,128]{1,0:T(8,128)(2,1)S(1)}, bf16[256,128]{1,0:T(8,128)(2,1)S(1)}, u32[]{:S(2)}, u32[]{:S(2)}) collective-permute-start(bf16[256,128]{1,0:T(8,128)(2,1)S(1)} %get-tuple-element.106), channel_id=1, source_target_pairs={{0,3},{1,2},{2,1},{3,0},{4,7},{5,6},{6,5},{7,4},{8,11},{9,10},{10,... | collective-permute-start | bytes 196616 | tf_op jit(solution)/shard_map/ppermute | solution.py:129
  92.3 0.6 collective-permute-done.39.refs_1_
  92.9 5.4 %collective-permute-done.40.refs_2_ = bf16[256,128]{1,0:T(8,128)(2,1)S(1)} collective-permute-done((bf16[256,128]{1,0:T(8,128)(2,1)S(1)}, bf16[256,128]{1,0:T(8,128)(2,1)S(1)}, u32[]{:S(2)}, u32[]{:S(2)}) %collective-permute-start.40) | collective-permute-done | bytes 65568 | tf_op jit(solution)/shard_map/ppermute | solution.py:129
  98.3 1.5 %shard_map.134 = (f32[256,128]{1,0:T(8,128)S(1)}, f32[256,128]{1,0:T(8,128)S(1)}, f32[256,128]{1,0:T(8,128)S(1)}, f32[256,128]{1,0:T(8,128)S(1)}) custom-call(bf16[1,8,512,512]{3,2,1,0:T(8,128)(2,1)S(1)} %copy-done, f32[8,256]{1,0:T(8,128)S(1)} %copy-done.2, bf16[256,128]{1,0:T(8,128)(2,1)S(1)} %get-tuple-element.103.refs_0_, ...), custom_call_target="tpu_custom_call" | custom-call | flops 1073741824 | bytes 4988928 | tf_op jit(solution)/shard_map/pallas_call | solution.py:112
  99.9 2.0 %collective-permute-start.42 = (f32[256,128]{1,0:T(8,128)S(1)}, f32[256,128]{1,0:T(8,128)S(1)}, u32[]{:S(2)}, u32[]{:S(2)}) collective-permute-start(f32[256,128]{1,0:T(8,128)S(1)} %get-tuple-element.108), channel_id=1, source_target_pairs={{0,1},{1,0},{2,3},{3,2},{4,5},{5,4},{6,7},{7,6},{8,9},{9,8},{10,11... | collective-permute-start | bytes 393224 | tf_op jit(solution)/shard_map/ppermute | solution.py:129
  101.9 2.4 %collective-permute-start.44 = (f32[256,128]{1,0:T(8,128)S(1)}, f32[256,128]{1,0:T(8,128)S(1)}, u32[]{:S(2)}, u32[]{:S(2)}) collective-permute-start(f32[256,128]{1,0:T(8,128)S(1)} %get-tuple-element.110), channel_id=1, source_target_pairs={{0,3},{1,2},{2,1},{3,0},{4,7},{5,6},{6,5},{7,4},{8,11},{9,10},{10,... | collective-permute-start | bytes 393224 | tf_op jit(solution)/shard_map/ppermute | solution.py:129
  104.4 1.1 collective-permute-start.29
  105.5 2.2 %collective-permute-done.42.refs_1_ = f32[256,128]{1,0:T(8,128)S(1)} collective-permute-done((f32[256,128]{1,0:T(8,128)S(1)}, f32[256,128]{1,0:T(8,128)S(1)}, u32[]{:S(2)}, u32[]{:S(2)}) %collective-permute-start.42) | collective-permute-done | bytes 131104 | tf_op jit(solution)/shard_map/ppermute | solution.py:129
  107.7 4.5 %collective-permute-done.43.refs_2_ = f32[256,128]{1,0:T(8,128)S(1)} collective-permute-done((f32[256,128]{1,0:T(8,128)S(1)}, f32[256,128]{1,0:T(8,128)S(1)}, u32[]{:S(2)}, u32[]{:S(2)}) %collective-permute-start.43) | collective-permute-done | bytes 131104 | tf_op jit(solution)/shard_map/ppermute | solution.py:129
  113.7 5.0 %shard_map.137 = (f32[256,256]{1,0:T(8,128)S(1)}, f32[1,128]{1,0:T(1,128)S(1)}) custom-call(f32[8,256]{1,0:T(8,128)S(1)} %copy-done.2, f32[160,128]{1,0:T(8,128)S(1)} %add.39.refs_0_, f32[160,128]{1,0:T(8,128)S(1)} %collective-permute-done.54.refs_1_), custom_call_target="tpu_custom_call" | custom-call | flops 6000000000 | bytes 434688 | tf_op jit(solution)/shard_map/pallas_call | solution.py:112
  118.8 0.9 collective-permute-start.51
  119.7 1.2 collective-permute-start.49
  120.9 1.5 %collective-permute-start.47 = (f32[256,128]{1,0:T(8,128)S(1)}, f32[256,128]{1,0:T(8,128)S(1)}, u32[]{:S(2)}, u32[]{:S(2)}) collective-permute-start(f32[256,128]{1,0:T(8,128)S(1)} %add.35), channel_id=1, source_target_pairs={{0,24},{4,28},{8,16},{12,20},{16,8},{20,12},{24,0},{28,4},{1,25},{... | collective-permute-start | bytes 393224 | tf_op jit(solution)/shard_map/ppermute | solution.py:129
  122.5 4.2 %shard_map.138.refs_8_ = f32[256,256]{1,0:T(8,128)S(1)} custom-call(f32[256,256]{1,0:T(8,128)S(1)} %get-tuple-element.122.half_ref), custom_call_target="tpu_custom_call" | custom-call | flops 6000000000 | bytes 524288 | tf_op jit(solution)/shard_map/pallas_call | solution.py:112
  126.7 2.5 %collective-permute-start.30 = (f32[64,128]{1,0:T(8,128)S(1)}, f32[64,128]{1,0:T(8,128)S(1)}, u32[]{:S(2)}, u32[]{:S(2)}) collective-permute-start(f32[64,128]{1,0:T(8,128)S(1)} %get-tuple-element.99), channel_id=1, source_target_pairs={{0,2},{1,3},{2,0},{3,1},{4,6},{5,7},{6,4},{7,5},{8,10},{9,11},{10,... | collective-permute-start | bytes 98312 | tf_op jit(solution)/shard_map/ppermute | solution.py:129
  129.3 2.5 %collective-permute-start.31 = (f32[64,128]{1,0:T(8,128)S(1)}, f32[64,128]{1,0:T(8,128)S(1)}, u32[]{:S(2)}, u32[]{:S(2)}) collective-permute-start(f32[64,128]{1,0:T(8,128)S(1)} %get-tuple-element.100), channel_id=1, source_target_pairs={{0,3},{1,2},{2,1},{3,0},{4,7},{5,6},{6,5},{7,4},{8,11},{9,10},{10,... | collective-permute-start | bytes 98312 | tf_op jit(solution)/shard_map/ppermute | solution.py:129
  131.8 1.2 shard_map.139
  133.0 1.9 %collective-permute-start.56 = (f32[64,128]{1,0:T(8,128)S(1)}, f32[64,128]{1,0:T(8,128)S(1)}, u32[]{:S(2)}, u32[]{:S(2)}) collective-permute-start(f32[64,128]{1,0:T(8,128)S(1)} %get-tuple-element.125), channel_id=1, source_target_pairs={{0,2},{1,3},{2,0},{3,1},{4,6},{5,7},{6,4},{7,5},{8,10},{9,11},{10,... | collective-permute-start | bytes 98312 | tf_op jit(solution)/shard_map/ppermute | solution.py:129
  134.9 2.5 %collective-permute-start.57 = (f32[64,128]{1,0:T(8,128)S(1)}, f32[64,128]{1,0:T(8,128)S(1)}, u32[]{:S(2)}, u32[]{:S(2)}) collective-permute-start(f32[64,128]{1,0:T(8,128)S(1)} %get-tuple-element.126), channel_id=1, source_target_pairs={{0,3},{1,2},{2,1},{3,0},{4,7},{5,6},{6,5},{7,4},{8,11},{9,10},{10,... | collective-permute-start | bytes 98312 | tf_op jit(solution)/shard_map/ppermute | solution.py:129
  137.4 0.7 shard_map.132
  138.1 2.5 %collective-permute-done.57.refs_3_ = f32[64,128]{1,0:T(8,128)S(1)} collective-permute-done((f32[64,128]{1,0:T(8,128)S(1)}, f32[64,128]{1,0:T(8,128)S(1)}, u32[]{:S(2)}, u32[]{:S(2)}) %collective-permute-start.57) | collective-permute-done | bytes 32800 | tf_op jit(solution)/shard_map/ppermute | solution.py:129
  140.6 0.7 shard_map.140
  (103 shorter events, 6.0 us)
Async XLA Ops:
  0.6 0.9 copy-start.1
  1.6 5.7 %collective-permute-start = (f32[64,128]{1,0:T(8,128)S(1)}, f32[64,128]{1,0:T(8,128)S(1)}, u32[]{:S(2)}, u32[]{:S(2)}) collective-permute-start(f32[64,128]{1,0:T(8,128)S(1)} %get-tuple-element.68), channel_id=1, source_target_pairs={{0,1},{1,0},{2,3},{3,2},{4,5},{5,4},{6,7},{7,6},{8,9},{9,8},{10,11... | collective-permute-start | bytes 98312 | tf_op jit(solution)/shard_map/ppermute | solution.py:129
  4.7 5.4 %collective-permute-start.1 = (f32[64,128]{1,0:T(8,128)S(1)}, f32[64,128]{1,0:T(8,128)S(1)}, u32[]{:S(2)}, u32[]{:S(2)}) collective-permute-start(f32[64,128]{1,0:T(8,128)S(1)} %get-tuple-element.69), channel_id=1, source_target_pairs={{0,2},{1,3},{2,0},{3,1},{4,6},{5,7},{6,4},{7,5},{8,10},{9,11},{10,... | collective-permute-start | bytes 98312 | tf_op jit(solution)/shard_map/ppermute | solution.py:129
  7.3 5.7 %collective-permute-start.2 = (f32[64,128]{1,0:T(8,128)S(1)}, f32[64,128]{1,0:T(8,128)S(1)}, u32[]{:S(2)}, u32[]{:S(2)}) collective-permute-start(f32[64,128]{1,0:T(8,128)S(1)} %get-tuple-element.70), channel_id=1, source_target_pairs={{0,3},{1,2},{2,1},{3,0},{4,7},{5,6},{6,5},{7,4},{8,11},{9,10},{10,... | collective-permute-start | bytes 98312 | tf_op jit(solution)/shard_map/ppermute | solution.py:129
  13.0 6.2 %collective-permute-start.4 = (bf16[512,128]{1,0:T(8,128)(2,1)S(1)}, bf16[512,128]{1,0:T(8,128)(2,1)S(1)}, u32[]{:S(2)}, u32[]{:S(2)}) collective-permute-start(bf16[512,128]{1,0:T(8,128)(2,1)S(1)} %get-tuple-element.71.refs_0_), channel_id=1, source_target_pairs={{0,8},{4,12},{8,0},{12,4},{16,24},{20,28},{24,16},{28,20},{1,9},{5... | collective-permute-start | bytes 393224 | tf_op jit(solution)/shard_map/ppermute | solution.py:129
  14.6 5.8 %collective-permute-start.6 = (bf16[512,128]{1,0:T(8,128)(2,1)S(1)}, bf16[512,128]{1,0:T(8,128)(2,1)S(1)}, u32[]{:S(2)}, u32[]{:S(2)}) collective-permute-start(bf16[512,128]{1,0:T(8,128)(2,1)S(1)} %get-tuple-element.71.refs_0_), channel_id=1, source_target_pairs={{0,16},{4,20},{8,24},{12,28},{16,0},{20,4},{24,8},{28,12},{1,17},{... | collective-permute-start | bytes 393224 | tf_op jit(solution)/shard_map/ppermute | solution.py:129
  16.1 5.9 %collective-permute-start.8 = (bf16[512,128]{1,0:T(8,128)(2,1)S(1)}, bf16[512,128]{1,0:T(8,128)(2,1)S(1)}, u32[]{:S(2)}, u32[]{:S(2)}) collective-permute-start(bf16[512,128]{1,0:T(8,128)(2,1)S(1)} %get-tuple-element.71.refs_0_), channel_id=1, source_target_pairs={{0,24},{4,28},{8,16},{12,20},{16,8},{20,12},{24,0},{28,4},{1,25},{... | collective-permute-start | bytes 393224 | tf_op jit(solution)/shard_map/ppermute | solution.py:129
  19.1 2.8 %collective-permute-start.3 = (bf16[512,128]{1,0:T(8,128)(2,1)S(1)}, bf16[512,128]{1,0:T(8,128)(2,1)S(1)}, u32[]{:S(2)}, u32[]{:S(2)}) collective-permute-start(bf16[512,128]{1,0:T(8,128)(2,1)S(1)} %get-tuple-element.71.refs_0_), channel_id=1, source_target_pairs={{0,4},{4,0},{8,12},{12,8},{16,20},{20,16},{24,28},{28,24},{1,5},{5... | collective-permute-start | bytes 393224 | tf_op jit(solution)/shard_map/ppermute | solution.py:129
  19.2 2.7 %collective-permute-start.5 = (bf16[512,128]{1,0:T(8,128)(2,1)S(1)}, bf16[512,128]{1,0:T(8,128)(2,1)S(1)}, u32[]{:S(2)}, u32[]{:S(2)}) collective-permute-start(bf16[512,128]{1,0:T(8,128)(2,1)S(1)} %collective-permute-done.4.refs_2_), channel_id=1, source_target_pairs={{0,4},{4,0},{8,12},{12,8},{16,20},{20,16},{24,28},{28,24},{1,5},{5... | collective-permute-start | bytes 393224 | tf_op jit(solution)/shard_map/ppermute | solution.py:129
  20.3 1.7 %collective-permute-start.7 = (bf16[512,128]{1,0:T(8,128)(2,1)S(1)}, bf16[512,128]{1,0:T(8,128)(2,1)S(1)}, u32[]{:S(2)}, u32[]{:S(2)}) collective-permute-start(bf16[512,128]{1,0:T(8,128)(2,1)S(1)} %collective-permute-done.6.refs_4_), channel_id=1, source_target_pairs={{0,4},{4,0},{8,12},{12,8},{16,20},{20,16},{24,28},{28,24},{1,5},{5... | collective-permute-start | bytes 393224 | tf_op jit(solution)/shard_map/ppermute | solution.py:129
  22.0 1.3 collective-permute-start.9
  23.9 6.0 %collective-permute-start.26 = (f32[160,128]{1,0:T(8,128)S(1)}, f32[160,128]{1,0:T(8,128)S(1)}, u32[]{:S(2)}, u32[]{:S(2)}) collective-permute-start(f32[160,128]{1,0:T(8,128)S(1)} %shard_map.128), channel_id=1, source_target_pairs={{0,1},{1,0},{2,3},{3,2},{4,5},{5,4},{6,7},{7,6},{8,9},{9,8},{10,11... | collective-permute-start | bytes 245768 | tf_op jit(solution)/shard_map/ppermute | solution.py:129
  23.9 4.8 %copy-start.6 = (f32[512,64]{0,1:T(8,128)S(1)}, f32[512,64]{0,1:T(8,128)}, u32[]{:S(2)}) copy-start(f32[512,64]{0,1:T(8,128)} %param.17) | copy-start | bytes 393220
  24.0 4.8 %copy-start.7 = (f32[512,64]{0,1:T(8,128)S(1)}, f32[512,64]{0,1:T(8,128)}, u32[]{:S(2)}) copy-start(f32[512,64]{0,1:T(8,128)} %param.16) | copy-start | bytes 393220
  24.0 4.8 %copy-start.8 = (f32[512,64]{0,1:T(8,128)S(1)}, f32[512,64]{0,1:T(8,128)}, u32[]{:S(2)}) copy-start(f32[512,64]{0,1:T(8,128)} %param.13) | copy-start | bytes 393220
  24.0 9.9 %copy-start = (bf16[1,8,512,512]{3,2,1,0:T(8,128)(2,1)S(1)}, bf16[1,8,512,512]{3,2,1,0:T(8,128)(2,1)}, u32[]{:S(2)}) copy-start(bf16[1,8,512,512]{3,2,1,0:T(8,128)(2,1)} %activity_ref.3) | copy-start | bytes 12582916
  24.0 9.9 %copy-start.2 = (f32[8,256]{1,0:T(8,128)S(1)}, f32[8,256]{1,0:T(8,128)}, u32[]{:S(2)}) copy-start(f32[8,256]{1,0:T(8,128)} %time_ref.7) | copy-start | bytes 24580
  24.3 6.6 %collective-permute-start.10 = (bf16[256,128]{1,0:T(8,128)(2,1)S(1)}, bf16[256,128]{1,0:T(8,128)(2,1)S(1)}, u32[]{:S(2)}, u32[]{:S(2)}) collective-permute-start(bf16[256,128]{1,0:T(8,128)(2,1)S(1)} %get-tuple-element.73), channel_id=1, source_target_pairs={{0,1},{1,0},{2,3},{3,2},{4,5},{5,4},{6,7},{7,6},{8,9},{9,8},{10,11... | collective-permute-start | bytes 196616 | tf_op jit(solution)/shard_map/ppermute | solution.py:129
  26.3 7.6 %collective-permute-start.11 = (bf16[256,128]{1,0:T(8,128)(2,1)S(1)}, bf16[256,128]{1,0:T(8,128)(2,1)S(1)}, u32[]{:S(2)}, u32[]{:S(2)}) collective-permute-start(bf16[256,128]{1,0:T(8,128)(2,1)S(1)} %get-tuple-element.74), channel_id=1, source_target_pairs={{0,2},{1,3},{2,0},{3,1},{4,6},{5,7},{6,4},{7,5},{8,10},{9,11},{10,... | collective-permute-start | bytes 196616 | tf_op jit(solution)/shard_map/ppermute | solution.py:129
  26.3 7.6 %collective-permute-start.12 = (bf16[256,128]{1,0:T(8,128)(2,1)S(1)}, bf16[256,128]{1,0:T(8,128)(2,1)S(1)}, u32[]{:S(2)}, u32[]{:S(2)}) collective-permute-start(bf16[256,128]{1,0:T(8,128)(2,1)S(1)} %get-tuple-element.75), channel_id=1, source_target_pairs={{0,3},{1,2},{2,1},{3,0},{4,7},{5,6},{6,5},{7,4},{8,11},{9,10},{10,... | collective-permute-start | bytes 196616 | tf_op jit(solution)/shard_map/ppermute | solution.py:129
  28.8 12.5 %collective-permute-start.23 = (f32[192,128]{1,0:T(8,128)S(1)}, f32[192,128]{1,0:T(8,128)S(1)}, u32[]{:S(2)}, u32[]{:S(2)}) collective-permute-start(f32[192,128]{1,0:T(8,128)S(1)} %get-tuple-element.90), channel_id=1, source_target_pairs={{0,1},{1,0},{2,3},{3,2},{4,5},{5,4},{6,7},{7,6},{8,9},{9,8},{10,11... | collective-permute-start | bytes 294920 | tf_op jit(solution)/shard_map/ppermute | solution.py:129
  30.0 18.7 %collective-permute-start.24 = (f32[192,128]{1,0:T(8,128)S(1)}, f32[192,128]{1,0:T(8,128)S(1)}, u32[]{:S(2)}, u32[]{:S(2)}) collective-permute-start(f32[192,128]{1,0:T(8,128)S(1)} %get-tuple-element.91), channel_id=1, source_target_pairs={{0,2},{1,3},{2,0},{3,1},{4,6},{5,7},{6,4},{7,5},{8,10},{9,11},{10,... | collective-permute-start | bytes 294920 | tf_op jit(solution)/shard_map/ppermute | solution.py:129
  30.9 17.8 %collective-permute-start.27 = (f32[160,128]{1,0:T(8,128)S(1)}, f32[160,128]{1,0:T(8,128)S(1)}, u32[]{:S(2)}, u32[]{:S(2)}) collective-permute-start(f32[160,128]{1,0:T(8,128)S(1)} %add.33), channel_id=1, source_target_pairs={{0,2},{1,3},{2,0},{3,1},{4,6},{5,7},{6,4},{7,5},{8,10},{9,11},{10,... | collective-permute-start | bytes 245768 | tf_op jit(solution)/shard_map/ppermute | solution.py:129
  35.4 19.8 %collective-permute-start.13 = (f32[256,128]{1,0:T(8,128)S(1)}, f32[256,128]{1,0:T(8,128)S(1)}, u32[]{:S(2)}, u32[]{:S(2)}) collective-permute-start(f32[256,128]{1,0:T(8,128)S(1)} %get-tuple-element.77), channel_id=1, source_target_pairs={{0,1},{1,0},{2,3},{3,2},{4,5},{5,4},{6,7},{7,6},{8,9},{9,8},{10,11... | collective-permute-start | bytes 393224 | tf_op jit(solution)/shard_map/ppermute | solution.py:129
  41.3 14.0 %collective-permute-start.14 = (f32[256,128]{1,0:T(8,128)S(1)}, f32[256,128]{1,0:T(8,128)S(1)}, u32[]{:S(2)}, u32[]{:S(2)}) collective-permute-start(f32[256,128]{1,0:T(8,128)S(1)} %get-tuple-element.78), channel_id=1, source_target_pairs={{0,2},{1,3},{2,0},{3,1},{4,6},{5,7},{6,4},{7,5},{8,10},{9,11},{10,... | collective-permute-start | bytes 393224 | tf_op jit(solution)/shard_map/ppermute | solution.py:129
  41.3 14.0 %collective-permute-start.15 = (f32[256,128]{1,0:T(8,128)S(1)}, f32[256,128]{1,0:T(8,128)S(1)}, u32[]{:S(2)}, u32[]{:S(2)}) collective-permute-start(f32[256,128]{1,0:T(8,128)S(1)} %get-tuple-element.79), channel_id=1, source_target_pairs={{0,3},{1,2},{2,1},{3,0},{4,7},{5,6},{6,5},{7,4},{8,11},{9,10},{10,... | collective-permute-start | bytes 393224 | tf_op jit(solution)/shard_map/ppermute | solution.py:129
  48.7 6.5 %collective-permute-start.25 = (f32[192,128]{1,0:T(8,128)S(1)}, f32[192,128]{1,0:T(8,128)S(1)}, u32[]{:S(2)}, u32[]{:S(2)}) collective-permute-start(f32[192,128]{1,0:T(8,128)S(1)} %get-tuple-element.92), channel_id=1, source_target_pairs={{0,3},{1,2},{2,1},{3,0},{4,7},{5,6},{6,5},{7,4},{8,11},{9,10},{10,... | collective-permute-start | bytes 294920 | tf_op jit(solution)/shard_map/ppermute | solution.py:129
  48.7 8.1 %collective-permute-start.28 = (f32[160,128]{1,0:T(8,128)S(1)}, f32[160,128]{1,0:T(8,128)S(1)}, u32[]{:S(2)}, u32[]{:S(2)}) collective-permute-start(f32[160,128]{1,0:T(8,128)S(1)} %add.34.refs_0_), channel_id=1, source_target_pairs={{0,4},{4,0},{8,12},{12,8},{16,20},{20,16},{24,28},{28,24},{1,5},{5... | collective-permute-start | bytes 245768 | tf_op jit(solution)/shard_map/ppermute | solution.py:129
  55.7 6.1 %collective-permute-start.21 = (f32[256,128]{1,0:T(8,128)S(1)}, f32[256,128]{1,0:T(8,128)S(1)}, u32[]{:S(2)}, u32[]{:S(2)}) collective-permute-start(f32[256,128]{1,0:T(8,128)S(1)} %get-tuple-element.87), channel_id=1, source_target_pairs={{0,4},{4,0},{8,12},{12,8},{16,20},{20,16},{24,28},{28,24},{1,5},{5... | collective-permute-start | bytes 393224 | tf_op jit(solution)/shard_map/ppermute | solution.py:129
  55.7 6.7 %collective-permute-start.19 = (f32[256,128]{1,0:T(8,128)S(1)}, f32[256,128]{1,0:T(8,128)S(1)}, u32[]{:S(2)}, u32[]{:S(2)}) collective-permute-start(f32[256,128]{1,0:T(8,128)S(1)} %get-tuple-element.85), channel_id=1, source_target_pairs={{0,4},{4,0},{8,12},{12,8},{16,20},{20,16},{24,28},{28,24},{1,5},{5... | collective-permute-start | bytes 393224 | tf_op jit(solution)/shard_map/ppermute | solution.py:129
  56.2 6.7 %collective-permute-start.17 = (f32[256,128]{1,0:T(8,128)S(1)}, f32[256,128]{1,0:T(8,128)S(1)}, u32[]{:S(2)}, u32[]{:S(2)}) collective-permute-start(f32[256,128]{1,0:T(8,128)S(1)} %get-tuple-element.83), channel_id=1, source_target_pairs={{0,4},{4,0},{8,12},{12,8},{16,20},{20,16},{24,28},{28,24},{1,5},{5... | collective-permute-start | bytes 393224 | tf_op jit(solution)/shard_map/ppermute | solution.py:129
  56.3 13.4 %collective-permute-start.16 = (f32[256,128]{1,0:T(8,128)S(1)}, f32[256,128]{1,0:T(8,128)S(1)}, u32[]{:S(2)}, u32[]{:S(2)}) collective-permute-start(f32[256,128]{1,0:T(8,128)S(1)} %get-tuple-element.81), channel_id=1, source_target_pairs={{0,4},{4,0},{8,12},{12,8},{16,20},{20,16},{24,28},{28,24},{1,5},{5... | collective-permute-start | bytes 393224 | tf_op jit(solution)/shard_map/ppermute | solution.py:129
  61.8 8.0 %collective-permute-start.22 = (f32[256,128]{1,0:T(8,128)S(1)}, f32[256,128]{1,0:T(8,128)S(1)}, u32[]{:S(2)}, u32[]{:S(2)}) collective-permute-start(f32[256,128]{1,0:T(8,128)S(1)} %add.32), channel_id=1, source_target_pairs={{0,8},{4,12},{8,0},{12,4},{16,24},{20,28},{24,16},{28,20},{1,9},{5... | collective-permute-start | bytes 393224 | tf_op jit(solution)/shard_map/ppermute | solution.py:129
  62.4 7.4 %collective-permute-start.20 = (f32[256,128]{1,0:T(8,128)S(1)}, f32[256,128]{1,0:T(8,128)S(1)}, u32[]{:S(2)}, u32[]{:S(2)}) collective-permute-start(f32[256,128]{1,0:T(8,128)S(1)} %add.31), channel_id=1, source_target_pairs={{0,16},{4,20},{8,24},{12,28},{16,0},{20,4},{24,8},{28,12},{1,17},{... | collective-permute-start | bytes 393224 | tf_op jit(solution)/shard_map/ppermute | solution.py:129
  62.9 7.6 %collective-permute-start.18 = (f32[256,128]{1,0:T(8,128)S(1)}, f32[256,128]{1,0:T(8,128)S(1)}, u32[]{:S(2)}, u32[]{:S(2)}) collective-permute-start(f32[256,128]{1,0:T(8,128)S(1)} %add.30), channel_id=1, source_target_pairs={{0,24},{4,28},{8,16},{12,20},{16,8},{20,12},{24,0},{28,4},{1,25},{... | collective-permute-start | bytes 393224 | tf_op jit(solution)/shard_map/ppermute | solution.py:129
  71.7 6.1 %collective-permute-start.33 = (bf16[512,128]{1,0:T(8,128)(2,1)S(1)}, bf16[512,128]{1,0:T(8,128)(2,1)S(1)}, u32[]{:S(2)}, u32[]{:S(2)}) collective-permute-start(bf16[512,128]{1,0:T(8,128)(2,1)S(1)} %get-tuple-element.102.refs_0_), channel_id=1, source_target_pairs={{0,8},{4,12},{8,0},{12,4},{16,24},{20,28},{24,16},{28,20},{1,9},{5... | collective-permute-start | bytes 393224 | tf_op jit(solution)/shard_map/ppermute | solution.py:129
  73.2 7.0 %collective-permute-start.35 = (bf16[512,128]{1,0:T(8,128)(2,1)S(1)}, bf16[512,128]{1,0:T(8,128)(2,1)S(1)}, u32[]{:S(2)}, u32[]{:S(2)}) collective-permute-start(bf16[512,128]{1,0:T(8,128)(2,1)S(1)} %get-tuple-element.102.refs_0_), channel_id=1, source_target_pairs={{0,16},{4,20},{8,24},{12,28},{16,0},{20,4},{24,8},{28,12},{1,17},{... | collective-permute-start | bytes 393224 | tf_op jit(solution)/shard_map/ppermute | solution.py:129
  74.1 6.1 %collective-permute-start.37 = (bf16[512,128]{1,0:T(8,128)(2,1)S(1)}, bf16[512,128]{1,0:T(8,128)(2,1)S(1)}, u32[]{:S(2)}, u32[]{:S(2)}) collective-permute-start(bf16[512,128]{1,0:T(8,128)(2,1)S(1)} %get-tuple-element.102.refs_0_), channel_id=1, source_target_pairs={{0,24},{4,28},{8,16},{12,20},{16,8},{20,12},{24,0},{28,4},{1,25},{... | collective-permute-start | bytes 393224 | tf_op jit(solution)/shard_map/ppermute | solution.py:129
  75.2 5.5 %collective-permute-start.32 = (bf16[512,128]{1,0:T(8,128)(2,1)S(1)}, bf16[512,128]{1,0:T(8,128)(2,1)S(1)}, u32[]{:S(2)}, u32[]{:S(2)}) collective-permute-start(bf16[512,128]{1,0:T(8,128)(2,1)S(1)} %get-tuple-element.102.refs_0_), channel_id=1, source_target_pairs={{0,4},{4,0},{8,12},{12,8},{16,20},{20,16},{24,28},{28,24},{1,5},{5... | collective-permute-start | bytes 393224 | tf_op jit(solution)/shard_map/ppermute | solution.py:129
  77.7 3.0 %collective-permute-start.34 = (bf16[512,128]{1,0:T(8,128)(2,1)S(1)}, bf16[512,128]{1,0:T(8,128)(2,1)S(1)}, u32[]{:S(2)}, u32[]{:S(2)}) collective-permute-start(bf16[512,128]{1,0:T(8,128)(2,1)S(1)} %collective-permute-done.33.refs_2_), channel_id=1, source_target_pairs={{0,4},{4,0},{8,12},{12,8},{16,20},{20,16},{24,28},{28,24},{1,5},{5... | collective-permute-start | bytes 393224 | tf_op jit(solution)/shard_map/ppermute | solution.py:129
  80.2 1.3 collective-permute-start.36
  80.2 1.5 %collective-permute-start.38 = (bf16[512,128]{1,0:T(8,128)(2,1)S(1)}, bf16[512,128]{1,0:T(8,128)(2,1)S(1)}, u32[]{:S(2)}, u32[]{:S(2)}) collective-permute-start(bf16[512,128]{1,0:T(8,128)(2,1)S(1)} %collective-permute-done.37.refs_6_), channel_id=1, source_target_pairs={{0,4},{4,0},{8,12},{12,8},{16,20},{20,16},{24,28},{28,24},{1,5},{5... | collective-permute-start | bytes 393224 | tf_op jit(solution)/shard_map/ppermute | solution.py:129
  82.5 9.7 %collective-permute-start.52 = (f32[160,128]{1,0:T(8,128)S(1)}, f32[160,128]{1,0:T(8,128)S(1)}, u32[]{:S(2)}, u32[]{:S(2)}) collective-permute-start(f32[160,128]{1,0:T(8,128)S(1)} %shard_map.136), channel_id=1, source_target_pairs={{0,1},{1,0},{2,3},{3,2},{4,5},{5,4},{6,7},{7,6},{8,9},{9,8},{10,11... | collective-permute-start | bytes 245768 | tf_op jit(solution)/shard_map/ppermute | solution.py:129
  87.7 5.2 %collective-permute-start.39 = (bf16[256,128]{1,0:T(8,128)(2,1)S(1)}, bf16[256,128]{1,0:T(8,128)(2,1)S(1)}, u32[]{:S(2)}, u32[]{:S(2)}) collective-permute-start(bf16[256,128]{1,0:T(8,128)(2,1)S(1)} %get-tuple-element.104), channel_id=1, source_target_pairs={{0,1},{1,0},{2,3},{3,2},{4,5},{5,4},{6,7},{7,6},{8,9},{9,8},{10,11... | collective-permute-start | bytes 196616 | tf_op jit(solution)/shard_map/ppermute | solution.py:129
  87.8 10.5 %collective-permute-start.40 = (bf16[256,128]{1,0:T(8,128)(2,1)S(1)}, bf16[256,128]{1,0:T(8,128)(2,1)S(1)}, u32[]{:S(2)}, u32[]{:S(2)}) collective-permute-start(bf16[256,128]{1,0:T(8,128)(2,1)S(1)} %get-tuple-element.105), channel_id=1, source_target_pairs={{0,2},{1,3},{2,0},{3,1},{4,6},{5,7},{6,4},{7,5},{8,10},{9,11},{10,... | collective-permute-start | bytes 196616 | tf_op jit(solution)/shard_map/ppermute | solution.py:129
  89.0 9.4 %collective-permute-start.41 = (bf16[256,128]{1,0:T(8,128)(2,1)S(1)}, bf16[256,128]{1,0:T(8,128)(2,1)S(1)}, u32[]{:S(2)}, u32[]{:S(2)}) collective-permute-start(bf16[256,128]{1,0:T(8,128)(2,1)S(1)} %get-tuple-element.106), channel_id=1, source_target_pairs={{0,3},{1,2},{2,1},{3,0},{4,7},{5,6},{6,5},{7,4},{8,11},{9,10},{10,... | collective-permute-start | bytes 196616 | tf_op jit(solution)/shard_map/ppermute | solution.py:129
  92.2 12.1 %collective-permute-start.53 = (f32[160,128]{1,0:T(8,128)S(1)}, f32[160,128]{1,0:T(8,128)S(1)}, u32[]{:S(2)}, u32[]{:S(2)}) collective-permute-start(f32[160,128]{1,0:T(8,128)S(1)} %add.38), channel_id=1, source_target_pairs={{0,2},{1,3},{2,0},{3,1},{4,6},{5,7},{6,4},{7,5},{8,10},{9,11},{10,... | collective-permute-start | bytes 245768 | tf_op jit(solution)/shard_map/ppermute | solution.py:129
  99.9 7.9 %collective-permute-start.42 = (f32[256,128]{1,0:T(8,128)S(1)}, f32[256,128]{1,0:T(8,128)S(1)}, u32[]{:S(2)}, u32[]{:S(2)}) collective-permute-start(f32[256,128]{1,0:T(8,128)S(1)} %get-tuple-element.108), channel_id=1, source_target_pairs={{0,1},{1,0},{2,3},{3,2},{4,5},{5,4},{6,7},{7,6},{8,9},{9,8},{10,11... | collective-permute-start | bytes 393224 | tf_op jit(solution)/shard_map/ppermute | solution.py:129
  101.9 10.4 %collective-permute-start.43 = (f32[256,128]{1,0:T(8,128)S(1)}, f32[256,128]{1,0:T(8,128)S(1)}, u32[]{:S(2)}, u32[]{:S(2)}) collective-permute-start(f32[256,128]{1,0:T(8,128)S(1)} %get-tuple-element.109), channel_id=1, source_target_pairs={{0,2},{1,3},{2,0},{3,1},{4,6},{5,7},{6,4},{7,5},{8,10},{9,11},{10,... | collective-permute-start | bytes 393224 | tf_op jit(solution)/shard_map/ppermute | solution.py:129
  101.9 10.4 %collective-permute-start.44 = (f32[256,128]{1,0:T(8,128)S(1)}, f32[256,128]{1,0:T(8,128)S(1)}, u32[]{:S(2)}, u32[]{:S(2)}) collective-permute-start(f32[256,128]{1,0:T(8,128)S(1)} %get-tuple-element.110), channel_id=1, source_target_pairs={{0,3},{1,2},{2,1},{3,0},{4,7},{5,6},{6,5},{7,4},{8,11},{9,10},{10,... | collective-permute-start | bytes 393224 | tf_op jit(solution)/shard_map/ppermute | solution.py:129
  104.3 9.0 %collective-permute-start.54 = (f32[160,128]{1,0:T(8,128)S(1)}, f32[160,128]{1,0:T(8,128)S(1)}, u32[]{:S(2)}, u32[]{:S(2)}) collective-permute-start(f32[160,128]{1,0:T(8,128)S(1)} %add.39.refs_0_), channel_id=1, source_target_pairs={{0,4},{4,0},{8,12},{12,8},{16,20},{20,16},{24,28},{28,24},{1,5},{5... | collective-permute-start | bytes 245768 | tf_op jit(solution)/shard_map/ppermute | solution.py:129
  104.4 30.5 %collective-permute-start.29 = (f32[64,128]{1,0:T(8,128)S(1)}, f32[64,128]{1,0:T(8,128)S(1)}, u32[]{:S(2)}, u32[]{:S(2)}) collective-permute-start(f32[64,128]{1,0:T(8,128)S(1)} %get-tuple-element.98), channel_id=1, source_target_pairs={{0,1},{1,0},{2,3},{3,2},{4,5},{5,4},{6,7},{7,6},{8,9},{9,8},{10,11... | collective-permute-start | bytes 98312 | tf_op jit(solution)/shard_map/ppermute | solution.py:129
  112.6 6.1 %collective-permute-start.50 = (f32[256,128]{1,0:T(8,128)S(1)}, f32[256,128]{1,0:T(8,128)S(1)}, u32[]{:S(2)}, u32[]{:S(2)}) collective-permute-start(f32[256,128]{1,0:T(8,128)S(1)} %get-tuple-element.118), channel_id=1, source_target_pairs={{0,4},{4,0},{8,12},{12,8},{16,20},{20,16},{24,28},{28,24},{1,5},{5... | collective-permute-start | bytes 393224 | tf_op jit(solution)/shard_map/ppermute | solution.py:129
  112.7 7.0 %collective-permute-start.48 = (f32[256,128]{1,0:T(8,128)S(1)}, f32[256,128]{1,0:T(8,128)S(1)}, u32[]{:S(2)}, u32[]{:S(2)}) collective-permute-start(f32[256,128]{1,0:T(8,128)S(1)} %get-tuple-element.116), channel_id=1, source_target_pairs={{0,4},{4,0},{8,12},{12,8},{16,20},{20,16},{24,28},{28,24},{1,5},{5... | collective-permute-start | bytes 393224 | tf_op jit(solution)/shard_map/ppermute | solution.py:129
  113.2 7.7 %collective-permute-start.46 = (f32[256,128]{1,0:T(8,128)S(1)}, f32[256,128]{1,0:T(8,128)S(1)}, u32[]{:S(2)}, u32[]{:S(2)}) collective-permute-start(f32[256,128]{1,0:T(8,128)S(1)} %get-tuple-element.114), channel_id=1, source_target_pairs={{0,4},{4,0},{8,12},{12,8},{16,20},{20,16},{24,28},{28,24},{1,5},{5... | collective-permute-start | bytes 393224 | tf_op jit(solution)/shard_map/ppermute | solution.py:129
  113.3 13.4 %collective-permute-start.45 = (f32[256,128]{1,0:T(8,128)S(1)}, f32[256,128]{1,0:T(8,128)S(1)}, u32[]{:S(2)}, u32[]{:S(2)}) collective-permute-start(f32[256,128]{1,0:T(8,128)S(1)} %get-tuple-element.112), channel_id=1, source_target_pairs={{0,4},{4,0},{8,12},{12,8},{16,20},{20,16},{24,28},{28,24},{1,5},{5... | collective-permute-start | bytes 393224 | tf_op jit(solution)/shard_map/ppermute | solution.py:129
  118.8 10.5 %collective-permute-start.51 = (f32[256,128]{1,0:T(8,128)S(1)}, f32[256,128]{1,0:T(8,128)S(1)}, u32[]{:S(2)}, u32[]{:S(2)}) collective-permute-start(f32[256,128]{1,0:T(8,128)S(1)} %add.37), channel_id=1, source_target_pairs={{0,8},{4,12},{8,0},{12,4},{16,24},{20,28},{24,16},{28,20},{1,9},{5... | collective-permute-start | bytes 393224 | tf_op jit(solution)/shard_map/ppermute | solution.py:129
  119.7 12.0 %collective-permute-start.49 = (f32[256,128]{1,0:T(8,128)S(1)}, f32[256,128]{1,0:T(8,128)S(1)}, u32[]{:S(2)}, u32[]{:S(2)}) collective-permute-start(f32[256,128]{1,0:T(8,128)S(1)} %add.36), channel_id=1, source_target_pairs={{0,16},{4,20},{8,24},{12,28},{16,0},{20,4},{24,8},{28,12},{1,17},{... | collective-permute-start | bytes 393224 | tf_op jit(solution)/shard_map/ppermute | solution.py:129
  120.9 10.8 %collective-permute-start.47 = (f32[256,128]{1,0:T(8,128)S(1)}, f32[256,128]{1,0:T(8,128)S(1)}, u32[]{:S(2)}, u32[]{:S(2)}) collective-permute-start(f32[256,128]{1,0:T(8,128)S(1)} %add.35), channel_id=1, source_target_pairs={{0,24},{4,28},{8,16},{12,20},{16,8},{20,12},{24,0},{28,4},{1,25},{... | collective-permute-start | bytes 393224 | tf_op jit(solution)/shard_map/ppermute | solution.py:129
  126.7 10.7 %collective-permute-start.30 = (f32[64,128]{1,0:T(8,128)S(1)}, f32[64,128]{1,0:T(8,128)S(1)}, u32[]{:S(2)}, u32[]{:S(2)}) collective-permute-start(f32[64,128]{1,0:T(8,128)S(1)} %get-tuple-element.99), channel_id=1, source_target_pairs={{0,2},{1,3},{2,0},{3,1},{4,6},{5,7},{6,4},{7,5},{8,10},{9,11},{10,... | collective-permute-start | bytes 98312 | tf_op jit(solution)/shard_map/ppermute | solution.py:129
  129.3 8.1 %collective-permute-start.31 = (f32[64,128]{1,0:T(8,128)S(1)}, f32[64,128]{1,0:T(8,128)S(1)}, u32[]{:S(2)}, u32[]{:S(2)}) collective-permute-start(f32[64,128]{1,0:T(8,128)S(1)} %get-tuple-element.100), channel_id=1, source_target_pairs={{0,3},{1,2},{2,1},{3,0},{4,7},{5,6},{6,5},{7,4},{8,11},{9,10},{10,... | collective-permute-start | bytes 98312 | tf_op jit(solution)/shard_map/ppermute | solution.py:129
  132.9 5.2 %collective-permute-start.55 = (f32[64,128]{1,0:T(8,128)S(1)}, f32[64,128]{1,0:T(8,128)S(1)}, u32[]{:S(2)}, u32[]{:S(2)}) collective-permute-start(f32[64,128]{1,0:T(8,128)S(1)} %get-tuple-element.124), channel_id=1, source_target_pairs={{0,1},{1,0},{2,3},{3,2},{4,5},{5,4},{6,7},{7,6},{8,9},{9,8},{10,11... | collective-permute-start | bytes 98312 | tf_op jit(solution)/shard_map/ppermute | solution.py:129
  133.0 5.1 %collective-permute-start.56 = (f32[64,128]{1,0:T(8,128)S(1)}, f32[64,128]{1,0:T(8,128)S(1)}, u32[]{:S(2)}, u32[]{:S(2)}) collective-permute-start(f32[64,128]{1,0:T(8,128)S(1)} %get-tuple-element.125), channel_id=1, source_target_pairs={{0,2},{1,3},{2,0},{3,1},{4,6},{5,7},{6,4},{7,5},{8,10},{9,11},{10,... | collective-permute-start | bytes 98312 | tf_op jit(solution)/shard_map/ppermute | solution.py:129
  134.9 5.7 %collective-permute-start.57 = (f32[64,128]{1,0:T(8,128)S(1)}, f32[64,128]{1,0:T(8,128)S(1)}, u32[]{:S(2)}, u32[]{:S(2)}) collective-permute-start(f32[64,128]{1,0:T(8,128)S(1)} %get-tuple-element.126), channel_id=1, source_target_pairs={{0,3},{1,2},{2,1},{3,0},{4,7},{5,6},{6,5},{7,4},{8,11},{9,10},{10,... | collective-permute-start | bytes 98312 | tf_op jit(solution)/shard_map/ppermute | solution.py:129
  (3 other events, 2.0 us)

commit v5 on v4

--- a/solution.py
+++ b/solution.py
@@ -369,10 +369,10 @@
         functools.partial(place_kernel, len(received)), [shape(received[0].shape)] * size,
         table, *received,
     )
-    order = [*reversed(range(1, size // 2)), 0]
+    order = list(reversed(range(1, size // 2)))
     arrived = {m: swap(placed[2 * m + 1], "wide", 1) for m in order}
-    terms = [placed[0], arrived[0]]
-    for m in order[:-1]:
+    terms = [placed[0], swap(placed[1], "wide", 1)]
+    for m in order:
         terms.append(swap(placed[2 * m] + arrived[m], "wide", 2 * m))
     return terms
 

time: 142 us -> 142 us (level)
  no operation moved by 1% of the time
where the time goes in v5:
time: 142 us; the launch traced here: 141 us
  starting transfers between devices  65 us (46%)
  waiting for transfers between devices  43.5 us (31%)
  Pallas kernels  28.7 us (20%)
  local copies, waits for them, and re-layouts  2.92 us (2%)
    ppermute x58, starting transfers between devices, swap(): return lax.ppermute(x, axis, [(i, i ^ mask) for i in range(size)])  65 us
    ppermute x58, waiting for transfers between devices, swap(): return lax.ppermute(x, axis, [(i, i ^ mask) for i in range(size)])  43.5 us
    pallas_call x21, Pallas kernels, kernel_call(): pl.pallas_call(kernel, out_shape=tuple(out_shape), in_specs=[spec] * len(...  28.7 us
    unnamed x18, local copies, waits for them, and re-layouts  2.92 us
  transfers between devices with their start and end apart: 58, of which 18 were waited for; matrix products, arithmetic and copies ran while one was open for 0% of the time, Pallas kernels for 18%

profile of v5, /device:TPU:0, one launch (start us, length us, event | category | flops | bytes accessed | tf_op | source)
XLA Modules:
  0.0 141.4 jit_solution(13065410394793736063)
XLA Ops:
  0.6 0.9 copy-done.1
  1.6 3.1 %collective-permute-start = (f32[64,128]{1,0:T(8,128)S(1)}, f32[64,128]{1,0:T(8,128)S(1)}, u32[]{:S(2)}, u32[]{:S(2)}) collective-permute-start(f32[64,128]{1,0:T(8,128)S(1)} %get-tuple-element.68), channel_id=1, source_target_pairs={{0,1},{1,0},{2,3},{3,2},{4,5},{5,4},{6,7},{7,6},{8,9},{9,8},{10,11... | collective-permute-start | bytes 98312 | tf_op jit(solution)/shard_map/ppermute | solution.py:129
  4.7 2.6 %collective-permute-start.1 = (f32[64,128]{1,0:T(8,128)S(1)}, f32[64,128]{1,0:T(8,128)S(1)}, u32[]{:S(2)}, u32[]{:S(2)}) collective-permute-start(f32[64,128]{1,0:T(8,128)S(1)} %get-tuple-element.69), channel_id=1, source_target_pairs={{0,2},{1,3},{2,0},{3,1},{4,6},{5,7},{6,4},{7,5},{8,10},{9,11},{10,... | collective-permute-start | bytes 98312 | tf_op jit(solution)/shard_map/ppermute | solution.py:129
  7.3 2.8 %collective-permute-done.1.refs_2_ = f32[64,128]{1,0:T(8,128)S(1)} collective-permute-done((f32[64,128]{1,0:T(8,128)S(1)}, f32[64,128]{1,0:T(8,128)S(1)}, u32[]{:S(2)}, u32[]{:S(2)}) %collective-permute-start.1) | collective-permute-done | bytes 32800 | tf_op jit(solution)/shard_map/ppermute | solution.py:129
  10.1 2.9 %collective-permute-done.2.refs_3_ = f32[64,128]{1,0:T(8,128)S(1)} collective-permute-done((f32[64,128]{1,0:T(8,128)S(1)}, f32[64,128]{1,0:T(8,128)S(1)}, u32[]{:S(2)}, u32[]{:S(2)}) %collective-permute-start.2) | collective-permute-done | bytes 32800 | tf_op jit(solution)/shard_map/ppermute | solution.py:129
  13.0 1.6 %collective-permute-start.4 = (bf16[512,128]{1,0:T(8,128)(2,1)S(1)}, bf16[512,128]{1,0:T(8,128)(2,1)S(1)}, u32[]{:S(2)}, u32[]{:S(2)}) collective-permute-start(bf16[512,128]{1,0:T(8,128)(2,1)S(1)} %get-tuple-element.71.refs_0_), channel_id=1, source_target_pairs={{0,8},{4,12},{8,0},{12,4},{16,24},{20,28},{24,16},{28,20},{1,9},{5... | collective-permute-start | bytes 393224 | tf_op jit(solution)/shard_map/ppermute | solution.py:129
  14.6 1.5 %collective-permute-start.6 = (bf16[512,128]{1,0:T(8,128)(2,1)S(1)}, bf16[512,128]{1,0:T(8,128)(2,1)S(1)}, u32[]{:S(2)}, u32[]{:S(2)}) collective-permute-start(bf16[512,128]{1,0:T(8,128)(2,1)S(1)} %get-tuple-element.71.refs_0_), channel_id=1, source_target_pairs={{0,16},{4,20},{8,24},{12,28},{16,0},{20,4},{24,8},{28,12},{1,17},{... | collective-permute-start | bytes 393224 | tf_op jit(solution)/shard_map/ppermute | solution.py:129
  16.6 0.7 copy-done.3
  17.2 0.7 copy-done.4
  17.9 0.7 copy-done.5
  18.6 0.6 shard_map.120
  19.7 0.6 collective-permute-done.6.refs_4_
  20.3 1.6 %collective-permute-done.8.refs_6_ = bf16[512,128]{1,0:T(8,128)(2,1)S(1)} collective-permute-done((bf16[512,128]{1,0:T(8,128)(2,1)S(1)}, bf16[512,128]{1,0:T(8,128)(2,1)S(1)}, u32[]{:S(2)}, u32[]{:S(2)}) %collective-permute-start.8) | collective-permute-done | bytes 131104 | tf_op jit(solution)/shard_map/ppermute | solution.py:129
  22.0 1.3 collective-permute-done.9.refs_7_
  23.3 0.6 shard_map.128
  24.3 2.0 %collective-permute-start.10 = (bf16[256,128]{1,0:T(8,128)(2,1)S(1)}, bf16[256,128]{1,0:T(8,128)(2,1)S(1)}, u32[]{:S(2)}, u32[]{:S(2)}) collective-permute-start(bf16[256,128]{1,0:T(8,128)(2,1)S(1)} %get-tuple-element.73), channel_id=1, source_target_pairs={{0,1},{1,0},{2,3},{3,2},{4,5},{5,4},{6,7},{7,6},{8,9},{9,8},{10,11... | collective-permute-start | bytes 196616 | tf_op jit(solution)/shard_map/ppermute | solution.py:129
  26.3 2.4 %collective-permute-start.12 = (bf16[256,128]{1,0:T(8,128)(2,1)S(1)}, bf16[256,128]{1,0:T(8,128)(2,1)S(1)}, u32[]{:S(2)}, u32[]{:S(2)}) collective-permute-start(bf16[256,128]{1,0:T(8,128)(2,1)S(1)} %get-tuple-element.75), channel_id=1, source_target_pairs={{0,3},{1,2},{2,1},{3,0},{4,7},{5,6},{6,5},{7,4},{8,11},{9,10},{10,... | collective-permute-start | bytes 196616 | tf_op jit(solution)/shard_map/ppermute | solution.py:129
  28.8 1.1 collective-permute-start.23
  30.0 0.9 collective-permute-start.24
  30.9 2.1 %collective-permute-start.27 = (f32[160,128]{1,0:T(8,128)S(1)}, f32[160,128]{1,0:T(8,128)S(1)}, u32[]{:S(2)}, u32[]{:S(2)}) collective-permute-start(f32[160,128]{1,0:T(8,128)S(1)} %add.33), channel_id=1, source_target_pairs={{0,2},{1,3},{2,0},{3,1},{4,6},{5,7},{6,4},{7,5},{8,10},{9,11},{10,... | collective-permute-start | bytes 245768 | tf_op jit(solution)/shard_map/ppermute | solution.py:129
  33.0 0.9 collective-permute-done.11.refs_2_
  33.9 1.5 %shard_map.124 = (f32[256,128]{1,0:T(8,128)S(1)}, f32[256,128]{1,0:T(8,128)S(1)}, f32[256,128]{1,0:T(8,128)S(1)}, f32[256,128]{1,0:T(8,128)S(1)}) custom-call(bf16[1,8,512,512]{3,2,1,0:T(8,128)(2,1)S(1)} %copy-done, f32[8,256]{1,0:T(8,128)S(1)} %copy-done.2, bf16[256,128]{1,0:T(8,128)(2,1)S(1)} %get-tuple-element.72.refs_0_, ...), custom_call_target="tpu_custom_call" | custom-call | flops 1073741824 | bytes 4988928 | tf_op jit(solution)/shard_map/pallas_call | solution.py:112
  35.4 5.9 %collective-permute-start.13 = (f32[256,128]{1,0:T(8,128)S(1)}, f32[256,128]{1,0:T(8,128)S(1)}, u32[]{:S(2)}, u32[]{:S(2)}) collective-permute-start(f32[256,128]{1,0:T(8,128)S(1)} %get-tuple-element.77), channel_id=1, source_target_pairs={{0,1},{1,0},{2,3},{3,2},{4,5},{5,4},{6,7},{7,6},{8,9},{9,8},{10,11... | collective-permute-start | bytes 393224 | tf_op jit(solution)/shard_map/ppermute | solution.py:129
  41.3 2.4 %collective-permute-start.15 = (f32[256,128]{1,0:T(8,128)S(1)}, f32[256,128]{1,0:T(8,128)S(1)}, u32[]{:S(2)}, u32[]{:S(2)}) collective-permute-start(f32[256,128]{1,0:T(8,128)S(1)} %get-tuple-element.79), channel_id=1, source_target_pairs={{0,3},{1,2},{2,1},{3,0},{4,7},{5,6},{6,5},{7,4},{8,11},{9,10},{10,... | collective-permute-start | bytes 393224 | tf_op jit(solution)/shard_map/ppermute | solution.py:129
  43.7 4.9 %collective-permute-done.27 = f32[160,128]{1,0:T(8,128)S(1)} collective-permute-done((f32[160,128]{1,0:T(8,128)S(1)}, f32[160,128]{1,0:T(8,128)S(1)}, u32[]{:S(2)}, u32[]{:S(2)}) %collective-permute-start.27) | collective-permute-done | bytes 81952 | tf_op jit(solution)/shard_map/ppermute | solution.py:129
  48.8 6.4 %collective-permute-done.25.refs_4_ = f32[192,128]{1,0:T(8,128)S(1)} collective-permute-done((f32[192,128]{1,0:T(8,128)S(1)}, f32[192,128]{1,0:T(8,128)S(1)}, u32[]{:S(2)}, u32[]{:S(2)}) %collective-permute-start.25) | collective-permute-done | bytes 98336 | tf_op jit(solution)/shard_map/ppermute | solution.py:129
  56.8 5.0 %shard_map.129 = (f32[256,256]{1,0:T(8,128)S(1)}, f32[1,128]{1,0:T(1,128)S(1)}) custom-call(f32[8,256]{1,0:T(8,128)S(1)} %copy-done.2, f32[160,128]{1,0:T(8,128)S(1)} %add.34.refs_0_, f32[160,128]{1,0:T(8,128)S(1)} %collective-permute-done.28.refs_1_), custom_call_target="tpu_custom_call" | custom-call | flops 6000000000 | bytes 434688 | tf_op jit(solution)/shard_map/pallas_call | solution.py:112
  61.8 0.6 collective-permute-start.22
  62.9 2.6 %collective-permute-start.18 = (f32[256,128]{1,0:T(8,128)S(1)}, f32[256,128]{1,0:T(8,128)S(1)}, u32[]{:S(2)}, u32[]{:S(2)}) collective-permute-start(f32[256,128]{1,0:T(8,128)S(1)} %add.30), channel_id=1, source_target_pairs={{0,24},{4,28},{8,16},{12,20},{16,8},{20,12},{24,0},{28,4},{1,25},{... | collective-permute-start | bytes 393224 | tf_op jit(solution)/shard_map/ppermute | solution.py:129
  65.5 4.2 %shard_map.130.refs_8_ = f32[256,256]{1,0:T(8,128)S(1)} custom-call(f32[256,256]{1,0:T(8,128)S(1)} %get-tuple-element.96.half_ref), custom_call_target="tpu_custom_call" | custom-call | flops 6000000000 | bytes 524288 | tf_op jit(solution)/shard_map/pallas_call | solution.py:112
  69.8 0.7 collective-permute-done.18.refs_2_
  70.5 1.2 shard_map.131
  71.7 1.6 %collective-permute-start.33 = (bf16[512,128]{1,0:T(8,128)(2,1)S(1)}, bf16[512,128]{1,0:T(8,128)(2,1)S(1)}, u32[]{:S(2)}, u32[]{:S(2)}) collective-permute-start(bf16[512,128]{1,0:T(8,128)(2,1)S(1)} %get-tuple-element.102.refs_0_), channel_id=1, source_target_pairs={{0,8},{4,12},{8,0},{12,4},{16,24},{20,28},{24,16},{28,20},{1,9},{5... | collective-permute-start | bytes 393224 | tf_op jit(solution)/shard_map/ppermute | solution.py:129
  73.2 0.9 collective-permute-start.35
  74.1 1.1 collective-permute-start.37
  75.2 2.5 %collective-permute-done.33.refs_2_ = bf16[512,128]{1,0:T(8,128)(2,1)S(1)} collective-permute-done((bf16[512,128]{1,0:T(8,128)(2,1)S(1)}, bf16[512,128]{1,0:T(8,128)(2,1)S(1)}, u32[]{:S(2)}, u32[]{:S(2)}) %collective-permute-start.33) | collective-permute-done | bytes 131104 | tf_op jit(solution)/shard_map/ppermute | solution.py:129
  77.7 2.5 %collective-permute-done.35.refs_4_ = bf16[512,128]{1,0:T(8,128)(2,1)S(1)} collective-permute-done((bf16[512,128]{1,0:T(8,128)(2,1)S(1)}, bf16[512,128]{1,0:T(8,128)(2,1)S(1)}, u32[]{:S(2)}, u32[]{:S(2)}) %collective-permute-start.35) | collective-permute-done | bytes 131104 | tf_op jit(solution)/shard_map/ppermute | solution.py:129
  80.2 0.5 collective-permute-start.38
  80.7 0.8 collective-permute-done.36.refs_5_
  81.7 0.7 shard_map.136
  82.5 5.0 %collective-permute-start.52 = (f32[160,128]{1,0:T(8,128)S(1)}, f32[160,128]{1,0:T(8,128)S(1)}, u32[]{:S(2)}, u32[]{:S(2)}) collective-permute-start(f32[160,128]{1,0:T(8,128)S(1)} %shard_map.136), channel_id=1, source_target_pairs={{0,1},{1,0},{2,3},{3,2},{4,5},{5,4},{6,7},{7,6},{8,9},{9,8},{10,11... | collective-permute-start | bytes 245768 | tf_op jit(solution)/shard_map/ppermute | solution.py:129
  87.8 1.1 collective-permute-start.40
  89.0 3.2 %collective-permute-start.41 = (bf16[256,128]{1,0:T(8,128)(2,1)S(1)}, bf16[256,128]{1,0:T(8,128)(2,1)S(1)}, u32[]{:S(2)}, u32[]{:S(2)}) collective-permute-start(bf16[256,128]{1,0:T(8,128)(2,1)S(1)} %get-tuple-element.106), channel_id=1, source_target_pairs={{0,3},{1,2},{2,1},{3,0},{4,7},{5,6},{6,5},{7,4},{8,11},{9,10},{10,... | collective-permute-start | bytes 196616 | tf_op jit(solution)/shard_map/ppermute | solution.py:129
  92.3 0.6 collective-permute-done.39.refs_1_
  92.9 5.4 %collective-permute-done.40.refs_2_ = bf16[256,128]{1,0:T(8,128)(2,1)S(1)} collective-permute-done((bf16[256,128]{1,0:T(8,128)(2,1)S(1)}, bf16[256,128]{1,0:T(8,128)(2,1)S(1)}, u32[]{:S(2)}, u32[]{:S(2)}) %collective-permute-start.40) | collective-permute-done | bytes 65568 | tf_op jit(solution)/shard_map/ppermute | solution.py:129
  98.3 1.5 %shard_map.134 = (f32[256,128]{1,0:T(8,128)S(1)}, f32[256,128]{1,0:T(8,128)S(1)}, f32[256,128]{1,0:T(8,128)S(1)}, f32[256,128]{1,0:T(8,128)S(1)}) custom-call(bf16[1,8,512,512]{3,2,1,0:T(8,128)(2,1)S(1)} %copy-done, f32[8,256]{1,0:T(8,128)S(1)} %copy-done.2, bf16[256,128]{1,0:T(8,128)(2,1)S(1)} %get-tuple-element.103.refs_0_, ...), custom_call_target="tpu_custom_call" | custom-call | flops 1073741824 | bytes 4988928 | tf_op jit(solution)/shard_map/pallas_call | solution.py:112
  99.9 2.0 %collective-permute-start.42 = (f32[256,128]{1,0:T(8,128)S(1)}, f32[256,128]{1,0:T(8,128)S(1)}, u32[]{:S(2)}, u32[]{:S(2)}) collective-permute-start(f32[256,128]{1,0:T(8,128)S(1)} %get-tuple-element.108), channel_id=1, source_target_pairs={{0,1},{1,0},{2,3},{3,2},{4,5},{5,4},{6,7},{7,6},{8,9},{9,8},{10,11... | collective-permute-start | bytes 393224 | tf_op jit(solution)/shard_map/ppermute | solution.py:129
  101.9 2.4 %collective-permute-start.44 = (f32[256,128]{1,0:T(8,128)S(1)}, f32[256,128]{1,0:T(8,128)S(1)}, u32[]{:S(2)}, u32[]{:S(2)}) collective-permute-start(f32[256,128]{1,0:T(8,128)S(1)} %get-tuple-element.110), channel_id=1, source_target_pairs={{0,3},{1,2},{2,1},{3,0},{4,7},{5,6},{6,5},{7,4},{8,11},{9,10},{10,... | collective-permute-start | bytes 393224 | tf_op jit(solution)/shard_map/ppermute | solution.py:129
  104.4 1.1 collective-permute-start.29
  105.5 2.2 %collective-permute-done.42.refs_1_ = f32[256,128]{1,0:T(8,128)S(1)} collective-permute-done((f32[256,128]{1,0:T(8,128)S(1)}, f32[256,128]{1,0:T(8,128)S(1)}, u32[]{:S(2)}, u32[]{:S(2)}) %collective-permute-start.42) | collective-permute-done | bytes 131104 | tf_op jit(solution)/shard_map/ppermute | solution.py:129
  107.7 4.5 %collective-permute-done.43.refs_2_ = f32[256,128]{1,0:T(8,128)S(1)} collective-permute-done((f32[256,128]{1,0:T(8,128)S(1)}, f32[256,128]{1,0:T(8,128)S(1)}, u32[]{:S(2)}, u32[]{:S(2)}) %collective-permute-start.43) | collective-permute-done | bytes 131104 | tf_op jit(solution)/shard_map/ppermute | solution.py:129
  113.7 5.0 %shard_map.137 = (f32[256,256]{1,0:T(8,128)S(1)}, f32[1,128]{1,0:T(1,128)S(1)}) custom-call(f32[8,256]{1,0:T(8,128)S(1)} %copy-done.2, f32[160,128]{1,0:T(8,128)S(1)} %add.39.refs_0_, f32[160,128]{1,0:T(8,128)S(1)} %collective-permute-done.54.refs_1_), custom_call_target="tpu_custom_call" | custom-call | flops 6000000000 | bytes 434688 | tf_op jit(solution)/shard_map/pallas_call | solution.py:112
  118.8 0.9 collective-permute-start.51
  119.7 1.2 collective-permute-start.49
  120.9 1.5 %collective-permute-start.47 = (f32[256,128]{1,0:T(8,128)S(1)}, f32[256,128]{1,0:T(8,128)S(1)}, u32[]{:S(2)}, u32[]{:S(2)}) collective-permute-start(f32[256,128]{1,0:T(8,128)S(1)} %add.35), channel_id=1, source_target_pairs={{0,24},{4,28},{8,16},{12,20},{16,8},{20,12},{24,0},{28,4},{1,25},{... | collective-permute-start | bytes 393224 | tf_op jit(solution)/shard_map/ppermute | solution.py:129
  122.5 4.2 %shard_map.138.refs_8_ = f32[256,256]{1,0:T(8,128)S(1)} custom-call(f32[256,256]{1,0:T(8,128)S(1)} %get-tuple-element.122.half_ref), custom_call_target="tpu_custom_call" | custom-call | flops 6000000000 | bytes 524288 | tf_op jit(solution)/shard_map/pallas_call | solution.py:112
  126.7 2.5 %collective-permute-start.30 = (f32[64,128]{1,0:T(8,128)S(1)}, f32[64,128]{1,0:T(8,128)S(1)}, u32[]{:S(2)}, u32[]{:S(2)}) collective-permute-start(f32[64,128]{1,0:T(8,128)S(1)} %get-tuple-element.99), channel_id=1, source_target_pairs={{0,2},{1,3},{2,0},{3,1},{4,6},{5,7},{6,4},{7,5},{8,10},{9,11},{10,... | collective-permute-start | bytes 98312 | tf_op jit(solution)/shard_map/ppermute | solution.py:129
  129.3 2.5 %collective-permute-start.31 = (f32[64,128]{1,0:T(8,128)S(1)}, f32[64,128]{1,0:T(8,128)S(1)}, u32[]{:S(2)}, u32[]{:S(2)}) collective-permute-start(f32[64,128]{1,0:T(8,128)S(1)} %get-tuple-element.100), channel_id=1, source_target_pairs={{0,3},{1,2},{2,1},{3,0},{4,7},{5,6},{6,5},{7,4},{8,11},{9,10},{10,... | collective-permute-start | bytes 98312 | tf_op jit(solution)/shard_map/ppermute | solution.py:129
  131.8 1.2 shard_map.139
  133.0 1.9 %collective-permute-start.56 = (f32[64,128]{1,0:T(8,128)S(1)}, f32[64,128]{1,0:T(8,128)S(1)}, u32[]{:S(2)}, u32[]{:S(2)}) collective-permute-start(f32[64,128]{1,0:T(8,128)S(1)} %get-tuple-element.125), channel_id=1, source_target_pairs={{0,2},{1,3},{2,0},{3,1},{4,6},{5,7},{6,4},{7,5},{8,10},{9,11},{10,... | collective-permute-start | bytes 98312 | tf_op jit(solution)/shard_map/ppermute | solution.py:129
  134.9 2.5 %collective-permute-start.57 = (f32[64,128]{1,0:T(8,128)S(1)}, f32[64,128]{1,0:T(8,128)S(1)}, u32[]{:S(2)}, u32[]{:S(2)}) collective-permute-start(f32[64,128]{1,0:T(8,128)S(1)} %get-tuple-element.126), channel_id=1, source_target_pairs={{0,3},{1,2},{2,1},{3,0},{4,7},{5,6},{6,5},{7,4},{8,11},{9,10},{10,... | collective-permute-start | bytes 98312 | tf_op jit(solution)/shard_map/ppermute | solution.py:129
  137.4 0.7 shard_map.132
  138.1 2.5 %collective-permute-done.57.refs_3_ = f32[64,128]{1,0:T(8,128)S(1)} collective-permute-done((f32[64,128]{1,0:T(8,128)S(1)}, f32[64,128]{1,0:T(8,128)S(1)}, u32[]{:S(2)}, u32[]{:S(2)}) %collective-permute-start.57) | collective-permute-done | bytes 32800 | tf_op jit(solution)/shard_map/ppermute | solution.py:129
  140.6 0.7 shard_map.140
  (103 shorter events, 6.0 us)
Async XLA Ops:
  0.6 0.9 copy-start.1
  1.6 5.7 %collective-permute-start = (f32[64,128]{1,0:T(8,128)S(1)}, f32[64,128]{1,0:T(8,128)S(1)}, u32[]{:S(2)}, u32[]{:S(2)}) collective-permute-start(f32[64,128]{1,0:T(8,128)S(1)} %get-tuple-element.68), channel_id=1, source_target_pairs={{0,1},{1,0},{2,3},{3,2},{4,5},{5,4},{6,7},{7,6},{8,9},{9,8},{10,11... | collective-permute-start | bytes 98312 | tf_op jit(solution)/shard_map/ppermute | solution.py:129
  4.7 5.4 %collective-permute-start.1 = (f32[64,128]{1,0:T(8,128)S(1)}, f32[64,128]{1,0:T(8,128)S(1)}, u32[]{:S(2)}, u32[]{:S(2)}) collective-permute-start(f32[64,128]{1,0:T(8,128)S(1)} %get-tuple-element.69), channel_id=1, source_target_pairs={{0,2},{1,3},{2,0},{3,1},{4,6},{5,7},{6,4},{7,5},{8,10},{9,11},{10,... | collective-permute-start | bytes 98312 | tf_op jit(solution)/shard_map/ppermute | solution.py:129
  7.3 5.7 %collective-permute-start.2 = (f32[64,128]{1,0:T(8,128)S(1)}, f32[64,128]{1,0:T(8,128)S(1)}, u32[]{:S(2)}, u32[]{:S(2)}) collective-permute-start(f32[64,128]{1,0:T(8,128)S(1)} %get-tuple-element.70), channel_id=1, source_target_pairs={{0,3},{1,2},{2,1},{3,0},{4,7},{5,6},{6,5},{7,4},{8,11},{9,10},{10,... | collective-permute-start | bytes 98312 | tf_op jit(solution)/shard_map/ppermute | solution.py:129
  13.0 6.2 %collective-permute-start.4 = (bf16[512,128]{1,0:T(8,128)(2,1)S(1)}, bf16[512,128]{1,0:T(8,128)(2,1)S(1)}, u32[]{:S(2)}, u32[]{:S(2)}) collective-permute-start(bf16[512,128]{1,0:T(8,128)(2,1)S(1)} %get-tuple-element.71.refs_0_), channel_id=1, source_target_pairs={{0,8},{4,12},{8,0},{12,4},{16,24},{20,28},{24,16},{28,20},{1,9},{5... | collective-permute-start | bytes 393224 | tf_op jit(solution)/shard_map/ppermute | solution.py:129
  14.6 5.8 %collective-permute-start.6 = (bf16[512,128]{1,0:T(8,128)(2,1)S(1)}, bf16[512,128]{1,0:T(8,128)(2,1)S(1)}, u32[]{:S(2)}, u32[]{:S(2)}) collective-permute-start(bf16[512,128]{1,0:T(8,128)(2,1)S(1)} %get-tuple-element.71.refs_0_), channel_id=1, source_target_pairs={{0,16},{4,20},{8,24},{12,28},{16,0},{20,4},{24,8},{28,12},{1,17},{... | collective-permute-start | bytes 393224 | tf_op jit(solution)/shard_map/ppermute | solution.py:129
  16.1 5.9 %collective-permute-start.8 = (bf16[512,128]{1,0:T(8,128)(2,1)S(1)}, bf16[512,128]{1,0:T(8,128)(2,1)S(1)}, u32[]{:S(2)}, u32[]{:S(2)}) collective-permute-start(bf16[512,128]{1,0:T(8,128)(2,1)S(1)} %get-tuple-element.71.refs_0_), channel_id=1, source_target_pairs={{0,24},{4,28},{8,16},{12,20},{16,8},{20,12},{24,0},{28,4},{1,25},{... | collective-permute-start | bytes 393224 | tf_op jit(solution)/shard_map/ppermute | solution.py:129
  19.1 2.8 %collective-permute-start.3 = (bf16[512,128]{1,0:T(8,128)(2,1)S(1)}, bf16[512,128]{1,0:T(8,128)(2,1)S(1)}, u32[]{:S(2)}, u32[]{:S(2)}) collective-permute-start(bf16[512,128]{1,0:T(8,128)(2,1)S(1)} %get-tuple-element.71.refs_0_), channel_id=1, source_target_pairs={{0,4},{4,0},{8,12},{12,8},{16,20},{20,16},{24,28},{28,24},{1,5},{5... | collective-permute-start | bytes 393224 | tf_op jit(solution)/shard_map/ppermute | solution.py:129
  19.2 2.7 %collective-permute-start.5 = (bf16[512,128]{1,0:T(8,128)(2,1)S(1)}, bf16[512,128]{1,0:T(8,128)(2,1)S(1)}, u32[]{:S(2)}, u32[]{:S(2)}) collective-permute-start(bf16[512,128]{1,0:T(8,128)(2,1)S(1)} %collective-permute-done.4.refs_2_), channel_id=1, source_target_pairs={{0,4},{4,0},{8,12},{12,8},{16,20},{20,16},{24,28},{28,24},{1,5},{5... | collective-permute-start | bytes 393224 | tf_op jit(solution)/shard_map/ppermute | solution.py:129
  20.3 1.7 %collective-permute-start.7 = (bf16[512,128]{1,0:T(8,128)(2,1)S(1)}, bf16[512,128]{1,0:T(8,128)(2,1)S(1)}, u32[]{:S(2)}, u32[]{:S(2)}) collective-permute-start(bf16[512,128]{1,0:T(8,128)(2,1)S(1)} %collective-permute-done.6.refs_4_), channel_id=1, source_target_pairs={{0,4},{4,0},{8,12},{12,8},{16,20},{20,16},{24,28},{28,24},{1,5},{5... | collective-permute-start | bytes 393224 | tf_op jit(solution)/shard_map/ppermute | solution.py:129
  22.0 1.3 collective-permute-start.9
  23.9 6.0 %collective-permute-start.26 = (f32[160,128]{1,0:T(8,128)S(1)}, f32[160,128]{1,0:T(8,128)S(1)}, u32[]{:S(2)}, u32[]{:S(2)}) collective-permute-start(f32[160,128]{1,0:T(8,128)S(1)} %shard_map.128), channel_id=1, source_target_pairs={{0,1},{1,0},{2,3},{3,2},{4,5},{5,4},{6,7},{7,6},{8,9},{9,8},{10,11... | collective-permute-start | bytes 245768 | tf_op jit(solution)/shard_map/ppermute | solution.py:129
  23.9 4.8 %copy-start.6 = (f32[512,64]{0,1:T(8,128)S(1)}, f32[512,64]{0,1:T(8,128)}, u32[]{:S(2)}) copy-start(f32[512,64]{0,1:T(8,128)} %param.17) | copy-start | bytes 393220
  24.0 4.8 %copy-start.7 = (f32[512,64]{0,1:T(8,128)S(1)}, f32[512,64]{0,1:T(8,128)}, u32[]{:S(2)}) copy-start(f32[512,64]{0,1:T(8,128)} %param.16) | copy-start | bytes 393220
  24.0 4.8 %copy-start.8 = (f32[512,64]{0,1:T(8,128)S(1)}, f32[512,64]{0,1:T(8,128)}, u32[]{:S(2)}) copy-start(f32[512,64]{0,1:T(8,128)} %param.13) | copy-start | bytes 393220
  24.0 9.9 %copy-start = (bf16[1,8,512,512]{3,2,1,0:T(8,128)(2,1)S(1)}, bf16[1,8,512,512]{3,2,1,0:T(8,128)(2,1)}, u32[]{:S(2)}) copy-start(bf16[1,8,512,512]{3,2,1,0:T(8,128)(2,1)} %activity_ref.3) | copy-start | bytes 12582916
  24.0 9.9 %copy-start.2 = (f32[8,256]{1,0:T(8,128)S(1)}, f32[8,256]{1,0:T(8,128)}, u32[]{:S(2)}) copy-start(f32[8,256]{1,0:T(8,128)} %time_ref.7) | copy-start | bytes 24580
  24.3 6.6 %collective-permute-start.10 = (bf16[256,128]{1,0:T(8,128)(2,1)S(1)}, bf16[256,128]{1,0:T(8,128)(2,1)S(1)}, u32[]{:S(2)}, u32[]{:S(2)}) collective-permute-start(bf16[256,128]{1,0:T(8,128)(2,1)S(1)} %get-tuple-element.73), channel_id=1, source_target_pairs={{0,1},{1,0},{2,3},{3,2},{4,5},{5,4},{6,7},{7,6},{8,9},{9,8},{10,11... | collective-permute-start | bytes 196616 | tf_op jit(solution)/shard_map/ppermute | solution.py:129
  26.3 7.6 %collective-permute-start.11 = (bf16[256,128]{1,0:T(8,128)(2,1)S(1)}, bf16[256,128]{1,0:T(8,128)(2,1)S(1)}, u32[]{:S(2)}, u32[]{:S(2)}) collective-permute-start(bf16[256,128]{1,0:T(8,128)(2,1)S(1)} %get-tuple-element.74), channel_id=1, source_target_pairs={{0,2},{1,3},{2,0},{3,1},{4,6},{5,7},{6,4},{7,5},{8,10},{9,11},{10,... | collective-permute-start | bytes 196616 | tf_op jit(solution)/shard_map/ppermute | solution.py:129
  26.3 7.6 %collective-permute-start.12 = (bf16[256,128]{1,0:T(8,128)(2,1)S(1)}, bf16[256,128]{1,0:T(8,128)(2,1)S(1)}, u32[]{:S(2)}, u32[]{:S(2)}) collective-permute-start(bf16[256,128]{1,0:T(8,128)(2,1)S(1)} %get-tuple-element.75), channel_id=1, source_target_pairs={{0,3},{1,2},{2,1},{3,0},{4,7},{5,6},{6,5},{7,4},{8,11},{9,10},{10,... | collective-permute-start | bytes 196616 | tf_op jit(solution)/shard_map/ppermute | solution.py:129
  28.8 12.5 %collective-permute-start.23 = (f32[192,128]{1,0:T(8,128)S(1)}, f32[192,128]{1,0:T(8,128)S(1)}, u32[]{:S(2)}, u32[]{:S(2)}) collective-permute-start(f32[192,128]{1,0:T(8,128)S(1)} %get-tuple-element.90), channel_id=1, source_target_pairs={{0,1},{1,0},{2,3},{3,2},{4,5},{5,4},{6,7},{7,6},{8,9},{9,8},{10,11... | collective-permute-start | bytes 294920 | tf_op jit(solution)/shard_map/ppermute | solution.py:129
  30.0 18.7 %collective-permute-start.24 = (f32[192,128]{1,0:T(8,128)S(1)}, f32[192,128]{1,0:T(8,128)S(1)}, u32[]{:S(2)}, u32[]{:S(2)}) collective-permute-start(f32[192,128]{1,0:T(8,128)S(1)} %get-tuple-element.91), channel_id=1, source_target_pairs={{0,2},{1,3},{2,0},{3,1},{4,6},{5,7},{6,4},{7,5},{8,10},{9,11},{10,... | collective-permute-start | bytes 294920 | tf_op jit(solution)/shard_map/ppermute | solution.py:129
  30.9 17.8 %collective-permute-start.27 = (f32[160,128]{1,0:T(8,128)S(1)}, f32[160,128]{1,0:T(8,128)S(1)}, u32[]{:S(2)}, u32[]{:S(2)}) collective-permute-start(f32[160,128]{1,0:T(8,128)S(1)} %add.33), channel_id=1, source_target_pairs={{0,2},{1,3},{2,0},{3,1},{4,6},{5,7},{6,4},{7,5},{8,10},{9,11},{10,... | collective-permute-start | bytes 245768 | tf_op jit(solution)/shard_map/ppermute | solution.py:129
  35.4 19.8 %collective-permute-start.13 = (f32[256,128]{1,0:T(8,128)S(1)}, f32[256,128]{1,0:T(8,128)S(1)}, u32[]{:S(2)}, u32[]{:S(2)}) collective-permute-start(f32[256,128]{1,0:T(8,128)S(1)} %get-tuple-element.77), channel_id=1, source_target_pairs={{0,1},{1,0},{2,3},{3,2},{4,5},{5,4},{6,7},{7,6},{8,9},{9,8},{10,11... | collective-permute-start | bytes 393224 | tf_op jit(solution)/shard_map/ppermute | solution.py:129
  41.3 14.0 %collective-permute-start.14 = (f32[256,128]{1,0:T(8,128)S(1)}, f32[256,128]{1,0:T(8,128)S(1)}, u32[]{:S(2)}, u32[]{:S(2)}) collective-permute-start(f32[256,128]{1,0:T(8,128)S(1)} %get-tuple-element.78), channel_id=1, source_target_pairs={{0,2},{1,3},{2,0},{3,1},{4,6},{5,7},{6,4},{7,5},{8,10},{9,11},{10,... | collective-permute-start | bytes 393224 | tf_op jit(solution)/shard_map/ppermute | solution.py:129
  41.3 14.0 %collective-permute-start.15 = (f32[256,128]{1,0:T(8,128)S(1)}, f32[256,128]{1,0:T(8,128)S(1)}, u32[]{:S(2)}, u32[]{:S(2)}) collective-permute-start(f32[256,128]{1,0:T(8,128)S(1)} %get-tuple-element.79), channel_id=1, source_target_pairs={{0,3},{1,2},{2,1},{3,0},{4,7},{5,6},{6,5},{7,4},{8,11},{9,10},{10,... | collective-permute-start | bytes 393224 | tf_op jit(solution)/shard_map/ppermute | solution.py:129
  48.7 6.5 %collective-permute-start.25 = (f32[192,128]{1,0:T(8,128)S(1)}, f32[192,128]{1,0:T(8,128)S(1)}, u32[]{:S(2)}, u32[]{:S(2)}) collective-permute-start(f32[192,128]{1,0:T(8,128)S(1)} %get-tuple-element.92), channel_id=1, source_target_pairs={{0,3},{1,2},{2,1},{3,0},{4,7},{5,6},{6,5},{7,4},{8,11},{9,10},{10,... | collective-permute-start | bytes 294920 | tf_op jit(solution)/shard_map/ppermute | solution.py:129
  48.7 8.1 %collective-permute-start.28 = (f32[160,128]{1,0:T(8,128)S(1)}, f32[160,128]{1,0:T(8,128)S(1)}, u32[]{:S(2)}, u32[]{:S(2)}) collective-permute-start(f32[160,128]{1,0:T(8,128)S(1)} %add.34.refs_0_), channel_id=1, source_target_pairs={{0,4},{4,0},{8,12},{12,8},{16,20},{20,16},{24,28},{28,24},{1,5},{5... | collective-permute-start | bytes 245768 | tf_op jit(solution)/shard_map/ppermute | solution.py:129
  55.7 6.1 %collective-permute-start.21 = (f32[256,128]{1,0:T(8,128)S(1)}, f32[256,128]{1,0:T(8,128)S(1)}, u32[]{:S(2)}, u32[]{:S(2)}) collective-permute-start(f32[256,128]{1,0:T(8,128)S(1)} %get-tuple-element.87), channel_id=1, source_target_pairs={{0,4},{4,0},{8,12},{12,8},{16,20},{20,16},{24,28},{28,24},{1,5},{5... | collective-permute-start | bytes 393224 | tf_op jit(solution)/shard_map/ppermute | solution.py:129
  55.7 6.7 %collective-permute-start.19 = (f32[256,128]{1,0:T(8,128)S(1)}, f32[256,128]{1,0:T(8,128)S(1)}, u32[]{:S(2)}, u32[]{:S(2)}) collective-permute-start(f32[256,128]{1,0:T(8,128)S(1)} %get-tuple-element.85), channel_id=1, source_target_pairs={{0,4},{4,0},{8,12},{12,8},{16,20},{20,16},{24,28},{28,24},{1,5},{5... | collective-permute-start | bytes 393224 | tf_op jit(solution)/shard_map/ppermute | solution.py:129
  56.2 6.7 %collective-permute-start.17 = (f32[256,128]{1,0:T(8,128)S(1)}, f32[256,128]{1,0:T(8,128)S(1)}, u32[]{:S(2)}, u32[]{:S(2)}) collective-permute-start(f32[256,128]{1,0:T(8,128)S(1)} %get-tuple-element.83), channel_id=1, source_target_pairs={{0,4},{4,0},{8,12},{12,8},{16,20},{20,16},{24,28},{28,24},{1,5},{5... | collective-permute-start | bytes 393224 | tf_op jit(solution)/shard_map/ppermute | solution.py:129
  56.3 13.4 %collective-permute-start.16 = (f32[256,128]{1,0:T(8,128)S(1)}, f32[256,128]{1,0:T(8,128)S(1)}, u32[]{:S(2)}, u32[]{:S(2)}) collective-permute-start(f32[256,128]{1,0:T(8,128)S(1)} %get-tuple-element.81), channel_id=1, source_target_pairs={{0,4},{4,0},{8,12},{12,8},{16,20},{20,16},{24,28},{28,24},{1,5},{5... | collective-permute-start | bytes 393224 | tf_op jit(solution)/shard_map/ppermute | solution.py:129
  61.8 8.0 %collective-permute-start.22 = (f32[256,128]{1,0:T(8,128)S(1)}, f32[256,128]{1,0:T(8,128)S(1)}, u32[]{:S(2)}, u32[]{:S(2)}) collective-permute-start(f32[256,128]{1,0:T(8,128)S(1)} %add.32), channel_id=1, source_target_pairs={{0,8},{4,12},{8,0},{12,4},{16,24},{20,28},{24,16},{28,20},{1,9},{5... | collective-permute-start | bytes 393224 | tf_op jit(solution)/shard_map/ppermute | solution.py:129
  62.4 7.4 %collective-permute-start.20 = (f32[256,128]{1,0:T(8,128)S(1)}, f32[256,128]{1,0:T(8,128)S(1)}, u32[]{:S(2)}, u32[]{:S(2)}) collective-permute-start(f32[256,128]{1,0:T(8,128)S(1)} %add.31), channel_id=1, source_target_pairs={{0,16},{4,20},{8,24},{12,28},{16,0},{20,4},{24,8},{28,12},{1,17},{... | collective-permute-start | bytes 393224 | tf_op jit(solution)/shard_map/ppermute | solution.py:129
  62.9 7.6 %collective-permute-start.18 = (f32[256,128]{1,0:T(8,128)S(1)}, f32[256,128]{1,0:T(8,128)S(1)}, u32[]{:S(2)}, u32[]{:S(2)}) collective-permute-start(f32[256,128]{1,0:T(8,128)S(1)} %add.30), channel_id=1, source_target_pairs={{0,24},{4,28},{8,16},{12,20},{16,8},{20,12},{24,0},{28,4},{1,25},{... | collective-permute-start | bytes 393224 | tf_op jit(solution)/shard_map/ppermute | solution.py:129
  71.7 6.1 %collective-permute-start.33 = (bf16[512,128]{1,0:T(8,128)(2,1)S(1)}, bf16[512,128]{1,0:T(8,128)(2,1)S(1)}, u32[]{:S(2)}, u32[]{:S(2)}) collective-permute-start(bf16[512,128]{1,0:T(8,128)(2,1)S(1)} %get-tuple-element.102.refs_0_), channel_id=1, source_target_pairs={{0,8},{4,12},{8,0},{12,4},{16,24},{20,28},{24,16},{28,20},{1,9},{5... | collective-permute-start | bytes 393224 | tf_op jit(solution)/shard_map/ppermute | solution.py:129
  73.2 7.0 %collective-permute-start.35 = (bf16[512,128]{1,0:T(8,128)(2,1)S(1)}, bf16[512,128]{1,0:T(8,128)(2,1)S(1)}, u32[]{:S(2)}, u32[]{:S(2)}) collective-permute-start(bf16[512,128]{1,0:T(8,128)(2,1)S(1)} %get-tuple-element.102.refs_0_), channel_id=1, source_target_pairs={{0,16},{4,20},{8,24},{12,28},{16,0},{20,4},{24,8},{28,12},{1,17},{... | collective-permute-start | bytes 393224 | tf_op jit(solution)/shard_map/ppermute | solution.py:129
  74.1 6.1 %collective-permute-start.37 = (bf16[512,128]{1,0:T(8,128)(2,1)S(1)}, bf16[512,128]{1,0:T(8,128)(2,1)S(1)}, u32[]{:S(2)}, u32[]{:S(2)}) collective-permute-start(bf16[512,128]{1,0:T(8,128)(2,1)S(1)} %get-tuple-element.102.refs_0_), channel_id=1, source_target_pairs={{0,24},{4,28},{8,16},{12,20},{16,8},{20,12},{24,0},{28,4},{1,25},{... | collective-permute-start | bytes 393224 | tf_op jit(solution)/shard_map/ppermute | solution.py:129
  75.2 5.5 %collective-permute-start.32 = (bf16[512,128]{1,0:T(8,128)(2,1)S(1)}, bf16[512,128]{1,0:T(8,128)(2,1)S(1)}, u32[]{:S(2)}, u32[]{:S(2)}) collective-permute-start(bf16[512,128]{1,0:T(8,128)(2,1)S(1)} %get-tuple-element.102.refs_0_), channel_id=1, source_target_pairs={{0,4},{4,0},{8,12},{12,8},{16,20},{20,16},{24,28},{28,24},{1,5},{5... | collective-permute-start | bytes 393224 | tf_op jit(solution)/shard_map/ppermute | solution.py:129
  77.7 3.0 %collective-permute-start.34 = (bf16[512,128]{1,0:T(8,128)(2,1)S(1)}, bf16[512,128]{1,0:T(8,128)(2,1)S(1)}, u32[]{:S(2)}, u32[]{:S(2)}) collective-permute-start(bf16[512,128]{1,0:T(8,128)(2,1)S(1)} %collective-permute-done.33.refs_2_), channel_id=1, source_target_pairs={{0,4},{4,0},{8,12},{12,8},{16,20},{20,16},{24,28},{28,24},{1,5},{5... | collective-permute-start | bytes 393224 | tf_op jit(solution)/shard_map/ppermute | solution.py:129
  80.2 1.3 collective-permute-start.36
  80.2 1.5 %collective-permute-start.38 = (bf16[512,128]{1,0:T(8,128)(2,1)S(1)}, bf16[512,128]{1,0:T(8,128)(2,1)S(1)}, u32[]{:S(2)}, u32[]{:S(2)}) collective-permute-start(bf16[512,128]{1,0:T(8,128)(2,1)S(1)} %collective-permute-done.37.refs_6_), channel_id=1, source_target_pairs={{0,4},{4,0},{8,12},{12,8},{16,20},{20,16},{24,28},{28,24},{1,5},{5... | collective-permute-start | bytes 393224 | tf_op jit(solution)/shard_map/ppermute | solution.py:129
  82.5 9.7 %collective-permute-start.52 = (f32[160,128]{1,0:T(8,128)S(1)}, f32[160,128]{1,0:T(8,128)S(1)}, u32[]{:S(2)}, u32[]{:S(2)}) collective-permute-start(f32[160,128]{1,0:T(8,128)S(1)} %shard_map.136), channel_id=1, source_target_pairs={{0,1},{1,0},{2,3},{3,2},{4,5},{5,4},{6,7},{7,6},{8,9},{9,8},{10,11... | collective-permute-start | bytes 245768 | tf_op jit(solution)/shard_map/ppermute | solution.py:129
  87.7 5.2 %collective-permute-start.39 = (bf16[256,128]{1,0:T(8,128)(2,1)S(1)}, bf16[256,128]{1,0:T(8,128)(2,1)S(1)}, u32[]{:S(2)}, u32[]{:S(2)}) collective-permute-start(bf16[256,128]{1,0:T(8,128)(2,1)S(1)} %get-tuple-element.104), channel_id=1, source_target_pairs={{0,1},{1,0},{2,3},{3,2},{4,5},{5,4},{6,7},{7,6},{8,9},{9,8},{10,11... | collective-permute-start | bytes 196616 | tf_op jit(solution)/shard_map/ppermute | solution.py:129
  87.8 10.5 %collective-permute-start.40 = (bf16[256,128]{1,0:T(8,128)(2,1)S(1)}, bf16[256,128]{1,0:T(8,128)(2,1)S(1)}, u32[]{:S(2)}, u32[]{:S(2)}) collective-permute-start(bf16[256,128]{1,0:T(8,128)(2,1)S(1)} %get-tuple-element.105), channel_id=1, source_target_pairs={{0,2},{1,3},{2,0},{3,1},{4,6},{5,7},{6,4},{7,5},{8,10},{9,11},{10,... | collective-permute-start | bytes 196616 | tf_op jit(solution)/shard_map/ppermute | solution.py:129
  89.0 9.4 %collective-permute-start.41 = (bf16[256,128]{1,0:T(8,128)(2,1)S(1)}, bf16[256,128]{1,0:T(8,128)(2,1)S(1)}, u32[]{:S(2)}, u32[]{:S(2)}) collective-permute-start(bf16[256,128]{1,0:T(8,128)(2,1)S(1)} %get-tuple-element.106), channel_id=1, source_target_pairs={{0,3},{1,2},{2,1},{3,0},{4,7},{5,6},{6,5},{7,4},{8,11},{9,10},{10,... | collective-permute-start | bytes 196616 | tf_op jit(solution)/shard_map/ppermute | solution.py:129
  92.2 12.1 %collective-permute-start.53 = (f32[160,128]{1,0:T(8,128)S(1)}, f32[160,128]{1,0:T(8,128)S(1)}, u32[]{:S(2)}, u32[]{:S(2)}) collective-permute-start(f32[160,128]{1,0:T(8,128)S(1)} %add.38), channel_id=1, source_target_pairs={{0,2},{1,3},{2,0},{3,1},{4,6},{5,7},{6,4},{7,5},{8,10},{9,11},{10,... | collective-permute-start | bytes 245768 | tf_op jit(solution)/shard_map/ppermute | solution.py:129
  99.9 7.9 %collective-permute-start.42 = (f32[256,128]{1,0:T(8,128)S(1)}, f32[256,128]{1,0:T(8,128)S(1)}, u32[]{:S(2)}, u32[]{:S(2)}) collective-permute-start(f32[256,128]{1,0:T(8,128)S(1)} %get-tuple-element.108), channel_id=1, source_target_pairs={{0,1},{1,0},{2,3},{3,2},{4,5},{5,4},{6,7},{7,6},{8,9},{9,8},{10,11... | collective-permute-start | bytes 393224 | tf_op jit(solution)/shard_map/ppermute | solution.py:129
  101.9 10.4 %collective-permute-start.43 = (f32[256,128]{1,0:T(8,128)S(1)}, f32[256,128]{1,0:T(8,128)S(1)}, u32[]{:S(2)}, u32[]{:S(2)}) collective-permute-start(f32[256,128]{1,0:T(8,128)S(1)} %get-tuple-element.109), channel_id=1, source_target_pairs={{0,2},{1,3},{2,0},{3,1},{4,6},{5,7},{6,4},{7,5},{8,10},{9,11},{10,... | collective-permute-start | bytes 393224 | tf_op jit(solution)/shard_map/ppermute | solution.py:129
  101.9 10.4 %collective-permute-start.44 = (f32[256,128]{1,0:T(8,128)S(1)}, f32[256,128]{1,0:T(8,128)S(1)}, u32[]{:S(2)}, u32[]{:S(2)}) collective-permute-start(f32[256,128]{1,0:T(8,128)S(1)} %get-tuple-element.110), channel_id=1, source_target_pairs={{0,3},{1,2},{2,1},{3,0},{4,7},{5,6},{6,5},{7,4},{8,11},{9,10},{10,... | collective-permute-start | bytes 393224 | tf_op jit(solution)/shard_map/ppermute | solution.py:129
  104.3 9.0 %collective-permute-start.54 = (f32[160,128]{1,0:T(8,128)S(1)}, f32[160,128]{1,0:T(8,128)S(1)}, u32[]{:S(2)}, u32[]{:S(2)}) collective-permute-start(f32[160,128]{1,0:T(8,128)S(1)} %add.39.refs_0_), channel_id=1, source_target_pairs={{0,4},{4,0},{8,12},{12,8},{16,20},{20,16},{24,28},{28,24},{1,5},{5... | collective-permute-start | bytes 245768 | tf_op jit(solution)/shard_map/ppermute | solution.py:129
  104.4 30.5 %collective-permute-start.29 = (f32[64,128]{1,0:T(8,128)S(1)}, f32[64,128]{1,0:T(8,128)S(1)}, u32[]{:S(2)}, u32[]{:S(2)}) collective-permute-start(f32[64,128]{1,0:T(8,128)S(1)} %get-tuple-element.98), channel_id=1, source_target_pairs={{0,1},{1,0},{2,3},{3,2},{4,5},{5,4},{6,7},{7,6},{8,9},{9,8},{10,11... | collective-permute-start | bytes 98312 | tf_op jit(solution)/shard_map/ppermute | solution.py:129
  112.6 6.1 %collective-permute-start.50 = (f32[256,128]{1,0:T(8,128)S(1)}, f32[256,128]{1,0:T(8,128)S(1)}, u32[]{:S(2)}, u32[]{:S(2)}) collective-permute-start(f32[256,128]{1,0:T(8,128)S(1)} %get-tuple-element.118), channel_id=1, source_target_pairs={{0,4},{4,0},{8,12},{12,8},{16,20},{20,16},{24,28},{28,24},{1,5},{5... | collective-permute-start | bytes 393224 | tf_op jit(solution)/shard_map/ppermute | solution.py:129
  112.7 7.0 %collective-permute-start.48 = (f32[256,128]{1,0:T(8,128)S(1)}, f32[256,128]{1,0:T(8,128)S(1)}, u32[]{:S(2)}, u32[]{:S(2)}) collective-permute-start(f32[256,128]{1,0:T(8,128)S(1)} %get-tuple-element.116), channel_id=1, source_target_pairs={{0,4},{4,0},{8,12},{12,8},{16,20},{20,16},{24,28},{28,24},{1,5},{5... | collective-permute-start | bytes 393224 | tf_op jit(solution)/shard_map/ppermute | solution.py:129
  113.2 7.7 %collective-permute-start.46 = (f32[256,128]{1,0:T(8,128)S(1)}, f32[256,128]{1,0:T(8,128)S(1)}, u32[]{:S(2)}, u32[]{:S(2)}) collective-permute-start(f32[256,128]{1,0:T(8,128)S(1)} %get-tuple-element.114), channel_id=1, source_target_pairs={{0,4},{4,0},{8,12},{12,8},{16,20},{20,16},{24,28},{28,24},{1,5},{5... | collective-permute-start | bytes 393224 | tf_op jit(solution)/shard_map/ppermute | solution.py:129
  113.3 13.4 %collective-permute-start.45 = (f32[256,128]{1,0:T(8,128)S(1)}, f32[256,128]{1,0:T(8,128)S(1)}, u32[]{:S(2)}, u32[]{:S(2)}) collective-permute-start(f32[256,128]{1,0:T(8,128)S(1)} %get-tuple-element.112), channel_id=1, source_target_pairs={{0,4},{4,0},{8,12},{12,8},{16,20},{20,16},{24,28},{28,24},{1,5},{5... | collective-permute-start | bytes 393224 | tf_op jit(solution)/shard_map/ppermute | solution.py:129
  118.8 10.5 %collective-permute-start.51 = (f32[256,128]{1,0:T(8,128)S(1)}, f32[256,128]{1,0:T(8,128)S(1)}, u32[]{:S(2)}, u32[]{:S(2)}) collective-permute-start(f32[256,128]{1,0:T(8,128)S(1)} %add.37), channel_id=1, source_target_pairs={{0,8},{4,12},{8,0},{12,4},{16,24},{20,28},{24,16},{28,20},{1,9},{5... | collective-permute-start | bytes 393224 | tf_op jit(solution)/shard_map/ppermute | solution.py:129
  119.7 12.0 %collective-permute-start.49 = (f32[256,128]{1,0:T(8,128)S(1)}, f32[256,128]{1,0:T(8,128)S(1)}, u32[]{:S(2)}, u32[]{:S(2)}) collective-permute-start(f32[256,128]{1,0:T(8,128)S(1)} %add.36), channel_id=1, source_target_pairs={{0,16},{4,20},{8,24},{12,28},{16,0},{20,4},{24,8},{28,12},{1,17},{... | collective-permute-start | bytes 393224 | tf_op jit(solution)/shard_map/ppermute | solution.py:129
  120.9 10.8 %collective-permute-start.47 = (f32[256,128]{1,0:T(8,128)S(1)}, f32[256,128]{1,0:T(8,128)S(1)}, u32[]{:S(2)}, u32[]{:S(2)}) collective-permute-start(f32[256,128]{1,0:T(8,128)S(1)} %add.35), channel_id=1, source_target_pairs={{0,24},{4,28},{8,16},{12,20},{16,8},{20,12},{24,0},{28,4},{1,25},{... | collective-permute-start | bytes 393224 | tf_op jit(solution)/shard_map/ppermute | solution.py:129
  126.7 10.7 %collective-permute-start.30 = (f32[64,128]{1,0:T(8,128)S(1)}, f32[64,128]{1,0:T(8,128)S(1)}, u32[]{:S(2)}, u32[]{:S(2)}) collective-permute-start(f32[64,128]{1,0:T(8,128)S(1)} %get-tuple-element.99), channel_id=1, source_target_pairs={{0,2},{1,3},{2,0},{3,1},{4,6},{5,7},{6,4},{7,5},{8,10},{9,11},{10,... | collective-permute-start | bytes 98312 | tf_op jit(solution)/shard_map/ppermute | solution.py:129
  129.3 8.1 %collective-permute-start.31 = (f32[64,128]{1,0:T(8,128)S(1)}, f32[64,128]{1,0:T(8,128)S(1)}, u32[]{:S(2)}, u32[]{:S(2)}) collective-permute-start(f32[64,128]{1,0:T(8,128)S(1)} %get-tuple-element.100), channel_id=1, source_target_pairs={{0,3},{1,2},{2,1},{3,0},{4,7},{5,6},{6,5},{7,4},{8,11},{9,10},{10,... | collective-permute-start | bytes 98312 | tf_op jit(solution)/shard_map/ppermute | solution.py:129
  132.9 5.2 %collective-permute-start.55 = (f32[64,128]{1,0:T(8,128)S(1)}, f32[64,128]{1,0:T(8,128)S(1)}, u32[]{:S(2)}, u32[]{:S(2)}) collective-permute-start(f32[64,128]{1,0:T(8,128)S(1)} %get-tuple-element.124), channel_id=1, source_target_pairs={{0,1},{1,0},{2,3},{3,2},{4,5},{5,4},{6,7},{7,6},{8,9},{9,8},{10,11... | collective-permute-start | bytes 98312 | tf_op jit(solution)/shard_map/ppermute | solution.py:129
  133.0 5.1 %collective-permute-start.56 = (f32[64,128]{1,0:T(8,128)S(1)}, f32[64,128]{1,0:T(8,128)S(1)}, u32[]{:S(2)}, u32[]{:S(2)}) collective-permute-start(f32[64,128]{1,0:T(8,128)S(1)} %get-tuple-element.125), channel_id=1, source_target_pairs={{0,2},{1,3},{2,0},{3,1},{4,6},{5,7},{6,4},{7,5},{8,10},{9,11},{10,... | collective-permute-start | bytes 98312 | tf_op jit(solution)/shard_map/ppermute | solution.py:129
  134.9 5.7 %collective-permute-start.57 = (f32[64,128]{1,0:T(8,128)S(1)}, f32[64,128]{1,0:T(8,128)S(1)}, u32[]{:S(2)}, u32[]{:S(2)}) collective-permute-start(f32[64,128]{1,0:T(8,128)S(1)} %get-tuple-element.126), channel_id=1, source_target_pairs={{0,3},{1,2},{2,1},{3,0},{4,7},{5,6},{6,5},{7,4},{8,11},{9,10},{10,... | collective-permute-start | bytes 98312 | tf_op jit(solution)/shard_map/ppermute | solution.py:129
  (3 other events, 2.0 us)
